TPU v7x, 32 devices: a whole 2x2x4 slice. The times are simulated.
32 devices in a mesh: dp: 2 (over core), row: 4 (over y, x), col: 4 (over z).
Axes of the slice: x: 2, y: 2, z: 4, core: 2. Of those that a mesh axis runs over, the one named last changes fastest.
Arguments:
- inputs: bfloat16 [768, 8192], P('col', ('dp', 'row')), may hold values from -6 to 6
- encoder: bfloat16 [768, 16384], P('col', ('dp', 'row')), may hold values from -6 to 6
- prefix: int32 [8], P(('dp', 'col')), may hold values from 102 to 512
- targets: int32 [8192], P(('dp', 'row')), may hold values from 0 to 32127
- gain_self: float32 [768], P('col'), may hold values from 0.1 to 1.9
- w_query: bfloat16 [768, 768], P('col', 'row'), may hold values from -0.4375 to 0.4375
- w_key: bfloat16 [768, 768], P('col', 'row'), may hold values from -0.21875 to 0.21875
- w_value: bfloat16 [768, 768], P('col', 'row'), may hold values from -0.21875 to 0.21875
- w_attn_out: bfloat16 [768, 768], P('row', 'col'), may hold values from -0.875 to 0.875
- gain_cross: float32 [768], P('col'), may hold values from 0.1 to 1.9
- w_cross_query: bfloat16 [768, 768], P('col', 'row'), may hold values from -0.4375 to 0.4375
- w_cross_key: bfloat16 [768, 768], P('col', 'row'), may hold values from -0.21875 to 0.21875
- w_cross_value: bfloat16 [768, 768], P('col', 'row'), may hold values from -0.21875 to 0.21875
- w_cross_out: bfloat16 [768, 768], P('row', 'col'), may hold values from -0.875 to 0.875
- gain_ff: float32 [768], P('col'), may hold values from 0.1 to 1.9
- w_gate: bfloat16 [768, 2048], P('col', 'row'), may hold values from -0.21875 to 0.21875
- w_up: bfloat16 [768, 2048], P('col', 'row'), may hold values from -0.21875 to 0.21875
- w_ff_out: bfloat16 [768, 2048], P('col', 'row'), may hold values from -0.125 to 0.125
- gain_final: float32 [768], P('col'), may hold values from 0.1 to 1.9
- embed_table: bfloat16 [768, 32128], P('row', 'col'), may hold values from -0.4375 to 0.4375
Outputs:
- output: bfloat16 [768, 8192], P('col', ('dp', 'row'))
- loss: float32 [8192], P(('dp', 'row'))
- grad_inputs: float32 [768, 8192], P('col', ('dp', 'row'))
- grad_encoder: float32 [768, 16384], P('col', ('dp', 'row'))
- grad_gain_self: float32 [768], P('col')
- grad_w_query: float32 [768, 768], P(('col', 'dp'), 'row')
- grad_w_key: float32 [768, 768], P(('col', 'dp'), 'row')
- grad_w_value: float32 [768, 768], P(('col', 'dp'), 'row')
- grad_w_attn_out: float32 [768, 768], P(('row', 'dp'), 'col')
- grad_gain_cross: float32 [768], P('col')
- grad_w_cross_query: float32 [768, 768], P(('col', 'dp'), 'row')
- grad_w_cross_key: float32 [768, 768], P(('col', 'dp'), 'row')
- grad_w_cross_value: float32 [768, 768], P(('col', 'dp'), 'row')
- grad_w_cross_out: float32 [768, 768], P(('row', 'dp'), 'col')
- grad_gain_ff: float32 [768], P('col')
- grad_w_gate: float32 [768, 2048], P(('col', 'dp'), 'row')
- grad_w_up: float32 [768, 2048], P(('col', 'dp'), 'row')
- grad_w_ff_out: float32 [768, 2048], P(('col', 'dp'), 'row')
- grad_gain_final: float32 [768], P('col')
- grad_embed_table: float32 [768, 32128], P(('dp', 'row'), 'col')
All inputs are finite; a program needn't handle non-finite values.
Results may differ from a plain program's by a relative error of at most 0.025.
Values may be sent and summed in bfloat16 or wider, within the bound.
No kernel may reach another device: no remote copies, remote signals or barrier semaphores. Data moves between devices by JAX's collectives and lax.ppermute only.
A program may use at most 256 MiB of HBM per device.

v0:
```python
import jax
import jax.numpy as jnp
from jax import lax
from jax.sharding import PartitionSpec as P

D = 768
HEAD = 64


EPS = 1e-06
NEGATIVE = -1e30


def matmul_plain(left, right):
    return lax.dot_general(
        left, right, (((1,), (0,)), ((), ())), preferred_element_type=jnp.float32
    )


def matmul_trans(left, right):
    return lax.dot_general(
        left, right, (((1,), (1,)), ((), ())), preferred_element_type=jnp.float32
    )


def matmul_outer(left, right):
    return lax.dot_general(
        left, right, (((0,), (0,)), ((), ())), preferred_element_type=jnp.float32
    )


def rows_gather(values):
    return lax.all_gather(values, "row", axis=0, tiled=True)


def cols_gather(values):
    return lax.all_gather(values, "col", axis=0, tiled=True)


def cols_sum(values):
    return lax.psum_scatter(values, "col", scatter_dimension=0, tiled=True)


def rows_sum(values):
    return lax.psum_scatter(values, "row", scatter_dimension=0, tiled=True)


def feature_sums(values):
    return lax.psum(values, "col")


def norm_forward(states, gain):
    (squares,) = feature_sums((jnp.sum(states * states, axis=1),))
    scale = lax.rsqrt(squares / D + EPS)
    return ((states * scale[:, None] * gain).astype(jnp.bfloat16), scale)


def norm_backward(states, gain, scale, incoming):
    weighted = incoming * gain
    (inner,) = feature_sums((jnp.sum(weighted * states, axis=1),))
    through = scale[:, None] * weighted - states * (scale * scale * scale * inner / D)[:, None]
    grad_gain = jnp.sum(incoming * states * scale[:, None], axis=0)
    return (through, grad_gain)


def project_in(activity, weight):
    gathered = rows_gather(activity)
    result = cols_sum(matmul_plain(gathered, weight))
    return (gathered, result)


def project_out(activity, weight):
    gathered = cols_gather(activity)
    return (gathered, rows_sum(matmul_plain(gathered, weight)))


def back_out(grad_rows, gathered, weight):
    spread = rows_gather(grad_rows)
    carried = cols_sum(matmul_trans(spread, weight))
    return (matmul_outer(gathered, spread), carried)


def back_in(grad_cols, gathered, weight):
    spread = cols_gather(grad_cols)
    return (matmul_outer(gathered, spread), rows_sum(matmul_trans(spread, weight)))


def visible_mask(start, block, key_len, length):
    rows_now = start + lax.broadcasted_iota(jnp.int32, (block, key_len), 0)
    columns = lax.broadcasted_iota(jnp.int32, (block, key_len), 1)
    return (columns <= rows_now) | (columns < length)


def attend_forward(query, key, value, prefix, causal):
    count = prefix.shape[0]
    heads = query.shape[1] // HEAD
    query_len = query.shape[0] // count
    key_len = key.shape[0] // count
    block = min(512, query_len)
    blocks = query_len // block
    factor = HEAD ** (-0.5)
    queries = query.reshape(count * blocks, block, heads, HEAD)
    keys_all = key.reshape(count, key_len, heads, HEAD)
    values_all = value.reshape(count, key_len, heads, HEAD)

    def one_block(number):
        sequence = number // blocks
        start = number % blocks * block
        scores = (
            jnp.einsum(
                "qhe,khe->hqk",
                queries[number],
                keys_all[sequence],
                preferred_element_type=jnp.float32,
            )
            * factor
        )
        if causal:
            scores = jnp.where(
                visible_mask(start, block, key_len, prefix[sequence])[None], scores, NEGATIVE
            )
        highest = jnp.max(scores, axis=2, keepdims=True)
        totals = highest + jnp.log(jnp.sum(jnp.exp(scores - highest), axis=2, keepdims=True))
        weights = jnp.exp(scores - totals).astype(jnp.bfloat16)
        mixed = jnp.einsum(
            "hqk,khe->qhe", weights, values_all[sequence], preferred_element_type=jnp.float32
        )
        return (mixed.astype(jnp.bfloat16).reshape(block, heads * HEAD), totals[:, :, 0])

    mixed, totals = lax.map(one_block, jnp.arange(count * blocks, dtype=jnp.int32))
    return (mixed.reshape(count * query_len, heads * HEAD), totals)


def attend_backward(query, key, value, grad_mixed, totals, prefix, causal):
    count = prefix.shape[0]
    heads = query.shape[1] // HEAD
    query_len = query.shape[0] // count
    key_len = key.shape[0] // count
    block = min(512, query_len)
    blocks = query_len // block
    factor = HEAD ** (-0.5)
    queries = query.reshape(count, blocks, block, heads, HEAD)
    incoming = grad_mixed.reshape(count, blocks, block, heads, HEAD)
    sums_all = totals.reshape(count, blocks, heads, block)
    keys_all = key.reshape(count, key_len, heads, HEAD)
    values_all = value.reshape(count, key_len, heads, HEAD)

    def one_sequence(sequence):
        key_seq = keys_all[sequence]
        value_seq = values_all[sequence]
        length = prefix[sequence]

        def one_block(carry, item):
            grad_key, grad_value = carry
            query_block, grad_block, total_block, number = item
            scores = (
                jnp.einsum("qhe,khe->hqk", query_block, key_seq, preferred_element_type=jnp.float32)
                * factor
            )
            if causal:
                scores = jnp.where(
                    visible_mask(number * block, block, key_len, length)[None], scores, NEGATIVE
                )
            weights = jnp.exp(scores - total_block[:, :, None])
            rounded = weights.astype(jnp.bfloat16)
            grad_weights = jnp.einsum(
                "qhe,khe->hqk", grad_block, value_seq, preferred_element_type=jnp.float32
            )
            centre = jnp.sum(weights * grad_weights, axis=2, keepdims=True)
            grad_scores = (weights * (grad_weights - centre)).astype(jnp.bfloat16)
            grad_query = (
                jnp.einsum("hqk,khe->qhe", grad_scores, key_seq, preferred_element_type=jnp.float32)
                * factor
            )
            grad_key = (
                grad_key
                + jnp.einsum(
                    "hqk,qhe->khe", grad_scores, query_block, preferred_element_type=jnp.float32
                )
                * factor
            )
            grad_value = grad_value + jnp.einsum(
                "hqk,qhe->khe", rounded, grad_block, preferred_element_type=jnp.float32
            )
            return ((grad_key, grad_value), grad_query)

        empty = jnp.zeros((key_len, heads, HEAD), jnp.float32)
        (grad_key, grad_value), grad_query = lax.scan(
            one_block,
            (empty, empty),
            (
                queries[sequence],
                incoming[sequence],
                sums_all[sequence],
                jnp.arange(blocks, dtype=jnp.int32),
            ),
        )
        return (grad_query, grad_key, grad_value)

    grad_query, grad_key, grad_value = lax.map(one_sequence, jnp.arange(count, dtype=jnp.int32))
    return (
        grad_query.reshape(count * query_len, heads * HEAD).astype(jnp.bfloat16),
        grad_key.reshape(count * key_len, heads * HEAD).astype(jnp.bfloat16),
        grad_value.reshape(count * key_len, heads * HEAD).astype(jnp.bfloat16),
    )


def exit_blocks(hidden_full, targets, table_full):
    rows_all = hidden_full.shape[0]
    block = min(512, rows_all)
    blocks = rows_all // block
    vocab_local = table_full.shape[1]
    wanted = (targets - lax.axis_index("col") * vocab_local).reshape(blocks, block)
    pieces = hidden_full.reshape(blocks, block, hidden_full.shape[1])
    return (pieces, wanted, blocks, block)


def exit_forward(hidden_full, table_full, targets):
    pieces, wanted, blocks, block = exit_blocks(hidden_full, targets, table_full)

    def one_block(item):
        piece, wanted_now = item
        logits = matmul_plain(piece, table_full)
        columns = lax.broadcasted_iota(jnp.int32, logits.shape, 1)
        picked = jnp.sum(jnp.where(columns == wanted_now[:, None], logits, 0.0), axis=1)
        return (jnp.sum(jnp.exp(logits), axis=1), picked)

    exps, picked = lax.map(one_block, (pieces, wanted))
    totals, picked = feature_sums((exps.reshape(blocks * block), picked.reshape(blocks * block)))
    logsum = jnp.log(totals)
    return (logsum, logsum - picked)


def exit_backward(hidden_full, table_full, targets, logsum):
    pieces, wanted, blocks, block = exit_blocks(hidden_full, targets, table_full)

    def one_block(grad_table, item):
        piece, wanted_now, total_now = item
        logits = matmul_plain(piece, table_full)
        columns = lax.broadcasted_iota(jnp.int32, logits.shape, 1)
        onehot = jnp.where(columns == wanted_now[:, None], 1.0, 0.0)
        grad_logits = (jnp.exp(logits - total_now[:, None]) - onehot).astype(jnp.bfloat16)
        grad_table = grad_table + matmul_outer(piece, grad_logits)
        return (grad_table, matmul_trans(grad_logits, table_full))

    empty = jnp.zeros(table_full.shape, jnp.float32)
    grad_table, grad_hidden = lax.scan(
        one_block, empty, (pieces, wanted, logsum.reshape(blocks, block))
    )
    return (grad_table, grad_hidden.reshape(blocks * block, table_full.shape[0]))


def gate_product(gate, upward):
    return jax.nn.gelu(gate, approximate=True) * upward


def local(
    inputs,
    encoder,
    prefix,
    targets,
    gain_self,
    w_query,
    w_key,
    w_value,
    w_attn_out,
    gain_cross,
    w_cross_query,
    w_cross_key,
    w_cross_value,
    w_cross_out,
    gain_ff,
    w_gate,
    w_up,
    w_ff_out,
    gain_final,
    embed_table,
):
    states = inputs.astype(jnp.float32).T
    enc_rows = encoder.T
    down_weight = w_ff_out.T
    local_width = w_query.shape[1]
    ff_width = w_gate.shape[1]
    triple_weight = jnp.concatenate([w_query, w_key, w_value], axis=1)
    pair_weight = jnp.concatenate([w_cross_key, w_cross_value], axis=1)
    gate_weight = jnp.concatenate([w_gate, w_up], axis=1)
    normed_self, scale_self = norm_forward(states, gain_self)
    gathered_self, projected = project_in(normed_self, triple_weight)
    projected = projected.astype(jnp.bfloat16)
    query = projected[:, :local_width]
    key = projected[:, local_width : 2 * local_width]
    value = projected[:, 2 * local_width :]
    attended, totals_self = attend_forward(query, key, value, prefix, True)
    gathered_attended, branch = project_out(attended, w_attn_out)
    first = states + branch
    normed_cross, scale_cross = norm_forward(first, gain_cross)
    gathered_cross, cross_query = project_in(normed_cross, w_cross_query)
    cross_query = cross_query.astype(jnp.bfloat16)
    gathered_encoder, pairs = project_in(enc_rows, pair_weight)
    pairs = pairs.astype(jnp.bfloat16)
    cross_key = pairs[:, :local_width]
    cross_value = pairs[:, local_width:]
    crossed, totals_cross = attend_forward(cross_query, cross_key, cross_value, prefix, False)
    gathered_crossed, branch = project_out(crossed, w_cross_out)
    second = first + branch
    normed_ff, scale_ff = norm_forward(second, gain_ff)
    gathered_ff, gate_upward = project_in(normed_ff, gate_weight)
    gate = gate_upward[:, :ff_width]
    upward = gate_upward[:, ff_width:]
    hidden = gate_product(gate, upward).astype(jnp.bfloat16)
    gathered_hidden, branch = project_out(hidden, down_weight)
    third = second + branch
    normed_final, scale_final = norm_forward(third, gain_final)
    hidden_full = lax.all_gather(normed_final, "col", axis=1, tiled=True)
    table_full = lax.all_gather(embed_table, "row", axis=0, tiled=True)
    logsum, loss = exit_forward(hidden_full, table_full, targets)
    grad_table, grad_full = exit_backward(hidden_full, table_full, targets, logsum)
    grad_normed = lax.psum_scatter(
        grad_full.astype(jnp.bfloat16), "col", scatter_dimension=1, tiled=True
    ).astype(jnp.float32)
    grad_third, grad_gfinal = norm_backward(third, gain_final, scale_final, grad_normed)
    grad_down, grad_hidden = back_out(grad_third.astype(jnp.bfloat16), gathered_hidden, down_weight)
    unused, pull = jax.vjp(gate_product, gate, upward)
    grad_gate, grad_upward = pull(grad_hidden)
    grad_gates = jnp.concatenate([grad_gate, grad_upward], axis=1).astype(jnp.bfloat16)
    grad_gate_weight, grad_normed = back_in(grad_gates, gathered_ff, gate_weight)
    through, grad_gff = norm_backward(second, gain_ff, scale_ff, grad_normed)
    grad_second = grad_third + through
    grad_crossout, grad_crossed = back_out(
        grad_second.astype(jnp.bfloat16), gathered_crossed, w_cross_out
    )
    grad_cquery, grad_ckey, grad_cvalue = attend_backward(
        cross_query,
        cross_key,
        cross_value,
        grad_crossed.astype(jnp.bfloat16),
        totals_cross,
        prefix,
        False,
    )
    grad_crossquery, grad_normed = back_in(grad_cquery, gathered_cross, w_cross_query)
    grad_pair_weight, grad_encoder = back_in(
        jnp.concatenate([grad_ckey, grad_cvalue], axis=1), gathered_encoder, pair_weight
    )
    through, grad_gcross = norm_backward(first, gain_cross, scale_cross, grad_normed)
    grad_first = grad_second + through
    grad_attnout, grad_attended = back_out(
        grad_first.astype(jnp.bfloat16), gathered_attended, w_attn_out
    )
    grad_query, grad_key, grad_value = attend_backward(
        query, key, value, grad_attended.astype(jnp.bfloat16), totals_self, prefix, True
    )
    grad_triple, grad_normed = back_in(
        jnp.concatenate([grad_query, grad_key, grad_value], axis=1), gathered_self, triple_weight
    )
    through, grad_gself = norm_backward(states, gain_self, scale_self, grad_normed)
    grad_inputs = grad_first + through
    summed = (
        lax.psum_scatter(
            grad_triple[:, :local_width].astype(jnp.bfloat16), "dp", scatter_dimension=0, tiled=True
        ).astype(jnp.float32),
        lax.psum_scatter(
            grad_triple[:, local_width : 2 * local_width].astype(jnp.bfloat16),
            "dp",
            scatter_dimension=0,
            tiled=True,
        ).astype(jnp.float32),
        lax.psum_scatter(
            grad_triple[:, 2 * local_width :].astype(jnp.bfloat16),
            "dp",
            scatter_dimension=0,
            tiled=True,
        ).astype(jnp.float32),
        lax.psum_scatter(
            grad_attnout.astype(jnp.bfloat16), "dp", scatter_dimension=0, tiled=True
        ).astype(jnp.float32),
        lax.psum_scatter(
            grad_crossquery.astype(jnp.bfloat16), "dp", scatter_dimension=0, tiled=True
        ).astype(jnp.float32),
        lax.psum_scatter(
            grad_pair_weight[:, :local_width].astype(jnp.bfloat16),
            "dp",
            scatter_dimension=0,
            tiled=True,
        ).astype(jnp.float32),
        lax.psum_scatter(
            grad_pair_weight[:, local_width:].astype(jnp.bfloat16),
            "dp",
            scatter_dimension=0,
            tiled=True,
        ).astype(jnp.float32),
        lax.psum_scatter(
            grad_crossout.astype(jnp.bfloat16), "dp", scatter_dimension=0, tiled=True
        ).astype(jnp.float32),
        lax.psum_scatter(
            grad_gate_weight[:, :ff_width].astype(jnp.bfloat16),
            "dp",
            scatter_dimension=0,
            tiled=True,
        ).astype(jnp.float32),
        lax.psum_scatter(
            grad_gate_weight[:, ff_width:].astype(jnp.bfloat16),
            "dp",
            scatter_dimension=0,
            tiled=True,
        ).astype(jnp.float32),
        lax.psum_scatter(
            grad_down.T.astype(jnp.bfloat16), "dp", scatter_dimension=0, tiled=True
        ).astype(jnp.float32),
    )
    gains = lax.psum((grad_gself, grad_gcross, grad_gff, grad_gfinal), ("dp", "row"))
    grad_table = lax.psum_scatter(grad_table, ("dp", "row"), scatter_dimension=0, tiled=True)
    return (
        third.astype(jnp.bfloat16).T,
        loss,
        grad_inputs.T,
        grad_encoder.T,
        gains[0],
        summed[0],
        summed[1],
        summed[2],
        summed[3],
        gains[1],
        summed[4],
        summed[5],
        summed[6],
        summed[7],
        gains[2],
        summed[8],
        summed[9],
        summed[10],
        gains[3],
        grad_table,
    )


def solution(mesh):
    return jax.shard_map(
        local,
        mesh=mesh,
        in_specs=(
            P("col", ("dp", "row")),
            P("col", ("dp", "row")),
            P(("dp", "col")),
            P(("dp", "row")),
            P("col"),
            P("col", "row"),
            P("col", "row"),
            P("col", "row"),
            P("row", "col"),
            P("col"),
            P("col", "row"),
            P("col", "row"),
            P("col", "row"),
            P("row", "col"),
            P("col"),
            P("col", "row"),
            P("col", "row"),
            P("col", "row"),
            P("col"),
            P("row", "col"),
        ),
        out_specs=(
            P("col", ("dp", "row")),
            P(("dp", "row")),
            P("col", ("dp", "row")),
            P("col", ("dp", "row")),
            P("col"),
            P(("col", "dp"), "row"),
            P(("col", "dp"), "row"),
            P(("col", "dp"), "row"),
            P(("row", "dp"), "col"),
            P("col"),
            P(("col", "dp"), "row"),
            P(("col", "dp"), "row"),
            P(("col", "dp"), "row"),
            P(("row", "dp"), "col"),
            P("col"),
            P(("col", "dp"), "row"),
            P(("col", "dp"), "row"),
            P(("col", "dp"), "row"),
            P("col"),
            P(("dp", "row"), "col"),
        ),
        check_vma=False,
    )
```

profile of v0, /device:TPU:0, one launch (start us, length us, event | category | flops | bytes accessed | tf_op | source)
XLA Modules:
  0.0 2995.1 jit_solution(4276362468103125092)
XLA Ops:
  24.4 29.3 all-gather.17.cloned.1.call-done
  60.4 161.4 %reduce-scatter.28.cloned.1.call-done = f32[1024,576]{0,1:T(8,128)} async-done(((f32[4096,576]{0,1:T(8,128)}), f32[1024,576]{0,1:T(8,128)}) %reduce-scatter.28.cloned.1.call-update) | async-done | bytes 2359312 | tf_op jit(solution)/shard_map/reduce_scatter | solution.py:41
  245.4 38.0 %all-gather.19.cloned.1.call-done = bf16[4096,192]{0,1:T(8,128)(2,1)} async-done(((bf16[1024,192]{0,1:T(8,128)(2,1)}), bf16[4096,192]{0,1:T(8,128)(2,1)}) %all-gather.19.cloned.1.call-update) | async-done | bytes 1572880 | tf_op jit(solution)/shard_map/all_gather | solution.py:37
  287.9 42.3 %reduce-scatter.30.cloned.1.call-done = f32[1024,192]{0,1:T(8,128)} async-done(((f32[4096,192]{0,1:T(8,128)}), f32[1024,192]{0,1:T(8,128)}) %reduce-scatter.30.cloned.1.call-update) | async-done | bytes 786448 | tf_op jit(solution)/shard_map/reduce_scatter | solution.py:45
  344.2 31.7 %all-gather.23.cloned.1.call-done = bf16[8192,192]{0,1:T(8,128)(2,1)} async-done(((bf16[2048,192]{0,1:T(8,128)(2,1)}), bf16[8192,192]{0,1:T(8,128)(2,1)}) %all-gather.23.cloned.1.call-update) | async-done | bytes 3145744 | tf_op jit(solution)/shard_map/all_gather | solution.py:33
  413.2 210.2 %reduce-scatter.34.cloned.1.call-done = f32[2048,384]{0,1:T(8,128)} async-done(((f32[8192,384]{0,1:T(8,128)}), f32[2048,384]{0,1:T(8,128)}) %reduce-scatter.34.cloned.1.call-update) | async-done | bytes 3145744 | tf_op jit(solution)/shard_map/reduce_scatter | solution.py:41
  625.6 61.4 %reduce-scatter.32.cloned.1.call-done = f32[1024,192]{0,1:T(8,128)} async-done(((f32[4096,192]{0,1:T(8,128)}), f32[1024,192]{0,1:T(8,128)}) %reduce-scatter.32.cloned.1.call-update) | async-done | bytes 786448 | tf_op jit(solution)/shard_map/reduce_scatter | solution.py:41
  710.7 37.2 %all-gather.25.cloned.1.call-done = bf16[4096,192]{0,1:T(8,128)(2,1)} async-done(((bf16[1024,192]{0,1:T(8,128)(2,1)}), bf16[4096,192]{0,1:T(8,128)(2,1)}) %all-gather.25.cloned.1.call-update) | async-done | bytes 1572880 | tf_op jit(solution)/shard_map/all_gather | solution.py:37
  751.7 42.9 %reduce-scatter.36.cloned.1.call-done = f32[1024,192]{0,1:T(8,128)} async-done(((f32[4096,192]{0,1:T(8,128)}), f32[1024,192]{0,1:T(8,128)}) %reduce-scatter.36.cloned.1.call-update) | async-done | bytes 786448 | tf_op jit(solution)/shard_map/reduce_scatter | solution.py:45
  846.6 280.4 %reduce-scatter.38.cloned.1.call-done = f32[1024,1024]{1,0:T(8,128)} async-done(((f32[4096,1024]{1,0:T(8,128)}), f32[1024,1024]{1,0:T(8,128)}) %reduce-scatter.38.cloned.1.call-update) | async-done | bytes 4194320 | tf_op jit(solution)/shard_map/reduce_scatter | solution.py:41
  1131.0 81.6 %all-gather.29.cloned.1.call-done = bf16[4096,512]{1,0:T(8,128)(2,1)} async-done(((bf16[1024,512]{1,0:T(8,128)(2,1)}), bf16[4096,512]{1,0:T(8,128)(2,1)}) %all-gather.29.cloned.1.call-update) | async-done | bytes 4194320 | tf_op jit(solution)/shard_map/all_gather | solution.py:37
  1218.0 42.6 %reduce-scatter.40.cloned.1.call-done = f32[1024,192]{0,1:T(8,128)} async-done(((f32[4096,192]{0,1:T(8,128)}), f32[1024,192]{0,1:T(8,128)}) %reduce-scatter.40.cloned.1.call-update) | async-done | bytes 786448 | tf_op jit(solution)/shard_map/reduce_scatter | solution.py:45
  1276.3 33.2 %all-gather.31.cloned.1.call-done = bf16[1024,768]{0,1:T(8,128)(2,1)} async-done(((bf16[1024,192]{0,1:T(8,128)(2,1)}), bf16[1024,768]{0,1:T(8,128)(2,1)}) %all-gather.31.cloned.1.call-update) | async-done | bytes 1572880 | tf_op jit(solution)/shard_map/all_gather | solution.py:314
  1311.2 119.9 %all-gather.33.cloned.1.call-done = bf16[768,8032]{1,0:T(8,128)(2,1)} async-done(((bf16[192,8032]{1,0:T(8,128)(2,1)}), bf16[768,8032]{1,0:T(8,128)(2,1)}) %all-gather.33.cloned.1.call-update) | async-done | bytes 12337168 | tf_op jit(solution)/shard_map/all_gather | solution.py:315
  1431.1 32.1 %while.105 = (s32[]{:T(128)}, f32[2,512]{1,0:T(2,128)S(1)}, f32[2,512]{1,0:T(2,128)S(1)}, bf16[2,512,768]{2,1,0:T(8,128)(2,1)S(1)}, bf16[768,8032]{1,0:T(8,128)(...) while((s32[]{:T(128)}, f32[2,512]{1,0:T(2,128)S(1)}, f32[2,512]{1,0:T(2,128)S(1)}, ...), condition=%wide.region_26.27_spmd, body=%wide.region_23.26_spmd.sunk | while | flops 6333070336 | bytes 13142117 | solution.py:228
  1475.7 100.7 %while.106 = (s32[]{:T(128)}, f32[768,8032]{0,1:T(8,128)}, bf16[2,512,768]{2,1,0:T(8,128)(2,1)}, bf16[2,512,768]{2,1,0:T(8,128)(2,1)S(1)}, bf16[768,8032]{1,0:T(...) while((s32[]{:T(128)}, f32[768,8032]{0,1:T(8,128)}, ...), condition=%wide.region_30.31_spmd.clone, body=%wide.region_29.30_spmd.clone.sunk | while | flops 18982764544 | bytes 101905008 | solution.py:247
  1579.3 32.6 %reduce-scatter.42.cloned.1.call-done = bf16[1024,192]{0,1:T(8,128)(2,1)} async-done(((bf16[1024,768]{0,1:T(8,128)(2,1)}), bf16[1024,192]{0,1:T(8,128)(2,1)}) %reduce-scatter.42.cloned.1.call-update) | async-done | bytes 393232 | tf_op jit(solution)/shard_map/reduce_scatter | solution.py:318
  1625.5 29.3 all-gather.35.cloned.1.call-done
  1661.0 144.6 %reduce-scatter.44.cloned.1.call-done = f32[1024,512]{1,0:T(8,128)} async-done(((f32[4096,512]{1,0:T(8,128)}), f32[1024,512]{1,0:T(8,128)}) %reduce-scatter.44.cloned.1.call-update) | async-done | bytes 2097168 | tf_op jit(solution)/shard_map/reduce_scatter | solution.py:41
  1810.8 150.5 %all-gather.37.cloned.1.call-done = bf16[4096,1024]{1,0:T(8,128)(2,1)} async-done(((bf16[1024,1024]{1,0:T(8,128)(2,1)}), bf16[4096,1024]{1,0:T(8,128)(2,1)}) %all-gather.37.cloned.1.call-update) | async-done | bytes 8388624 | tf_op jit(solution)/shard_map/all_gather | solution.py:37
  1969.3 42.3 %reduce-scatter.46.cloned.1.call-done = f32[1024,192]{0,1:T(8,128)} async-done(((f32[4096,192]{0,1:T(8,128)}), f32[1024,192]{0,1:T(8,128)}) %reduce-scatter.46.cloned.1.call-update) | async-done | bytes 786448 | tf_op jit(solution)/shard_map/reduce_scatter | solution.py:45
  2059.9 60.3 %reduce-scatter.48.cloned.1.call-done = f32[1024,192]{0,1:T(8,128)} async-done(((f32[4096,192]{0,1:T(8,128)}), f32[1024,192]{0,1:T(8,128)}) %reduce-scatter.48.cloned.1.call-update) | async-done | bytes 786448 | tf_op jit(solution)/shard_map/reduce_scatter | solution.py:41
  2126.8 54.4 %while.107 = (s32[]{:T(128)}, f32[2048,3,64]{0,2,1:T(8,128)S(1)}, f32[2048,3,64]{0,2,1:T(8,128)}, bf16[2,512,3,64]{1,3,2,0:T(8,128)(2,1)}, bf16[2,512,3,64]{1,3,...) while((s32[]{:T(128)}, f32[2048,3,64]{0,2,1:T(8,128)S(1)}, ...), condition=%wide.region_41.42_spmd.clone, body=%wide.region_39.41_spmd.clone.sunk | while | flops 2053077504 | bytes 206485744 | solution.py:188
  2183.6 37.2 %all-gather.41.cloned.1.call-done = bf16[4096,192]{0,1:T(8,128)(2,1)} async-done(((bf16[1024,192]{0,1:T(8,128)(2,1)}), bf16[4096,192]{0,1:T(8,128)(2,1)}) %all-gather.41.cloned.1.call-update) | async-done | bytes 1572880 | tf_op jit(solution)/shard_map/all_gather | solution.py:37
  2224.5 42.9 %reduce-scatter.50.cloned.1.call-done = f32[1024,192]{0,1:T(8,128)} async-done(((f32[4096,192]{0,1:T(8,128)}), f32[1024,192]{0,1:T(8,128)}) %reduce-scatter.50.cloned.1.call-update) | async-done | bytes 786448 | tf_op jit(solution)/shard_map/reduce_scatter | solution.py:45
  2317.8 57.4 %reduce-scatter.52.cloned.1.call-done = f32[1024,192]{0,1:T(8,128)} async-done(((f32[4096,192]{0,1:T(8,128)}), f32[1024,192]{0,1:T(8,128)}) %reduce-scatter.52.cloned.1.call-update) | async-done | bytes 786448 | tf_op jit(solution)/shard_map/reduce_scatter | solution.py:41
  2377.5 37.5 %while.108 = (s32[]{:T(128)}, f32[1024,3,64]{0,2,1:T(8,128)}, f32[1024,3,64]{0,2,1:T(8,128)}, bf16[2,512,3,64]{1,3,2,0:T(8,128)(2,1)}, bf16[2,512,3,64]{1,3,2,0:...) while((s32[]{:T(128)}, f32[1024,3,64]{0,2,1:T(8,128)}, ...), condition=%wide.region_48.49_spmd.clone, body=%wide.region_46.48_spmd.clone.sunk | while | flops 1032355840 | bytes 115659200 | solution.py:188
  2437.3 55.6 %all-gather.47.cloned.1.call-done = bf16[8192,384]{0,1:T(8,128)(2,1)} async-done(((bf16[2048,384]{0,1:T(8,128)(2,1)}), bf16[8192,384]{0,1:T(8,128)(2,1)}) %all-gather.47.cloned.1.call-update) | async-done | bytes 6291472 | tf_op jit(solution)/shard_map/all_gather | solution.py:37
  2503.1 79.6 %all-gather.45.cloned.1.call-done = bf16[4096,576]{0,1:T(8,128)(2,1)} async-done(((bf16[1024,576]{0,1:T(8,128)(2,1)}), bf16[4096,576]{0,1:T(8,128)(2,1)}) %all-gather.45.cloned.1.call-update) | async-done | bytes 4718608 | tf_op jit(solution)/shard_map/all_gather | solution.py:37
  2707.8 47.0 %reduce-scatter.54.cloned.1.call-done = f32[1024,192]{0,1:T(8,128)} async-done(((f32[4096,192]{0,1:T(8,128)}), f32[1024,192]{0,1:T(8,128)}) %reduce-scatter.54.cloned.1.call-update) | async-done | bytes 786448 | tf_op jit(solution)/shard_map/reduce_scatter | solution.py:45
  2785.8 128.5 %reduce-scatter.80.cloned.1.call-done = f32[96,8032]{1,0:T(8,128)} async-done(((f32[768,8032]{1,0:T(8,128)}), f32[96,8032]{1,0:T(8,128)}) %reduce-scatter.80.cloned.1.call-update) | async-done | bytes 3084304 | tf_op jit(solution)/shard_map/reduce_scatter | solution.py:412
  2914.4 73.6 %reduce-scatter.56.cloned.1.call-done = f32[2048,192]{0,1:T(8,128)} async-done(((f32[8192,192]{0,1:T(8,128)}), f32[2048,192]{0,1:T(8,128)}) %reduce-scatter.56.cloned.1.call-update) | async-done | bytes 1572880 | tf_op jit(solution)/shard_map/reduce_scatter | solution.py:45
  (514 shorter events, 813.4 us)
Async XLA Ops:
  24.3 197.4 %reduce-scatter.28.cloned.1.call-start = ((), (), s32[]{:S(2)}) async-start(), calls=%async_computation.28 | async-start | bytes 11796480 | tf_op jit(solution)/shard_map/reduce_scatter | solution.py:41
  60.3 223.1 %all-gather.19.cloned.1.call-start = ((), (), s32[]{:S(2)}) async-start(), calls=%async_computation.29 | async-start | bytes 1966080 | tf_op jit(solution)/shard_map/all_gather | solution.py:37
  287.8 121.4 %all-gather.21.cloned.1.call-start = ((), (), s32[]{:S(2)}) async-start(), calls=%async_computation.31 | async-start | bytes 1966080 | tf_op jit(solution)/shard_map/all_gather | solution.py:33
  344.1 279.3 %reduce-scatter.34.cloned.1.call-start = ((), (), s32[]{:S(2)}) async-start(), calls=%async_computation.34 | async-start | bytes 15728640 | tf_op jit(solution)/shard_map/reduce_scatter | solution.py:41
  384.3 302.7 %reduce-scatter.32.cloned.1.call-start = ((), (), s32[]{:S(2)}) async-start(), calls=%async_computation.32 | async-start | bytes 3932160 | tf_op jit(solution)/shard_map/reduce_scatter | solution.py:41
  412.9 335.1 %all-gather.25.cloned.1.call-start = ((), (), s32[]{:S(2)}) async-start(), calls=%async_computation.35 | async-start | bytes 1966080 | tf_op jit(solution)/shard_map/all_gather | solution.py:37
  808.6 318.4 %reduce-scatter.38.cloned.1.call-start = ((), (), s32[]{:S(2)}) async-start(), calls=%async_computation.38 | async-start | bytes 20971520 | tf_op jit(solution)/shard_map/reduce_scatter | solution.py:41
  846.5 366.0 %all-gather.29.cloned.1.call-start = ((), (), s32[]{:S(2)}) async-start(), calls=%async_computation.39 | async-start | bytes 5242880 | tf_op jit(solution)/shard_map/all_gather | solution.py:37
  1130.9 129.6 %reduce-scatter.40.cloned.1.call-start = ((), (), s32[]{:S(2)}) async-start(), calls=%async_computation.40 | async-start | bytes 3932160 | tf_op jit(solution)/shard_map/reduce_scatter | solution.py:45
  1275.0 156.1 %all-gather.33.cloned.1.call-start = ((), (), s32[]{:S(2)}) async-start(), calls=%async_computation.42 | async-start | bytes 15482880 | tf_op jit(solution)/shard_map/all_gather | solution.py:315
  1275.6 336.4 %reduce-scatter.42.cloned.1.call-start = ((), (), s32[]{:S(2)}) async-start(), calls=%async_computation.43 | async-start | bytes 1966080 | tf_op jit(solution)/shard_map/reduce_scatter | solution.py:318
  1625.5 180.0 %reduce-scatter.44.cloned.1.call-start = ((), (), s32[]{:S(2)}) async-start(), calls=%async_computation.45 | async-start | bytes 10485760 | tf_op jit(solution)/shard_map/reduce_scatter | solution.py:41
  1660.9 300.4 %all-gather.37.cloned.1.call-start = ((), (), s32[]{:S(2)}) async-start(), calls=%async_computation.46 | async-start | bytes 10485760 | tf_op jit(solution)/shard_map/all_gather | solution.py:37
  1810.8 200.8 %reduce-scatter.46.cloned.1.call-start = ((), (), s32[]{:S(2)}) async-start(), calls=%async_computation.47 | async-start | bytes 3932160 | tf_op jit(solution)/shard_map/reduce_scatter | solution.py:45
  2027.8 92.4 %reduce-scatter.48.cloned.1.call-start = ((), (), s32[]{:S(2)}) async-start(), calls=%async_computation.49 | async-start | bytes 3932160 | tf_op jit(solution)/shard_map/reduce_scatter | solution.py:41
  2059.8 160.9 %all-gather.41.cloned.1.call-start = ((), (), s32[]{:S(2)}) async-start(), calls=%async_computation.50 | async-start | bytes 1966080 | tf_op jit(solution)/shard_map/all_gather | solution.py:37
  2314.8 178.0 %all-gather.47.cloned.1.call-start = ((), (), s32[]{:S(2)}) async-start(), calls=%async_computation.56 | async-start | bytes 7864320 | tf_op jit(solution)/shard_map/all_gather | solution.py:37
  2317.7 264.9 %all-gather.45.cloned.1.call-start = ((), (), s32[]{:S(2)}) async-start(), calls=%async_computation.54 | async-start | bytes 5898240 | tf_op jit(solution)/shard_map/all_gather | solution.py:37
  2420.1 208.2 %reduce-scatter.78.cloned.1.call-start = ((), (), s32[]{:S(2)}) async-start(), calls=%async_computation.68 | async-start | bytes 294912 | tf_op jit(solution)/shard_map/reduce_scatter | solution.py:407
  2424.1 205.8 %reduce-scatter.74.cloned.1.call-start = ((), (), s32[]{:S(2)}) async-start(), calls=%async_computation.66 | async-start | bytes 294912 | tf_op jit(solution)/shard_map/reduce_scatter | solution.py:395
  2430.8 200.7 %reduce-scatter.76.cloned.1.call-start = ((), (), s32[]{:S(2)}) async-start(), calls=%async_computation.67 | async-start | bytes 294912 | tf_op jit(solution)/shard_map/reduce_scatter | solution.py:401
  2431.5 201.5 %reduce-scatter.72.cloned.1.call-start = ((), (), s32[]{:S(2)}) async-start(), calls=%async_computation.65 | async-start | bytes 147456 | tf_op jit(solution)/shard_map/reduce_scatter | solution.py:392
  2434.3 203.4 %reduce-scatter.66.cloned.1.call-start = ((), (), s32[]{:S(2)}) async-start(), calls=%async_computation.62 | async-start | bytes 147456 | tf_op jit(solution)/shard_map/reduce_scatter | solution.py:377
  2437.0 212.2 %reduce-scatter.68.cloned.1.call-start = ((), (), s32[]{:S(2)}) async-start(), calls=%async_computation.63 | async-start | bytes 147456 | tf_op jit(solution)/shard_map/reduce_scatter | solution.py:380
  2499.5 161.0 %reduce-scatter.70.cloned.1.call-start = ((), (), s32[]{:S(2)}) async-start(), calls=%async_computation.64 | async-start | bytes 147456 | tf_op jit(solution)/shard_map/reduce_scatter | solution.py:386
  2500.1 171.8 %reduce-scatter.64.cloned.1.call-start = ((), (), s32[]{:S(2)}) async-start(), calls=%async_computation.61 | async-start | bytes 147456 | tf_op jit(solution)/shard_map/reduce_scatter | solution.py:374
  2503.1 180.4 %reduce-scatter.58.cloned.1.call-start = ((), (), s32[]{:S(2)}) async-start(), calls=%async_computation.58 | async-start | bytes 147456 | tf_op jit(solution)/shard_map/reduce_scatter | solution.py:359
  2587.7 107.1 %reduce-scatter.60.cloned.1.call-start = ((), (), s32[]{:S(2)}) async-start(), calls=%async_computation.59 | async-start | bytes 147456 | tf_op jit(solution)/shard_map/reduce_scatter | solution.py:362
  2588.3 118.1 %reduce-scatter.62.cloned.1.call-start = ((), (), s32[]{:S(2)}) async-start(), calls=%async_computation.60 | async-start | bytes 147456 | tf_op jit(solution)/shard_map/reduce_scatter | solution.py:368
  2589.0 165.7 %reduce-scatter.54.cloned.1.call-start = ((), (), s32[]{:S(2)}) async-start(), calls=%async_computation.55 | async-start | bytes 3932160 | tf_op jit(solution)/shard_map/reduce_scatter | solution.py:45
  2594.6 319.8 %reduce-scatter.80.cloned.1.call-start = ((), (), s32[]{:S(2)}) async-start(), calls=%async_computation.69 | async-start | bytes 27869184 | tf_op jit(solution)/shard_map/reduce_scatter | solution.py:412
  2619.4 368.6 %reduce-scatter.56.cloned.1.call-start = ((), (), s32[]{:S(2)}) async-start(), calls=%async_computation.57 | async-start | bytes 7864320 | tf_op jit(solution)/shard_map/reduce_scatter | solution.py:45
  (111 other events, 7802.9 us)
Sparse Core Ops, SparseCore 0:
  24.5 29.1 all-gather.16
  60.5 161.2 reduce-scatter.27
  245.5 37.9 all-gather.18
  287.3 42.8 reduce-scatter.29
  331.9 43.9 all-gather.22
  378.2 30.9 all-gather.20
  411.5 211.8 reduce-scatter.33
  625.7 61.3 reduce-scatter.31
  710.8 37.0 all-gather.24
  751.8 42.8 reduce-scatter.35
  808.7 28.1 all-gather.26
  846.7 280.2 reduce-scatter.37
  1131.0 81.4 all-gather.28
  1218.1 42.4 reduce-scatter.39
  1275.1 34.3 all-gather.30
  1311.3 119.7 all-gather.32
  1579.4 32.5 reduce-scatter.41
  1625.6 29.1 all-gather.34
  1661.0 144.4 reduce-scatter.43
  1810.9 150.3 all-gather.36
  1969.4 42.1 reduce-scatter.45
  2027.9 28.2 all-gather.38
  2059.9 60.2 reduce-scatter.47
  2183.6 37.1 all-gather.40
  2224.5 42.8 reduce-scatter.49
  2282.9 28.1 all-gather.42
  2314.9 60.2 reduce-scatter.51
  2377.4 115.3 all-gather.46
  2495.0 87.5 all-gather.44
  2709.6 45.1 reduce-scatter.53
  2759.6 154.7 reduce-scatter.79
  2917.8 70.1 reduce-scatter.55
  (11 shorter events, 91.8 us)
where the time goes:
time: 3010 us; the launch traced here: 3000 us
  waiting for transfers between devices  2370 us (79%)
  matrix products  328 us (11%)
  blocking collectives  120 us (4%)
  other arithmetic  91.8 us (3%)
  local copies, waits for them, and re-layouts  53.2 us (2%)
    reduce_scatter x7, waiting for transfers between devices, cols_sum(): return lax.psum_scatter(values, 'col', scatter_dimension=0, tiled=True)  976 us
    all_gather x7, waiting for transfers between devices, cols_gather(): return lax.all_gather(values, 'col', axis=0, tiled=True)  480 us
    reduce_scatter x7, waiting for transfers between devices, rows_sum(): return lax.psum_scatter(values, 'row', scatter_dimension=0, tiled=True)  334 us
    all_gather x7, waiting for transfers between devices, rows_gather(): return lax.all_gather(values, 'row', axis=0, tiled=True)  200 us
    reduce_scatter x1, waiting for transfers between devices, local(): lax.psum_scatter(grad_table, ('dp', 'row'), scatter_dimension=0, tiled=True)  129 us
    all_gather x1, waiting for transfers between devices, local(): table_full = lax.all_gather(embed_table, 'row', axis=0, tiled=True)  120 us
    dot_general x11, matrix products, matmul_plain(): lax.dot_general(left, right, (((1,), (0,)), ((), ())), preferred_element_...  109 us
    psum x9, blocking collectives, feature_sums(): return lax.psum(values, 'col')  105 us
  transfers between devices with their start and end apart: 43, of which 39 were waited for; matrix products, arithmetic and copies ran while one was open for 5% of the time, Pallas kernels for 0%

commit v1 on v0

v1 whole, which is shorter than its diff:
```python
from functools import partial

import jax
import jax.numpy as jnp
from jax import lax
from jax.experimental import pallas as pl
from jax.experimental.pallas import tpu as pltpu
from jax.sharding import PartitionSpec as P

HEAD = 64
EPS = 1e-06
NEGATIVE = -1e30
BF = jnp.bfloat16
F32 = jnp.float32
MIB = 1 << 20


def mm(left, right, dims):
    return lax.dot_general(left, right, (dims, ((), ())), preferred_element_type=F32)


def nn(left, right):
    return mm(left, right, ((1,), (0,)))


def tn(left, right):
    return mm(left, right, ((0,), (0,)))


def nt(left, right):
    return mm(left, right, ((1,), (1,)))


def params(mib, axes=1):
    return pltpu.CompilerParams(
        dimension_semantics=("arbitrary",) * axes, vmem_limit_bytes=mib * MIB
    )


def whole(shape):
    return pl.BlockSpec(shape, lambda *_: (0,) * len(shape))


def scores_of(key, query, start, prefix, causal):
    scores = tn(key, query * jnp.asarray(HEAD**-0.5, BF))
    if causal:
        keys = lax.broadcasted_iota(jnp.int32, scores.shape, 0)
        rows = lax.broadcasted_iota(jnp.int32, scores.shape, 1) + start
        scores = jnp.where((keys <= rows) | (keys < prefix), scores, NEGATIVE)
    return scores


def attend_forward(info, query, key, value, causal):
    (q_arr, q_row, q_moves), (k_arr, k_row), (v_arr, v_row) = query, key, value
    tq = info["tq"]
    blocks = q_arr.shape[0]
    heads = info["heads"]
    tk = k_arr.shape[2]

    def body(s_ref, q_ref, k_ref, v_ref, o_ref, l_ref):
        scores = scores_of(k_ref[0], q_ref[0], s_ref[0] * tq, s_ref[1], causal)
        top = jnp.max(scores, axis=0, keepdims=True)
        weights = jnp.exp(scores - top)
        total = jnp.sum(weights, axis=0, keepdims=True)
        mixed = nn(v_ref[0], weights.astype(BF))
        o_ref[0] = (mixed / total).astype(BF)
        l_ref[0] = top + jnp.log(total)

    return pl.pallas_call(
        body,
        out_shape=(
            jax.ShapeDtypeStruct((blocks, heads * HEAD, tq), BF),
            jax.ShapeDtypeStruct((blocks * heads, 1, tq), F32),
        ),
        grid_spec=pltpu.PrefetchScalarGridSpec(
            num_scalar_prefetch=1,
            grid=(blocks, heads),
            in_specs=[
                pl.BlockSpec(
                    (1, HEAD, tq), lambda b, h, s: (b, q_row + h, s[0] if q_moves else 0)
                ),
                pl.BlockSpec((1, HEAD, tk), lambda b, h, s: (b, k_row + h, 0)),
                pl.BlockSpec((1, HEAD, tk), lambda b, h, s: (b, v_row + h, 0)),
            ],
            out_specs=(
                pl.BlockSpec((1, HEAD, tq), lambda b, h, s: (b, h, 0)),
                pl.BlockSpec((1, 1, tq), lambda b, h, s: (b * heads + h, 0, 0)),
            ),
        ),
        compiler_params=params(48, 2),
    )(info["scalars"], q_arr, k_arr, v_arr)


def attend_backward(info, query, key, value, incoming, totals, causal):
    (q_arr, q_row, q_moves), (k_arr, k_row), (v_arr, v_row) = query, key, value
    tq = info["tq"]
    blocks = q_arr.shape[0]
    heads = info["heads"]
    tk = k_arr.shape[2]

    def body(s_ref, q_ref, k_ref, v_ref, g_ref, l_ref, dq_ref, dk_ref, dv_ref):
        q = q_ref[0]
        scores = scores_of(k_ref[0], q, s_ref[0] * tq, s_ref[1], causal)
        weights = jnp.exp(scores - l_ref[0])
        dp = tn(v_ref[0], g_ref[0])
        inner = weights * dp
        centre = jnp.sum(inner, axis=0, keepdims=True)
        ds = (inner - weights * centre).astype(BF)
        dv_ref[0] = nt(g_ref[0], weights.astype(BF)).astype(BF)
        dq_ref[0] = (nn(k_ref[0], ds) * HEAD**-0.5).astype(BF)
        dk_ref[0] = (nt(q, ds) * HEAD**-0.5).astype(BF)

    return pl.pallas_call(
        body,
        out_shape=(
            jax.ShapeDtypeStruct((blocks, heads * HEAD, tq), BF),
            jax.ShapeDtypeStruct((blocks, heads * HEAD, tk), BF),
            jax.ShapeDtypeStruct((blocks, heads * HEAD, tk), BF),
        ),
        grid_spec=pltpu.PrefetchScalarGridSpec(
            num_scalar_prefetch=1,
            grid=(blocks, heads),
            in_specs=[
                pl.BlockSpec(
                    (1, HEAD, tq), lambda b, h, s: (b, q_row + h, s[0] if q_moves else 0)
                ),
                pl.BlockSpec((1, HEAD, tk), lambda b, h, s: (b, k_row + h, 0)),
                pl.BlockSpec((1, HEAD, tk), lambda b, h, s: (b, v_row + h, 0)),
                pl.BlockSpec((1, HEAD, tq), lambda b, h, s: (b, h, 0)),
                pl.BlockSpec((1, 1, tq), lambda b, h, s: (b * heads + h, 0, 0)),
            ],
            out_specs=(
                pl.BlockSpec((1, HEAD, tq), lambda b, h, s: (b, h, 0)),
                pl.BlockSpec((1, HEAD, tk), lambda b, h, s: (b, h, 0)),
                pl.BlockSpec((1, HEAD, tk), lambda b, h, s: (b, h, 0)),
            ),
        ),
        compiler_params=params(48, 2),
    )(info["scalars"], q_arr, k_arr, v_arr, incoming, totals)


GELU_A = 0.7978845608028654
GELU_B = 0.044715


def gelu_parts(gate):
    inner = jnp.tanh(GELU_A * (gate + GELU_B * gate * gate * gate))
    value = 0.5 * gate * (1.0 + inner)
    slope = 0.5 * (1.0 + inner) + 0.5 * gate * (1.0 - inner * inner) * (
        GELU_A * (1.0 + 3.0 * GELU_B * gate * gate)
    )
    return value, slope


def ff_forward(packs, normed):
    blocks, d, lanes = packs[0].shape
    wide = lanes // 3
    tokens = normed.shape[1]
    n = len(packs)

    def body(*refs):
        w_refs, x_ref, save_refs, out_ref = refs[:n], refs[n], refs[n + 1 : 2 * n + 1], refs[-1]

        @pl.when(pl.program_id(0) == 0)
        def _():
            out_ref[...] = jnp.zeros_like(out_ref)

        for w_ref, save_ref in zip(w_refs, save_refs):
            both = tn(w_ref[0, :, : 2 * wide], x_ref[...])
            save_ref[0] = both
            value, _ = gelu_parts(both[:wide])
            hidden = (value * both[wide:]).astype(BF)
            out_ref[...] += nn(w_ref[0, :, 2 * wide :], hidden)

    return pl.pallas_call(
        body,
        grid=(blocks,),
        in_specs=[pl.BlockSpec((1, d, lanes), lambda b: (b, 0, 0))] * n
        + [whole((d, tokens))],
        out_specs=[pl.BlockSpec((1, 2 * wide, tokens), lambda b: (b, 0, 0))] * n
        + [whole((d, tokens))],
        out_shape=[jax.ShapeDtypeStruct((blocks, 2 * wide, tokens), F32)] * n
        + [jax.ShapeDtypeStruct((d, tokens), F32)],
        compiler_params=params(48),
    )(*packs, normed)


def ff_backward(packs, saved, normed, grad):
    blocks, d, lanes = packs[0].shape
    wide = lanes // 3
    tokens = normed.shape[1]
    n = len(packs)

    def body(*refs):
        w_refs, save_refs = refs[:n], refs[n : 2 * n]
        x_ref, g_ref = refs[2 * n], refs[2 * n + 1]
        dw_refs, out_ref = refs[2 * n + 2 : 3 * n + 2], refs[-1]

        @pl.when(pl.program_id(0) == 0)
        def _():
            out_ref[...] = jnp.zeros_like(out_ref)

        for w_ref, save_ref, dw_ref in zip(w_refs, save_refs, dw_refs):
            dh = tn(w_ref[0, :, 2 * wide :], g_ref[...])
            gate, up = save_ref[0, :wide], save_ref[0, wide:]
            value, slope = gelu_parts(gate)
            hidden = (value * up).astype(BF)
            grads = jnp.concatenate(
                [(dh * up * slope).astype(BF), (dh * value).astype(BF)], axis=0
            )
            dw_ref[0, :, : 2 * wide] = nt(x_ref[...], grads).astype(BF)
            dw_ref[0, :, 2 * wide :] = nt(g_ref[...], hidden).astype(BF)
            out_ref[...] += nn(w_ref[0, :, : 2 * wide], grads)

    return pl.pallas_call(
        body,
        grid=(blocks,),
        in_specs=[pl.BlockSpec((1, d, lanes), lambda b: (b, 0, 0))] * n
        + [pl.BlockSpec((1, 2 * wide, tokens), lambda b: (b, 0, 0))] * n
        + [whole((d, tokens))] * 2,
        out_specs=[pl.BlockSpec((1, d, lanes), lambda b: (b, 0, 0))] * n
        + [whole((d, tokens))],
        out_shape=[jax.ShapeDtypeStruct((blocks, d, lanes), BF)] * n
        + [jax.ShapeDtypeStruct((d, tokens), F32)],
        compiler_params=params(56),
    )(*packs, *saved, normed, grad)


def project(pack, normed, low, high):
    blocks, d, _ = pack.shape
    tokens = normed.shape[1]

    def body(w_ref, x_ref, o_ref):
        o_ref[0] = tn(w_ref[0, :, low:high], x_ref[...]).astype(BF)

    return pl.pallas_call(
        body,
        grid=(blocks,),
        in_specs=[pl.BlockSpec((1, d, pack.shape[2]), lambda b: (b, 0, 0)), whole((d, tokens))],
        out_specs=pl.BlockSpec((1, high - low, tokens), lambda b: (b, 0, 0)),
        out_shape=jax.ShapeDtypeStruct((blocks, high - low, tokens), BF),
        compiler_params=params(40),
    )(pack, normed)


def combine(pack, rows, low, high, kind=F32):
    blocks, d, _ = pack.shape
    tokens = rows.shape[2]

    def body(w_ref, x_ref, o_ref):
        @pl.when(pl.program_id(0) == 0)
        def _():
            o_ref[...] = jnp.zeros_like(o_ref)

        o_ref[...] += nn(w_ref[0, :, low:high], x_ref[0])

    return pl.pallas_call(
        body,
        grid=(blocks,),
        in_specs=[
            pl.BlockSpec((1, d, pack.shape[2]), lambda b: (b, 0, 0)),
            pl.BlockSpec((1, high - low, tokens), lambda b: (b, 0, 0)),
        ],
        out_specs=whole((d, tokens)),
        out_shape=jax.ShapeDtypeStruct((d, tokens), kind),
        compiler_params=params(40),
    )(pack, rows)


def weight_grads(pairs, lanes):
    d = pairs[0][0].shape[0]
    blocks = pairs[0][1].shape[0]
    n = len(pairs)
    lefts = [left for left, _ in pairs]
    rights = [right for _, right in pairs]

    def body(*refs):
        out_ref = refs[-1]
        at = 0
        for left_ref, right_ref in zip(refs[:n], refs[n : 2 * n]):
            width = right_ref.shape[1]
            out_ref[0, :, at : at + width] = nt(left_ref[...], right_ref[0]).astype(BF)
            at += width

    return pl.pallas_call(
        body,
        grid=(blocks,),
        in_specs=[whole(left.shape) for left in lefts]
        + [pl.BlockSpec((1,) + right.shape[1:], lambda b: (b, 0, 0)) for right in rights],
        out_specs=pl.BlockSpec((1, d, lanes), lambda b: (b, 0, 0)),
        out_shape=jax.ShapeDtypeStruct((blocks, d, lanes), BF),
        compiler_params=params(48),
    )(*lefts, *rights)


def source_grads(pack, own, own_low, wide, wide_low, place, width, kind):
    blocks, d, lanes = pack.shape
    tq = own.shape[2] if own is not None else 0
    n = len(wide)
    tokens = wide[0].shape[2]
    step = min(1024, tokens)

    def body(*refs):
        s_ref, w_ref = refs[0], refs[1]
        wide_refs = refs[2 : 2 + n]
        o_ref = refs[-1]
        acc = jnp.zeros((d, step), F32)
        for b in range(blocks):
            for at, ref in zip(wide_low, wide_refs):
                acc += nn(w_ref[b, :, at : at + width], ref[b])
        o_ref[...] = acc.astype(kind)
        if own is not None:
            own_ref = refs[2 + n]
            part = jnp.zeros((d, tq), F32)
            for b in range(blocks):
                part += nn(w_ref[b, :, own_low : own_low + width], own_ref[b])
            where = pl.ds(pl.multiple_of(s_ref[0] * tq, tq), tq)
            o_ref[:, where] += part.astype(kind)

    return pl.pallas_call(
        body,
        out_shape=jax.ShapeDtypeStruct((d, tokens), kind),
        grid_spec=pltpu.PrefetchScalarGridSpec(
            num_scalar_prefetch=1,
            grid=(tokens // step,),
            in_specs=[pl.BlockSpec((blocks, d, lanes), lambda i, s: (0, 0, 0))]
            + [pl.BlockSpec((blocks, width, step), lambda i, s: (0, 0, i))] * n
            + (
                [pl.BlockSpec((blocks, width, tq), lambda i, s: (0, 0, 0))]
                if own is not None
                else []
            ),
            out_specs=pl.BlockSpec((d, step), lambda i, s: (0, i)),
        ),
        compiler_params=params(40),
    )(place, pack, *wide, *([own] if own is not None else []))


VB = 512


def assemble(s_ref, own_ref, one_ref, two_ref, out_ref):
    size = own_ref.shape[0]
    out_ref[:size] = own_ref[...]
    out_ref[pl.ds(pl.multiple_of((1 + s_ref[1]) * size, size), size), :] = one_ref[...]
    out_ref[pl.ds(pl.multiple_of((2 - s_ref[1]) * size, size), size), :] = two_ref[0]
    out_ref[3 * size :] = two_ref[1]


def table_specs(size):
    return [
        pl.BlockSpec((size, VB), lambda v, s: (0, v)),
        pl.BlockSpec((size, VB), lambda v, s: (0, v)),
        pl.BlockSpec((2, size, VB), lambda v, s: (0, 0, v)),
    ]


def vocab_forward(scalars, hidden, table, wanted):
    chunks, d, step = hidden.shape
    own, one, two = table
    size, width = own.shape
    parts = width // VB

    def body(s_ref, h_ref, own_ref, one_ref, two_ref, t_ref, e_ref, m_ref, top_ref, sum_ref, pick_ref, blk, flip):
        vb = pl.program_id(0)

        @pl.when(vb == 0)
        def _():
            top_ref[...] = jnp.full_like(top_ref, NEGATIVE)
            sum_ref[...] = jnp.zeros_like(sum_ref)
            pick_ref[...] = jnp.zeros_like(pick_ref)

        assemble(s_ref, own_ref, one_ref, two_ref, blk)
        flip[...] = blk[...].T
        ids = lax.broadcasted_iota(jnp.int32, (VB, step), 0) + vb * VB

        def one_chunk(n, carry):
            logits = nn(flip[...], h_ref[n])
            pick_ref[n] += jnp.sum(
                jnp.where(ids == t_ref[n], logits, 0.0), axis=0, keepdims=True
            )
            logits = jnp.where(ids < s_ref[0], logits, NEGATIVE)
            before = top_ref[n]
            top = jnp.maximum(before, jnp.max(logits, axis=0, keepdims=True))
            exps = jnp.exp(logits - top)
            sum_ref[n] = sum_ref[n] * jnp.exp(before - top) + jnp.sum(
                exps, axis=0, keepdims=True
            )
            top_ref[n] = top
            m_ref[0, n] = top
            e_ref[n] = exps.astype(BF)
            return carry

        lax.fori_loop(0, chunks, one_chunk, 0)

    row = jax.ShapeDtypeStruct((chunks, 1, step), F32)
    return pl.pallas_call(
        body,
        out_shape=(
            jax.ShapeDtypeStruct((chunks, width, step), BF),
            jax.ShapeDtypeStruct((parts, chunks, 1, step), F32),
            row,
            row,
            row,
        ),
        grid_spec=pltpu.PrefetchScalarGridSpec(
            num_scalar_prefetch=1,
            grid=(parts,),
            in_specs=[whole((chunks, d, step))] + table_specs(size) + [whole((chunks, 1, step))],
            out_specs=(
                pl.BlockSpec((chunks, VB, step), lambda v, s: (0, v, 0)),
                pl.BlockSpec((1, chunks, 1, step), lambda v, s: (v, 0, 0, 0)),
                whole((chunks, 1, step)),
                whole((chunks, 1, step)),
                whole((chunks, 1, step)),
            ),
            scratch_shapes=[pltpu.VMEM((d, VB), BF), pltpu.VMEM((VB, d), BF)],
        ),
        compiler_params=params(48),
    )(scalars, hidden, own, one, two, wanted)


def vocab_hidden_grad(scalars, exps, tops, logsum, table, wanted):
    chunks, width, step = exps.shape
    own, one, two = table
    size = own.shape[0]
    d = 4 * size
    parts = width // VB

    def body(s_ref, e_ref, m_ref, l_ref, own_ref, one_ref, two_ref, t_ref, g_ref, o_ref, blk, acc):
        vb = pl.program_id(0)

        @pl.when(vb == 0)
        def _():
            acc[...] = jnp.zeros_like(acc)

        assemble(s_ref, own_ref, one_ref, two_ref, blk)
        ids = lax.broadcasted_iota(jnp.int32, (VB, step), 0) + vb * VB

        def one_chunk(n, carry):
            scale = jnp.exp(m_ref[0, n] - l_ref[n])
            probs = e_ref[n].astype(F32) * scale
            grads = jnp.where(ids == t_ref[n], probs - 1.0, probs).astype(BF)
            g_ref[n] = grads
            acc[n] += nn(blk[...], grads)
            return carry

        lax.fori_loop(0, chunks, one_chunk, 0)

        @pl.when(vb == parts - 1)
        def _():
            o_ref[...] = acc[...].astype(BF)

    return pl.pallas_call(
        body,
        out_shape=(
            jax.ShapeDtypeStruct((chunks, width, step), BF),
            jax.ShapeDtypeStruct((chunks, d, step), BF),
        ),
        grid_spec=pltpu.PrefetchScalarGridSpec(
            num_scalar_prefetch=1,
            grid=(parts,),
            in_specs=[
                pl.BlockSpec((chunks, VB, step), lambda v, s: (0, v, 0)),
                pl.BlockSpec((1, chunks, 1, step), lambda v, s: (v, 0, 0, 0)),
                whole((chunks, 1, step)),
            ]
            + table_specs(size)
            + [whole((chunks, 1, step))],
            out_specs=(
                pl.BlockSpec((chunks, VB, step), lambda v, s: (0, v, 0)),
                whole((chunks, d, step)),
            ),
            scratch_shapes=[pltpu.VMEM((d, VB), BF), pltpu.VMEM((chunks, d, step), F32)],
        ),
        input_output_aliases={1: 0},
        compiler_params=params(56),
    )(scalars, exps, tops, logsum, own, one, two, wanted)


def vocab_table_grad(places, hidden, grads):
    chunks, width, step = grads.shape
    d = hidden.shape[1]
    unit = d // 8
    parts = width // VB

    def body(s_ref, h_ref, g_ref, o_ref):
        acc = nt(h_ref[0], g_ref[0])
        for n in range(1, chunks):
            acc += nt(h_ref[n], g_ref[n])
        for u in range(8):
            spot = pl.ds(pl.multiple_of(s_ref[u] * unit, unit), unit)
            o_ref[spot, :] = acc[u * unit : (u + 1) * unit].astype(BF)

    return pl.pallas_call(
        body,
        out_shape=jax.ShapeDtypeStruct((d, width), BF),
        grid_spec=pltpu.PrefetchScalarGridSpec(
            num_scalar_prefetch=1,
            grid=(parts,),
            in_specs=[
                whole((chunks, d, step)),
                pl.BlockSpec((chunks, VB, step), lambda v, s: (0, v, 0)),
            ],
            out_specs=pl.BlockSpec((d, VB), lambda v, s: (0, v)),
        ),
        compiler_params=params(48),
    )(places, hidden, grads)


def norm_forward(states, gain):
    scale = lax.rsqrt(jnp.mean(states * states, axis=0, keepdims=True) + EPS)
    return ((states * scale * gain).astype(BF), scale)


def norm_backward(states, gain, scale, incoming):
    weighted = incoming * gain
    inner = jnp.mean(weighted * states, axis=0, keepdims=True)
    through = scale * weighted - states * (scale * scale * scale * inner)
    return (through, jnp.sum(incoming * states * scale, axis=1))


class Moves:
    def __init__(self, dp):
        self.dp = dp

    def core(self, x):
        return lax.ppermute(x, "dp", [(i, i ^ 1) for i in range(self.dp)])

    def col(self, x, bit):
        return lax.ppermute(x, "col", [(i, i ^ bit) for i in range(4)])

    def rows(self, x, pairs):
        perm = []
        for i in range(self.dp):
            for r in range(4):
                flip, bit = pairs[i % 2]
                perm.append((i * 4 + r, (i ^ flip) * 4 + (r ^ bit)))
        return lax.ppermute(x, ("dp", "row"), perm)

    def spread(self, x, turn, back=False):
        perm = []
        for i in range(self.dp):
            for c in range(4):
                dest = (i - i % 2 + c // 2) * 4 + 2 * (i % 2) + (c % 2 ^ turn)
                perm.append((dest, i * 4 + c) if back else (i * 4 + c, dest))
        return lax.ppermute(x, ("dp", "col"), perm)


STEP_ONE = {0: (0, 1), 1: (0, 2)}
STEP_TWO = {0: (1, 2), 1: (1, 1)}
STEP_TWO_BACK = {0: (1, 1), 1: (1, 2)}
SAME_TWO = {0: (0, 2), 1: (0, 1)}


def local(
    inputs,
    encoder,
    prefix,
    targets,
    gain_self,
    w_query,
    w_key,
    w_value,
    w_attn_out,
    gain_cross,
    w_cross_query,
    w_cross_key,
    w_cross_value,
    w_cross_out,
    gain_ff,
    w_gate,
    w_up,
    w_ff_out,
    gain_final,
    embed_table,
    *,
    dp,
):
    move = Moves(dp)
    dpi = lax.axis_index("dp")
    core = dpi % 2
    row = lax.axis_index("row")
    col = lax.axis_index("col")
    first_core = core == 0
    side = col // 2
    half = col % 2
    block = inputs.shape[0]
    d = 4 * block
    seq = inputs.shape[1]
    tq = seq // 2
    tc = tq // 2
    heads = w_query.shape[1] // HEAD
    ff_half = w_gate.shape[1] // 2
    vocab = embed_table.shape[1]
    width = -(-vocab // (2 * VB)) * VB
    mine = side == core

    def pick(flag, a, b):
        return jnp.where(flag, a, b)

    def bring(x):
        got = jnp.stack([move.spread(x, 0), move.spread(x, 1)])
        other = move.core(got)
        near, far = pick(mine, got, other), pick(mine, other, got)
        return jnp.concatenate([near[0], far[0], near[1], far[1]], axis=0)

    def hand_back(parts):
        hi = [pick(mine, parts[0], parts[1]), pick(mine, parts[2], parts[3])]
        got = [move.spread(hi[0], 0, True), move.spread(hi[1], 1, True)]
        return pick(
            half == 0,
            jnp.concatenate([got[0], got[1]], axis=1),
            jnp.concatenate([got[1], got[0]], axis=1),
        )

    def fold_back(partial_sum):
        blocks4 = partial_sum.reshape(4, block, -1)
        near = jnp.stack([blocks4[0], blocks4[2]])
        far = jnp.stack([blocks4[1], blocks4[3]])
        keep, send = pick(mine, near, far), pick(mine, far, near)
        total = (keep.astype(F32) + move.core(send).astype(F32)).astype(BF)
        whole_sum = (total[0].astype(F32) + move.col(total[1], 1).astype(F32)).astype(BF)
        perm = []
        for i in range(dp):
            for c in range(4):
                perm.append((i * 4 + c, (i - i % 2 + c // 2) * 4 + 2 * (i % 2) + c % 2))
        return lax.ppermute(whole_sum, ("dp", "col"), perm)

    def gather_pair(zero, one):
        own = pick(first_core, zero, one)
        got = jnp.stack([own, move.col(own, 2)])
        got = jnp.concatenate([got, move.col(got, 1)]).reshape(d, own.shape[1])
        both = jnp.stack([got, move.rows(got, STEP_ONE)])
        other = move.rows(both, STEP_TWO)
        return pick(first_core, both, other), pick(first_core, other, both)

    def scatter_pair(zero, one):
        send, keep = pick(first_core, one, zero), pick(first_core, zero, one)
        got = move.rows(send, STEP_TWO_BACK)
        both = (keep.astype(F32) + got.astype(F32)).astype(BF)
        got = move.rows(both[1], STEP_ONE)
        one_block = (both[0].astype(F32) + got.astype(F32)).astype(BF)
        cut = one_block.reshape(2, 2, block, one_block.shape[1])
        cut = (cut[0].astype(F32) + move.col(cut[1], 1).astype(F32)).astype(BF)
        return cut[0].astype(F32) + move.col(cut[1], 2).astype(F32)

    padded = jnp.pad(embed_table, ((0, 0), (0, 2 * width - vocab)))
    table_own = pick(first_core, padded[:, :width], padded[:, width:])

    pack_self = jnp.concatenate([w_query, w_key, w_value, w_attn_out.T], axis=1)
    pack_cross = jnp.concatenate([w_cross_query, w_cross_key, w_cross_value, w_cross_out.T], axis=1)
    pack_ff = [
        jnp.concatenate([w[:, s : s + ff_half] for w in (w_gate, w_up, w_ff_out)], axis=1)
        for s in (0, ff_half)
    ]
    gains_own = jnp.stack([gain_self, gain_cross, gain_ff, gain_final])
    gains = jnp.stack([gains_own, move.col(gains_own, 2)])
    gains = jnp.concatenate([gains, move.col(gains, 1)])
    gains = gains.transpose(1, 0, 2).reshape(4, d, 1)
    g_self, g_cross, g_ff, g_final = (gains[n] for n in range(4))

    perm = []
    for i in range(dp):
        for r in range(4):
            for c in range(4):
                dest = ((i - i % 2 + r // 2) * 4 + c) * 4 + 2 * (i % 2) + r % 2
                perm.append(((i * 4 + r) * 4 + c, dest))
    length = lax.ppermute(prefix, ("dp", "row", "col"), perm)
    scalars = jnp.concatenate([half[None], length]).astype(jnp.int32)
    info = {"tq": tq, "heads": heads, "scalars": scalars}

    states_low = bring(inputs)
    ws, wc = gather_pair(pack_self, pack_cross)
    enc_all = bring(encoder)
    wf = gather_pair(*pack_ff)
    table_one = move.rows(table_own, STEP_ONE)
    table_two = move.rows(jnp.stack([table_own, table_one]), SAME_TWO)
    table = (table_own, table_one, table_two)

    hw = heads * HEAD
    states_all = states_low.astype(F32)
    normed_all, scale_all = norm_forward(states_all, g_self)

    def own_lanes(x, axis=1):
        return lax.dynamic_slice_in_dim(x, half * tq, tq, axis)

    states = own_lanes(states_low).astype(F32)
    qkv = project(ws, normed_all, 0, 3 * hw)
    self_args = ((qkv, 0, True), (qkv, heads), (qkv, 2 * heads))
    attended, totals_self = attend_forward(info, *self_args, True)
    branch = combine(ws, attended, 3 * hw, 4 * hw)
    first = states + (branch + move.core(branch))

    normed_cross, scale_cross = norm_forward(first, g_cross)
    cq = project(wc, normed_cross, 0, hw)
    ckv = project(wc, enc_all, hw, 3 * hw)
    cross_args = ((cq, 0, False), (ckv, 0), (ckv, heads))
    crossed, totals_cross = attend_forward(info, *cross_args, False)
    branch = combine(wc, crossed, 3 * hw, 4 * hw)
    second = first + (branch + move.core(branch))

    normed_ff, scale_ff = norm_forward(second, g_ff)
    *saved, branch = ff_forward(wf, normed_ff)
    third = second + (branch + move.core(branch))
    out_low = third.astype(BF)
    output = hand_back(out_low.reshape(4, block, tq))

    normed_final, scale_final = norm_forward(third, g_final)

    def swap_bits(n):
        return n // 2 + 2 * (n % 2)

    def reorder(x, index):
        parts = x.reshape(4, block, x.shape[-1])
        return jnp.concatenate(
            [lax.dynamic_index_in_dim(parts, i, 0, keepdims=False) for i in index], axis=0
        )

    piece = lax.dynamic_slice_in_dim(normed_final, core * tc, tc, 1)
    piece = reorder(piece, [swap_bits(col ^ row ^ s) for s in range(4)])
    got = jnp.stack([piece, move.col(piece, 2)])
    got = jnp.concatenate([got, move.col(got, 1)])
    hidden = jnp.concatenate([got, move.core(got)])

    other_targets = move.core(targets)
    near, far = pick(mine, targets, other_targets), pick(mine, other_targets, targets)

    def target_chunks(which_core):
        out = []
        for seq_targets, lo in ((near, half), (far, half), (near, 1 - half), (far, 1 - half)):
            out.append(lax.dynamic_slice_in_dim(seq_targets, lo * tq + which_core * tc, tc, 0))
        return out

    wanted = jnp.stack(target_chunks(core) + target_chunks(1 - core))
    wanted = wanted - col * vocab
    wanted = jnp.where((wanted >= 0) & (wanted < vocab), wanted - core * width, -1)[:, None, :]
    valid = jnp.where(first_core, width, vocab - width)
    vocab_scalars = jnp.stack([valid, core]).astype(jnp.int32)
    exps, tops, top, total, picked = vocab_forward(vocab_scalars, hidden, table, wanted)

    def merge(items):
        peak = items[0][0]
        for item in items[1:]:
            peak = jnp.maximum(peak, item[0])
        amount = sum(item[1] * jnp.exp(item[0] - peak) for item in items)
        return jnp.stack([peak, amount, sum(item[2] for item in items)])

    stats = jnp.stack([top[:, 0], total[:, 0], picked[:, 0]])
    stats = merge([stats, jnp.roll(move.core(stats), 4, axis=1)])
    cube = stats.reshape(3, 2, 2, 2, tc)
    items = [cube]
    for bit in (1, 2, 3):
        come = move.col(cube, bit)
        if bit & 1:
            come = come[:, :, ::-1]
        if bit & 2:
            come = come[:, :, :, ::-1]
        items.append(come)
    stats = merge(items).reshape(3, 8, tc)
    logsum = stats[0] + jnp.log(stats[1])
    losses = logsum - stats[2]

    by_core = losses.reshape(2, 2, 2, tc)
    by_core = pick(first_core, by_core, by_core[::-1])
    by_seq = pick(mine, by_core[:, :, 0], by_core[:, :, 1])
    by_half = pick(half == 0, by_seq, by_seq[:, ::-1])
    loss = by_half.transpose(1, 0, 2).reshape(seq)

    grads, grad_hidden = vocab_hidden_grad(
        vocab_scalars, exps, tops, logsum[:, None], table, wanted
    )
    part = (grad_hidden[:4].astype(F32) + move.core(grad_hidden[4:]).astype(F32)).astype(BF)
    part = (part[:2].astype(F32) + move.col(part[2:], 1).astype(F32)).astype(BF)
    part = (part[0].astype(F32) + move.col(part[1], 2).astype(F32)).astype(BF)
    part = reorder(part, [col ^ row ^ swap_bits(n) for n in range(4)])
    other = move.core(part)
    grad_normed = jnp.concatenate(
        [pick(first_core, part, other), pick(first_core, other, part)], axis=1
    ).astype(F32)

    row_hi, row_lo = row // 2, row % 2
    places = []
    for unit in range(8):
        s_hi, s_lo, sub = unit // 4, unit // 2 % 2, unit % 2
        to_hi = row_lo ^ s_lo ^ row_hi
        to_lo = sub ^ row_lo
        upper = row_hi ^ s_hi
        places.append(
            jnp.where(first_core, to_lo * 4 + to_hi * 2, to_hi * 4 + to_lo * 2) + upper
        )
    places = jnp.stack(places).astype(jnp.int32)
    grad_table = vocab_table_grad(places, hidden, grads)

    through, gg_final = norm_backward(third, g_final, scale_final, grad_normed)
    grad_third = through
    *ff_weight_grads, partial_normed = ff_backward(wf, saved, normed_ff, grad_third.astype(BF))
    grad_normed = partial_normed + move.core(partial_normed)
    through, gg_ff = norm_backward(second, g_ff, scale_ff, grad_normed)
    grad_second = grad_third + through

    low = grad_second.astype(BF)
    grad_crossed = project(wc, low, 3 * hw, 4 * hw)
    dcq, dck, dcv = attend_backward(info, *cross_args, grad_crossed, totals_cross, False)
    partial_normed = combine(wc, dcq, 0, hw)
    grad_normed = partial_normed + move.core(partial_normed)
    through, gg_cross = norm_backward(first, g_cross, scale_cross, grad_normed)
    grad_first = grad_second + through
    grad_enc = source_grads(wc, None, 0, (dck, dcv), (hw, 2 * hw), scalars, hw, BF)
    cross_weight_grads = weight_grads(
        [(normed_cross, dcq), (enc_all, dck), (enc_all, dcv), (low, crossed)], 4 * hw
    )

    low = grad_first.astype(BF)
    grad_attended = project(ws, low, 3 * hw, 4 * hw)
    dq, dk, dv = attend_backward(info, *self_args, grad_attended, totals_self, True)
    partial_normed = source_grads(ws, dq, 0, (dk, dv), (hw, 2 * hw), scalars, hw, F32)
    through, gg_self = norm_backward(states_all, g_self, scale_all, partial_normed)
    zero = jnp.zeros_like(grad_first)
    spot = pick(
        half == 0,
        jnp.concatenate([grad_first, zero], axis=1),
        jnp.concatenate([zero, grad_first], axis=1),
    )
    grad_states = (through + pick(first_core, spot, 0.0)).astype(BF)
    self_weight_grads = weight_grads(
        [(own_lanes(normed_all), dq), (normed_all, dk), (normed_all, dv), (low, attended)], 4 * hw
    )

    grad_encoder = fold_back(grad_enc).astype(F32)
    grad_inputs = fold_back(grad_states).astype(F32)

    table_sum = None
    if dp == 2:
        cut = grad_table.reshape(2, d // 2, width)
        cut = (cut[0].astype(F32) + move.rows(cut[1], STEP_ONE).astype(F32)).astype(BF)
        cut = cut.reshape(2, d // 4, width)
        cut = cut[0].astype(F32) + move.rows(cut[1], SAME_TWO).astype(F32)
        cut = cut.reshape(2, d // 8, width)
        keep, send = pick(first_core, cut[0], cut[1]), pick(first_core, cut[1], cut[0])
        got = move.core(send.astype(BF)).astype(F32)
        table_sum = jnp.concatenate(
            [pick(first_core, keep, got), pick(first_core, got, keep)[:, : vocab - width]], axis=1
        )
    else:
        units = grad_table.reshape(8, d // 8, width)
        ordered = []
        for e in range(8):
            rel = (e // 2) ^ row
            at = places[rel * 2 + e % 2]
            ordered.append(lax.dynamic_index_in_dim(units, at, 0, keepdims=False))
        full = jnp.concatenate(ordered, axis=0)
        blank = jnp.zeros_like(full)
        full = pick(
            first_core,
            jnp.concatenate([full, blank], axis=1),
            jnp.concatenate([blank, full], axis=1),
        )[:, :vocab]
        table_sum = lax.psum_scatter(
            full, ("dp", "row"), scatter_dimension=0, tiled=True
        ).astype(F32)

    sum_attn = scatter_pair(self_weight_grads, cross_weight_grads)
    sum_ff = scatter_pair(*ff_weight_grads)

    def split_cores(x, flip_out):
        if flip_out:
            x = jnp.concatenate([x[:, : 3 * hw], x[:, 3 * hw :].T], axis=1)
        rows_half = block // 2
        top_half, low_half = x[:rows_half], x[rows_half:]
        if dp == 2:
            keep = pick(first_core, top_half, low_half)
            got = move.core(pick(first_core, low_half, top_half))
            return pick(first_core, keep, got), pick(first_core, got, keep)
        zero_pack = pick(first_core, x, 0.0).astype(BF)
        one_pack = pick(first_core, 0.0, x).astype(BF)
        both = lax.psum_scatter(
            jnp.concatenate([zero_pack, one_pack], axis=1), "dp", scatter_dimension=0, tiled=True
        ).astype(F32)
        return both[:, : x.shape[1]], both[:, x.shape[1] :]

    out_self, out_cross = split_cores(sum_attn, True)
    out_ff0, out_ff1 = split_cores(sum_ff, False)

    def ff_part(n):
        sl = slice(n * ff_half, (n + 1) * ff_half)
        return jnp.concatenate([out_ff0[:, sl], out_ff1[:, sl]], axis=1)

    once = jnp.where(first_core, 1.0, 0.0)
    packed = jnp.stack([gg_self, gg_cross * once, gg_ff * once, gg_final * once])
    packed = packed.reshape(4, 4, block)
    packed = jnp.stack(
        [
            lax.dynamic_index_in_dim(packed, swap_bits(col ^ f), 1, keepdims=False)
            for f in range(4)
        ],
        axis=1,
    )
    packed = lax.psum(packed, ("dp", "row", "col"))
    packed = lax.dynamic_index_in_dim(packed, col, 1, keepdims=False)

    return (
        output,
        loss,
        grad_inputs,
        grad_encoder,
        packed[0],
        out_self[:, :hw],
        out_self[:, hw : 2 * hw],
        out_self[:, 2 * hw : 3 * hw],
        out_self[:, 3 * hw :],
        packed[1],
        out_cross[:, :hw],
        out_cross[:, hw : 2 * hw],
        out_cross[:, 2 * hw : 3 * hw],
        out_cross[:, 3 * hw :],
        packed[2],
        ff_part(0),
        ff_part(1),
        ff_part(2),
        packed[3],
        table_sum,
    )


def solution(mesh):
    return jax.shard_map(
        partial(local, dp=mesh.shape["dp"]),
        mesh=mesh,
        in_specs=(
            P("col", ("dp", "row")),
            P("col", ("dp", "row")),
            P(("dp", "col")),
            P(("dp", "row")),
            P("col"),
            P("col", "row"),
            P("col", "row"),
            P("col", "row"),
            P("row", "col"),
            P("col"),
            P("col", "row"),
            P("col", "row"),
            P("col", "row"),
            P("row", "col"),
            P("col"),
            P("col", "row"),
            P("col", "row"),
            P("col", "row"),
            P("col"),
            P("row", "col"),
        ),
        out_specs=(
            P("col", ("dp", "row")),
            P(("dp", "row")),
            P("col", ("dp", "row")),
            P("col", ("dp", "row")),
            P("col"),
            P(("col", "dp"), "row"),
            P(("col", "dp"), "row"),
            P(("col", "dp"), "row"),
            P(("row", "dp"), "col"),
            P("col"),
            P(("col", "dp"), "row"),
            P(("col", "dp"), "row"),
            P(("col", "dp"), "row"),
            P(("row", "dp"), "col"),
            P("col"),
            P(("col", "dp"), "row"),
            P(("col", "dp"), "row"),
            P(("col", "dp"), "row"),
            P("col"),
            P(("dp", "row"), "col"),
        ),
        check_vma=False,
    )
```

time: 3010 us -> 675 us (0.22)
  waiting for transfers between devices: 2370 us -> 185 us
  matrix products: 328 us -> 0 us
  Pallas kernels: 0 us -> 199 us
  starting transfers between devices: 2.8 us -> 77.1 us
  blocking collectives: 120 us -> 50.1 us
    reduce_scatter x27 -> x0, waiting for transfers between devices: 1530 us -> none  [the longest x7 976 us: cols_sum(): return lax.psum_scatter(values, 'col', scatter_dimension=0, tiled=True)]
    all_gather x16 -> x0, waiting for transfers between devices: 833 us -> none  [the longest x7 480 us: cols_gather(): return lax.all_gather(values, 'col', axis=0, tiled=True)]
    dot_general x57 -> x0, matrix products: 328 us -> none  [the longest x11 109 us: matmul_plain(): lax.dot_general(left, right, (((1,), (0,)), ((), ())), preferred_element_...]
    pallas_call x0 -> x21, Pallas kernels: none -> 199 us  [the longest x1 38.7 us: vocab_forward(): pl.pallas_call(body, out_shape=(jax.ShapeDtypeStruct((chunks, width, step...]
    ppermute x0 -> x57, waiting for transfers between devices: none -> 185 us  [the longest x19 162 us: col(): return lax.ppermute(x, 'col', [(i, i ^ bit) for i in range(4)])]
    ppermute x0 -> x57, starting transfers between devices: none -> 77.1 us  [the longest x19 26.6 us: col(): return lax.ppermute(x, 'col', [(i, i ^ bit) for i in range(4)])]
    psum x10 -> x1, blocking collectives: 120 us -> 50.1 us  [local(): packed = lax.psum(packed, ('dp', 'row', 'col'))]
  transfers between devices with their start and end apart: 43 -> 57, of which waited for: 39 -> 19; matrix products, arithmetic and copies ran while one was open for 5% -> 19% of each run, Pallas kernels for 0% -> 18%
where the time goes in v1:
time: 675 us; the launch traced here: 667 us
  Pallas kernels  199 us (29%)
  waiting for transfers between devices  185 us (27%)
  other arithmetic  110 us (16%)
  starting transfers between devices  77.1 us (11%)
  blocking collectives  50.1 us (7%)
  local copies, waits for them, and re-layouts  42.9 us (6%)
    ppermute x19, waiting for transfers between devices, col(): return lax.ppermute(x, 'col', [(i, i ^ bit) for i in range(4)])  162 us
    psum x1, blocking collectives, local(): packed = lax.psum(packed, ('dp', 'row', 'col'))  50.1 us
    pallas_call x1, Pallas kernels, vocab_forward(): pl.pallas_call(body, out_shape=(jax.ShapeDtypeStruct((chunks, width, step...  38.7 us
    pallas_call x1, Pallas kernels, vocab_hidden_grad(): pl.pallas_call(body, out_shape=(jax.ShapeDtypeStruct((chunks, width, step...  35.3 us
    pallas_call x2, Pallas kernels, attend_backward(): pl.pallas_call(body, out_shape=(jax.ShapeDtypeStruct((blocks, heads * HEA...  33.7 us
    select_n x25, other arithmetic, pick(): return jnp.where(flag, a, b)  27.1 us
    ppermute x19, starting transfers between devices, col(): return lax.ppermute(x, 'col', [(i, i ^ bit) for i in range(4)])  26.6 us
    ppermute x12, starting transfers between devices, rows(): return lax.ppermute(x, ('dp', 'row'), perm)  21.6 us
  transfers between devices with their start and end apart: 57, of which 19 were waited for; matrix products, arithmetic and copies ran while one was open for 19% of the time, Pallas kernels for 18%

profile of v1, /device:TPU:0, one launch (start us, length us, event | category | flops | bytes accessed | tf_op | source)
XLA Modules:
  0.0 666.7 jit_solution(1324006317021478993)
XLA Ops:
  4.2 4.1 collective-permute-start.3
  8.6 13.0 %collective-permute-done.3 = bf16[192,768]{1,0:T(8,128)(2,1)S(1)} collective-permute-done((bf16[192,768]{1,0:T(8,128)(2,1)S(1)}, bf16[192,768]{1,0:T(8,128)(2,1)S(1)}, u32[]{:S(2)}, u32[]{:S(2)}) %collective-permute-start.3) | collective-permute-done | bytes 294944 | tf_op jit(solution)/shard_map/ppermute | solution.py:531
  22.6 13.8 %collective-permute-done.4 = bf16[2,192,768]{2,1,0:T(8,128)(2,1)S(1)} collective-permute-done((bf16[2,192,768]{2,1,0:T(8,128)(2,1)S(1)}, bf16[2,192,768]{2,1,0:T(8,128)(2,1)S(1)}, u32[]{:S(2)}, u32[]{:S(2)}) %collective-permute-start.4) | collective-permute-done | bytes 589856 | tf_op jit(solution)/shard_map/ppermute | solution.py:531
  39.5 4.5 collective-permute-start
  48.0 10.8 %collective-permute-done.8 = f32[4,192]{1,0:T(4,128)S(1)} collective-permute-done((f32[4,192]{1,0:T(4,128)S(1)}, f32[4,192]{1,0:T(4,128)S(1)}, u32[]{:S(2)}, u32[]{:S(2)}) %collective-permute-start.8) | collective-permute-done | bytes 3104 | tf_op jit(solution)/shard_map/ppermute | solution.py:531
  58.8 7.4 %collective-permute-start.11 = (bf16[192,2048]{1,0:T(8,128)(2,1)}, bf16[192,2048]{1,0:T(8,128)(2,1)}, u32[]{:S(2)}, u32[]{:S(2)}) collective-permute-start(bf16[192,2048]{1,0:T(8,128)(2,1)} %param.21), channel_id=1, source_target_pairs={{0,0},{1,1},{2,16},{3,17},{16,2},{17,3},{18,18},{19,19},{4,4},{5,5... | collective-permute-start | bytes 2359304 | tf_op jit(solution)/shard_map/ppermute | solution.py:547
  67.9 4.3 collective-permute-start.6
  78.7 27.5 %collective-permute-done.15 = bf16[192,768]{1,0:T(8,128)(2,1)S(1)} collective-permute-done((bf16[192,768]{1,0:T(8,128)(2,1)}, bf16[192,768]{1,0:T(8,128)(2,1)S(1)}, u32[]{:S(2)}, u32[]{:S(2)}) %collective-permute-start.15) | collective-permute-done | bytes 294944 | tf_op jit(solution)/shard_map/ppermute | solution.py:531
  111.7 11.5 %collective-permute-done.16 = bf16[2,192,768]{2,1,0:T(8,128)(2,1)} collective-permute-done((bf16[2,192,768]{2,1,0:T(8,128)(2,1)}, bf16[2,192,768]{2,1,0:T(8,128)(2,1)}, u32[]{:S(2)}, u32[]{:S(2)}) %collective-permute-start.16) | collective-permute-done | bytes 589856 | tf_op jit(solution)/shard_map/ppermute | solution.py:531
  132.8 8.0 %shard_map.348 = (bf16[2,192,512]{2,1,0:T(8,128)(2,1)S(1)}, f32[6,1,512]{2,1,0:T(1,128)S(1)}) custom-call(s32[2]{0:T(128)S(1)} %pad_add_fusion.s_ref.refs_0_, bf16[2,576,1024]{2,1,0:T(8,128)(2,1)S(1)} %shard_map.347.q_ref.k_ref.v_ref, bf16[2,576,1024]{2,1,0:T(8,128)(2,1)S(1)} %shard_map.347.q_ref.k_ref.v_ref, ...), custom_call_target="tpu_custom_call" | custom-call | tf_op jit(solution)/shard_map/pallas_call | solution.py:69
  157.8 13.5 %shard_map.352 = (bf16[2,192,512]{2,1,0:T(8,128)(2,1)S(1)}, f32[6,1,512]{2,1,0:T(1,128)S(1)}) custom-call(s32[2]{0:T(128)S(1)} %pad_add_fusion.s_ref.refs_0_, bf16[2,192,512]{2,1,0:T(8,128)(2,1)S(1)} %shard_map.350.q_ref, bf16[2,384,2048]{2,1,0:T(8,128)(2,1)S(1)} %shard_map.351.k_ref.v_ref, bf16[2,384,2048]{2,1,0:T(8,128)(2,1)S(1)} %shard_map.351.k_ref.v_ref), custom_call_target="tpu_custom_call" | custom-call | tf_op jit(solution)/shard_map/pallas_call | solution.py:69
  174.8 5.0 broadcast_select_fusion.2
  183.3 6.8 %shard_map.354 = (f32[2,512,512]{2,1,0:T(8,128)S(1)}, f32[2,512,512]{2,1,0:T(8,128)}, f32[768,512]{1,0:T(8,128)}) custom-call(bf16[2,768,768]{2,1,0:T(8,128)(2,1)} %get-tuple-element.99.refs_0_, bf16[2,768,768]{2,1,0:T(8,128)(2,1)} %get-tuple-element.98.refs_1_, bf16[768,512]{1,0:T(8,128)(2,1)S(1)} %multiply_convert_fusion.refs_2_.refs_4_), custom_call_target="tpu_custom_call" | custom-call | tf_op jit(solution)/shard_map/pallas_call | solution.py:175
  202.8 10.3 %collective-permute-done.25.one_ref = bf16[192,4096]{1,0:T(8,128)(2,1)} collective-permute-done((bf16[192,4096]{1,0:T(8,128)(2,1)}, bf16[192,4096]{1,0:T(8,128)(2,1)}, u32[]{:S(2)}, u32[]{:S(2)}) %collective-permute-start.25) | collective-permute-done | bytes 1572896 | tf_op jit(solution)/shard_map/ppermute | solution.py:539
  221.3 19.1 %collective-permute-done.23 = bf16[2,768,256]{2,1,0:T(8,128)(2,1)S(1)} collective-permute-done((bf16[2,768,256]{2,1,0:T(8,128)(2,1)S(1)}, bf16[2,768,256]{2,1,0:T(8,128)(2,1)S(1)}, u32[]{:S(2)}, u32[]{:S(2)}) %collective-permute-start.23) | collective-permute-done | bytes 786464 | tf_op jit(solution)/shard_map/ppermute | solution.py:531
  249.7 4.3 collective-permute-done.26.two_ref
  254.1 38.7 %shard_map.355 = (bf16[8,4096,256]{2,1,0:T(8,128)(2,1)}, f32[8,8,1,256]{3,2,1,0:T(1,128)S(1)}, f32[8,1,256]{2,1,0:T(1,128)S(1)}, f32[8,1,256]{2,1,0:T(1,128)S(1)}, f32[8,1,256]{2,1,0:T(1,128)S(1)}) custom-call(s32[2]{0:T(128)S(1)} %copy-done.20, bf16[8,768,256]{2,1,0:T(8,128)(2,1)} %pad_maximum_fusion.1.h_ref, bf16[192,4096]{1,0:T(8,128)(2,1)} %fusion.17.own_ref, ...), custom_call_target="tpu_custom_call" | custom-call | tf_op jit(solution)/shard_map/pallas_call | solution.py:397
  302.2 35.3 %shard_map.356 = (bf16[8,4096,256]{2,1,0:T(8,128)(2,1)}, bf16[8,768,256]{2,1,0:T(8,128)(2,1)}) custom-call(s32[2]{0:T(128)} %pad_add_fusion.1.s_ref, bf16[8,4096,256]{2,1,0:T(8,128)(2,1)} %get-tuple-element.49.e_ref, f32[8,8,1,256]{3,2,1,0:T(1,128)} %copy-done.17, f32[8,1,256]{2,1,0:T(1,128)} %bitcast.247, ...), custom_call_target="tpu_custom_call", output_to_operand_aliasing={{0}: (1, {})} | custom-call | tf_op jit(solution)/shard_map/pallas_call | solution.py:454
  349.9 17.9 %shard_map.367 = bf16[768,4096]{1,0:T(8,128)(2,1)} custom-call(s32[8]{0:T(128)S(1)} %copy-done.21, bf16[8,768,256]{2,1,0:T(8,128)(2,1)S(1)} %copy-done.8, bf16[8,4096,256]{2,1,0:T(8,128)(2,1)} %get-tuple-element.65.g_ref), custom_call_target="tpu_custom_call" | custom-call | tf_op jit(solution)/shard_map/pallas_call | solution.py:495
  367.9 4.1 slice.594
  381.8 14.8 %collective-permute-done.34 = bf16[768,256]{1,0:T(8,128)(2,1)} collective-permute-done((bf16[768,256]{1,0:T(8,128)(2,1)}, bf16[768,256]{1,0:T(8,128)(2,1)}, u32[]{:S(2)}, u32[]{:S(2)}) %collective-permute-start.34) | collective-permute-done | bytes 393248 | tf_op jit(solution)/shard_map/ppermute | solution.py:531
  401.8 11.4 %shard_map.357 = (bf16[2,768,768]{2,1,0:T(8,128)(2,1)}, bf16[2,768,768]{2,1,0:T(8,128)(2,1)}, f32[768,512]{1,0:T(8,128)}) custom-call(bf16[2,768,768]{2,1,0:T(8,128)(2,1)} %get-tuple-element.99.refs_0_, bf16[2,768,768]{2,1,0:T(8,128)(2,1)} %get-tuple-element.98.refs_1_, f32[2,512,512]{2,1,0:T(8,128)} %copy-done.11, ...), custom_call_target="tpu_custom_call" | custom-call | tf_op jit(solution)/shard_map/pallas_call | solution.py:215
  419.2 4.1 add_convert_fusion
  436.1 21.0 %shard_map.359 = (bf16[2,192,512]{2,1,0:T(8,128)(2,1)S(1)}, bf16[2,192,2048]{2,1,0:T(8,128)(2,1)S(1)}, bf16[2,192,2048]{2,1,0:T(8,128)(2,1)S(1)}) custom-call(s32[2]{0:T(128)S(1)} %pad_add_fusion.s_ref.refs_0_, bf16[2,192,512]{2,1,0:T(8,128)(2,1)S(1)} %shard_map.350.q_ref, bf16[2,384,2048]{2,1,0:T(8,128)(2,1)} %copy-done.2, bf16[2,384,2048]{2,1,0:T(8,128)(2,1)} %copy-done.2, ...), custom_call_target="tpu_custom_call" | custom-call | tf_op jit(solution)/shard_map/pallas_call | solution.py:113
  460.1 4.6 shard_map.364
  467.5 8.5 %shard_map.366 = bf16[2,768,768]{2,1,0:T(8,128)(2,1)} custom-call(bf16[768,512]{1,0:T(8,128)(2,1)S(1)} %multiply_convert_fusion.1.x_ref.refs_0_, bf16[768,2048]{1,0:T(8,128)(2,1)} %copy-done.5, bf16[768,2048]{1,0:T(8,128)(2,1)} %copy-done.5, bf16[768,512]{1,0:T(8,128)(2,1)S(1)} %get-tuple-element.84.x_ref.refs_3_, ...), custom_call_target="tpu_custom_call" | custom-call | tf_op jit(solution)/shard_map/pallas_call | solution.py:285
  499.6 12.7 %shard_map.362 = (bf16[2,192,512]{2,1,0:T(8,128)(2,1)S(1)}, bf16[2,192,1024]{2,1,0:T(8,128)(2,1)S(1)}, bf16[2,192,1024]{2,1,0:T(8,128)(2,1)S(1)}) custom-call(s32[2]{0:T(128)S(1)} %pad_add_fusion.s_ref.refs_0_, bf16[2,576,1024]{2,1,0:T(8,128)(2,1)S(1)} %shard_map.347.q_ref.k_ref.v_ref, bf16[2,576,1024]{2,1,0:T(8,128)(2,1)S(1)} %shard_map.347.q_ref.k_ref.v_ref, ...), custom_call_target="tpu_custom_call" | custom-call | tf_op jit(solution)/shard_map/pallas_call | solution.py:113
  538.3 50.1 %psum.7 = f32[4,4,192]{2,1,0:T(4,128)S(1)} all-reduce(f32[4,4,192]{2,1,0:T(4,128)S(1)} %pad_maximum_fusion.27), channel_id=1, replica_groups=mesh['dp'=2,'row'=4,'col'=4] {'dp','row','col'}, use_global_device_ids=true, to_apply=%region_12.13 | all-reduce | flops 3072 | bytes 24576 | tf_op jit(solution)/shard_map/psum | solution.py:899
  600.2 9.7 %collective-permute-done.52 = bf16[192,768]{1,0:T(8,128)(2,1)S(1)} collective-permute-done((bf16[192,768]{1,0:T(8,128)(2,1)S(1)}, bf16[192,768]{1,0:T(8,128)(2,1)S(1)}, u32[]{:S(2)}, u32[]{:S(2)}) %collective-permute-start.52) | collective-permute-done | bytes 294944 | tf_op jit(solution)/shard_map/ppermute | solution.py:531
  616.9 4.5 collective-permute-start.40
  621.4 12.1 %collective-permute-done.46 = bf16[2,192,768]{2,1,0:T(8,128)(2,1)S(1)} collective-permute-done((bf16[2,192,768]{2,1,0:T(8,128)(2,1)S(1)}, bf16[2,192,768]{2,1,0:T(8,128)(2,1)S(1)}, u32[]{:S(2)}, u32[]{:S(2)}) %collective-permute-start.46) | collective-permute-done | bytes 589856 | tf_op jit(solution)/shard_map/ppermute | solution.py:531
  633.9 23.9 %collective-permute-done.47 = bf16[192,768]{1,0:T(8,128)(2,1)S(1)} collective-permute-done((bf16[192,768]{1,0:T(8,128)(2,1)S(1)}, bf16[192,768]{1,0:T(8,128)(2,1)S(1)}, u32[]{:S(2)}, u32[]{:S(2)}) %collective-permute-start.47) | collective-permute-done | bytes 294944 | tf_op jit(solution)/shard_map/ppermute | solution.py:531
  (518 shorter events, 226.4 us)
Async XLA Ops:
  36.5 29.8 %collective-permute-start.5 = (bf16[768,768]{1,0:T(8,128)(2,1)S(1)}, bf16[768,768]{1,0:T(8,128)(2,1)S(1)}, u32[]{:S(2)}, u32[]{:S(2)}) collective-permute-start(bf16[768,768]{1,0:T(8,128)(2,1)S(1)} %bitcast.208), channel_id=1, source_target_pairs={{0,4},{4,0},{8,12},{12,8},{16,24},{20,28},{24,16},{28,20},{1,5},{5... | collective-permute-start | bytes 3538952 | tf_op jit(solution)/shard_map/ppermute | solution.py:539
  37.8 30.1 %collective-permute-start.1 = (bf16[192,1024]{1,0:T(8,128)(2,1)}, bf16[192,1024]{1,0:T(8,128)(2,1)}, u32[]{:S(2)}, u32[]{:S(2)}) collective-permute-start(bf16[192,1024]{1,0:T(8,128)(2,1)} %param.20), channel_id=1, source_target_pairs={{0,1},{1,0},{2,17},{3,16},{16,3},{17,2},{18,19},{19,18},{4,5},{5,4... | collective-permute-start | bytes 1179656 | tf_op jit(solution)/shard_map/ppermute | solution.py:547
  39.5 32.7 %collective-permute-start = (bf16[192,1024]{1,0:T(8,128)(2,1)}, bf16[192,1024]{1,0:T(8,128)(2,1)}, u32[]{:S(2)}, u32[]{:S(2)}) collective-permute-start(bf16[192,1024]{1,0:T(8,128)(2,1)} %param.20), channel_id=1, source_target_pairs={{0,0},{1,1},{2,16},{3,17},{16,2},{17,3},{18,18},{19,19},{4,4},{5,5... | collective-permute-start | bytes 1179656 | tf_op jit(solution)/shard_map/ppermute | solution.py:547
  47.0 62.3 %collective-permute-start.12 = (bf16[192,2048]{1,0:T(8,128)(2,1)}, bf16[192,2048]{1,0:T(8,128)(2,1)S(1)}, u32[]{:S(2)}, u32[]{:S(2)}) collective-permute-start(bf16[192,2048]{1,0:T(8,128)(2,1)} %param.21), channel_id=1, source_target_pairs={{0,1},{1,0},{2,17},{3,16},{16,3},{17,2},{18,19},{19,18},{4,5},{5,4... | collective-permute-start | bytes 2359304 | tf_op jit(solution)/shard_map/ppermute | solution.py:547
  58.8 50.5 %collective-permute-start.11 = (bf16[192,2048]{1,0:T(8,128)(2,1)}, bf16[192,2048]{1,0:T(8,128)(2,1)}, u32[]{:S(2)}, u32[]{:S(2)}) collective-permute-start(bf16[192,2048]{1,0:T(8,128)(2,1)} %param.21), channel_id=1, source_target_pairs={{0,0},{1,1},{2,16},{3,17},{16,2},{17,3},{18,18},{19,19},{4,4},{5,5... | collective-permute-start | bytes 2359304 | tf_op jit(solution)/shard_map/ppermute | solution.py:547
  66.3 40.0 %collective-permute-start.15 = (bf16[192,768]{1,0:T(8,128)(2,1)}, bf16[192,768]{1,0:T(8,128)(2,1)S(1)}, u32[]{:S(2)}, u32[]{:S(2)}) collective-permute-start(bf16[192,768]{1,0:T(8,128)(2,1)} %maximum_select_fusion.4), channel_id=1, source_target_pairs={{0,2},{1,3},{2,0},{3,1},{4,6},{5,7},{6,4},{7,5},{8,10},{9,11},{10,... | collective-permute-start | bytes 884744 | tf_op jit(solution)/shard_map/ppermute | solution.py:531
  67.9 60.0 %collective-permute-start.6 = (bf16[2,768,768]{2,1,0:T(8,128)(2,1)}, bf16[2,768,768]{2,1,0:T(8,128)(2,1)}, u32[]{:S(2)}, u32[]{:S(2)}) collective-permute-start(bf16[2,768,768]{2,1,0:T(8,128)(2,1)} %pad_maximum_fusion.4), channel_id=1, source_target_pairs={{0,24},{4,28},{8,16},{12,20},{16,4},{20,0},{24,12},{28,8},{1,25},{... | collective-permute-start | bytes 7077896 | tf_op jit(solution)/shard_map/ppermute | solution.py:539
  76.1 31.1 %collective-permute-start.9 = (f32[2,4,192]{2,1,0:T(4,128)S(1)}, f32[2,4,192]{2,1,0:T(4,128)S(1)}, u32[]{:S(2)}, u32[]{:S(2)}) collective-permute-start(f32[2,4,192]{2,1,0:T(4,128)S(1)} %pad_maximum_fusion.30), channel_id=1, source_target_pairs={{0,1},{1,0},{2,3},{3,2},{4,5},{5,4},{6,7},{7,6},{8,9},{9,8},{10,11... | collective-permute-start | bytes 18440 | tf_op jit(solution)/shard_map/ppermute | solution.py:531
  110.6 35.8 %collective-permute-start.13 = (bf16[2,192,2048]{2,1,0:T(8,128)(2,1)S(1)}, bf16[2,192,2048]{2,1,0:T(8,128)(2,1)S(1)}, u32[]{:S(2)}, u32[]{:S(2)}) collective-permute-start(bf16[2,192,2048]{2,1,0:T(8,128)(2,1)S(1)} %pad_maximum_fusion.7), channel_id=1, source_target_pairs={{0,16},{16,0},{1,17},{17,1},{2,18},{18,2},{3,19},{19,3},{4,20},{20... | collective-permute-start | bytes 4718600 | tf_op jit(solution)/shard_map/ppermute | solution.py:528
  143.7 31.1 %collective-permute-start.18 = (bf16[2,768,768]{2,1,0:T(8,128)(2,1)}, bf16[2,768,768]{2,1,0:T(8,128)(2,1)}, u32[]{:S(2)}, u32[]{:S(2)}) collective-permute-start(bf16[2,768,768]{2,1,0:T(8,128)(2,1)} %pad_maximum_fusion.5), channel_id=1, source_target_pairs={{0,24},{4,28},{8,16},{12,20},{16,4},{20,0},{24,12},{28,8},{1,25},{... | collective-permute-start | bytes 7077896 | tf_op jit(solution)/shard_map/ppermute | solution.py:539
  192.3 20.7 %collective-permute-start.25 = (bf16[192,4096]{1,0:T(8,128)(2,1)}, bf16[192,4096]{1,0:T(8,128)(2,1)}, u32[]{:S(2)}, u32[]{:S(2)}) collective-permute-start(bf16[192,4096]{1,0:T(8,128)(2,1)} %fusion.17.own_ref), channel_id=1, source_target_pairs={{0,4},{4,0},{8,12},{12,8},{16,24},{20,28},{24,16},{28,20},{1,5},{5... | collective-permute-start | bytes 4718600 | tf_op jit(solution)/shard_map/ppermute | solution.py:539
  201.1 20.1 %collective-permute-start.22 = (bf16[768,256]{1,0:T(8,128)(2,1)S(1)}, bf16[768,256]{1,0:T(8,128)(2,1)S(1)}, u32[]{:S(2)}, u32[]{:S(2)}) collective-permute-start(bf16[768,256]{1,0:T(8,128)(2,1)S(1)} %get-tuple-element.140), channel_id=1, source_target_pairs={{0,2},{1,3},{2,0},{3,1},{4,6},{5,7},{6,4},{7,5},{8,10},{9,11},{10,... | collective-permute-start | bytes 1179656 | tf_op jit(solution)/shard_map/ppermute | solution.py:531
  216.5 37.6 %collective-permute-start.26 = (bf16[2,192,4096]{2,1,0:T(8,128)(2,1)}, bf16[2,192,4096]{2,1,0:T(8,128)(2,1)}, u32[]{:S(2)}, u32[]{:S(2)}) collective-permute-start(bf16[2,192,4096]{2,1,0:T(8,128)(2,1)} %pad_maximum_fusion.2), channel_id=1, source_target_pairs={{0,8},{4,12},{8,0},{12,4},{16,20},{20,16},{24,28},{28,24},{1,9},{5... | collective-permute-start | bytes 9437192 | tf_op jit(solution)/shard_map/ppermute | solution.py:539
  221.2 19.2 %collective-permute-start.23 = (bf16[2,768,256]{2,1,0:T(8,128)(2,1)S(1)}, bf16[2,768,256]{2,1,0:T(8,128)(2,1)S(1)}, u32[]{:S(2)}, u32[]{:S(2)}) collective-permute-start(bf16[2,768,256]{2,1,0:T(8,128)(2,1)S(1)} %pad_maximum_fusion.14), channel_id=1, source_target_pairs={{0,1},{1,0},{2,3},{3,2},{4,5},{5,4},{6,7},{7,6},{8,9},{9,8},{10,11... | collective-permute-start | bytes 2359304 | tf_op jit(solution)/shard_map/ppermute | solution.py:531
  345.2 28.4 %collective-permute-start.33 = (bf16[2,768,256]{2,1,0:T(8,128)(2,1)}, bf16[2,768,256]{2,1,0:T(8,128)(2,1)}, u32[]{:S(2)}, u32[]{:S(2)}) collective-permute-start(bf16[2,768,256]{2,1,0:T(8,128)(2,1)} %slice.546), channel_id=1, source_target_pairs={{0,1},{1,0},{2,3},{3,2},{4,5},{5,4},{6,7},{7,6},{8,9},{9,8},{10,11... | collective-permute-start | bytes 2359304 | tf_op jit(solution)/shard_map/ppermute | solution.py:531
  371.9 47.3 %collective-permute-start.54 = (bf16[384,4096]{1,0:T(8,128)(2,1)}, bf16[384,4096]{1,0:T(8,128)(2,1)}, u32[]{:S(2)}, u32[]{:S(2)}) collective-permute-start(bf16[384,4096]{1,0:T(8,128)(2,1)} %slice.594), channel_id=1, source_target_pairs={{0,4},{4,0},{8,12},{12,8},{16,24},{20,28},{24,16},{28,20},{1,5},{5... | collective-permute-start | bytes 9437192 | tf_op jit(solution)/shard_map/ppermute | solution.py:539
  376.6 20.0 %collective-permute-start.34 = (bf16[768,256]{1,0:T(8,128)(2,1)}, bf16[768,256]{1,0:T(8,128)(2,1)}, u32[]{:S(2)}, u32[]{:S(2)}) collective-permute-start(bf16[768,256]{1,0:T(8,128)(2,1)} %slice_bitcast_fusion.20), channel_id=1, source_target_pairs={{0,2},{1,3},{2,0},{3,1},{4,6},{5,7},{6,4},{7,5},{8,10},{9,11},{10,... | collective-permute-start | bytes 1179656 | tf_op jit(solution)/shard_map/ppermute | solution.py:531
  418.7 65.1 %collective-permute-start.49 = (bf16[2,768,768]{2,1,0:T(8,128)(2,1)}, bf16[2,768,768]{2,1,0:T(8,128)(2,1)}, u32[]{:S(2)}, u32[]{:S(2)}) collective-permute-start(bf16[2,768,768]{2,1,0:T(8,128)(2,1)} %broadcast_select_fusion), channel_id=1, source_target_pairs={{0,20},{4,16},{8,28},{12,24},{16,8},{20,12},{24,0},{28,4},{1,21},{... | collective-permute-start | bytes 7077896 | tf_op jit(solution)/shard_map/ppermute | solution.py:539
  423.6 52.4 %collective-permute-start.55 = (bf16[192,4096]{1,0:T(8,128)(2,1)S(1)}, bf16[192,4096]{1,0:T(8,128)(2,1)}, u32[]{:S(2)}, u32[]{:S(2)}) collective-permute-start(bf16[192,4096]{1,0:T(8,128)(2,1)S(1)} %slice.596), channel_id=1, source_target_pairs={{0,8},{4,12},{8,0},{12,4},{16,20},{20,16},{24,28},{28,24},{1,9},{5... | collective-permute-start | bytes 4718600 | tf_op jit(solution)/shard_map/ppermute | solution.py:539
  431.8 49.4 %collective-permute-start.21 = (bf16[192,512]{1,0:T(8,128)(2,1)}, bf16[192,512]{1,0:T(8,128)(2,1)}, u32[]{:S(2)}, u32[]{:S(2)}) collective-permute-start(bf16[192,512]{1,0:T(8,128)(2,1)} %get-tuple-element.130), channel_id=1, source_target_pairs={{1,0},{0,1},{17,2},{16,3},{3,16},{2,17},{19,18},{18,19},{5,4},{4,5... | collective-permute-start | bytes 589832 | tf_op jit(solution)/shard_map/ppermute | solution.py:547
  431.8 49.9 %collective-permute-start.20 = (bf16[192,512]{1,0:T(8,128)(2,1)}, bf16[192,512]{1,0:T(8,128)(2,1)}, u32[]{:S(2)}, u32[]{:S(2)}) collective-permute-start(bf16[192,512]{1,0:T(8,128)(2,1)} %get-tuple-element.129), channel_id=1, source_target_pairs={{0,0},{1,1},{16,2},{17,3},{2,16},{3,17},{18,18},{19,19},{4,4},{5,5... | collective-permute-start | bytes 589832 | tf_op jit(solution)/shard_map/ppermute | solution.py:547
  459.2 33.4 %collective-permute-start.37 = (f32[768,512]{1,0:T(8,128)}, f32[768,512]{1,0:T(8,128)}, u32[]{:S(2)}, u32[]{:S(2)}) collective-permute-start(f32[768,512]{1,0:T(8,128)} %shard_map.360), channel_id=1, source_target_pairs={{0,16},{16,0},{1,17},{17,1},{2,18},{18,2},{3,19},{19,3},{4,20},{20... | collective-permute-start | bytes 4718600 | tf_op jit(solution)/shard_map/ppermute | solution.py:528
  476.0 52.0 %collective-permute-start.41 = (bf16[2,192,2048]{2,1,0:T(8,128)(2,1)}, bf16[2,192,2048]{2,1,0:T(8,128)(2,1)}, u32[]{:S(2)}, u32[]{:S(2)}) collective-permute-start(bf16[2,192,2048]{2,1,0:T(8,128)(2,1)} %broadcast_select_fusion.6), channel_id=1, source_target_pairs={{0,16},{16,0},{1,17},{17,1},{2,18},{18,2},{3,19},{19,3},{4,20},{20... | collective-permute-start | bytes 4718600 | tf_op jit(solution)/shard_map/ppermute | solution.py:528
  488.4 47.0 %collective-permute-start.50 = (bf16[768,768]{1,0:T(8,128)(2,1)}, bf16[768,768]{1,0:T(8,128)(2,1)}, u32[]{:S(2)}, u32[]{:S(2)}) collective-permute-start(bf16[768,768]{1,0:T(8,128)(2,1)} %slice_bitcast_fusion), channel_id=1, source_target_pairs={{0,4},{4,0},{8,12},{12,8},{16,24},{20,28},{24,16},{28,20},{1,5},{5... | collective-permute-start | bytes 3538952 | tf_op jit(solution)/shard_map/ppermute | solution.py:539
  519.3 79.2 %collective-permute-start.38 = (bf16[2,192,1024]{2,1,0:T(8,128)(2,1)}, bf16[2,192,1024]{2,1,0:T(8,128)(2,1)}, u32[]{:S(2)}, u32[]{:S(2)}) collective-permute-start(bf16[2,192,1024]{2,1,0:T(8,128)(2,1)} %broadcast_select_fusion.10), channel_id=1, source_target_pairs={{0,16},{16,0},{1,17},{17,1},{2,18},{18,2},{3,19},{19,3},{4,20},{20... | collective-permute-start | bytes 2359304 | tf_op jit(solution)/shard_map/ppermute | solution.py:528
  526.3 63.9 %collective-permute-start.44 = (bf16[2,768,768]{2,1,0:T(8,128)(2,1)}, bf16[2,768,768]{2,1,0:T(8,128)(2,1)}, u32[]{:S(2)}, u32[]{:S(2)}) collective-permute-start(bf16[2,768,768]{2,1,0:T(8,128)(2,1)} %broadcast_select_fusion.1), channel_id=1, source_target_pairs={{0,20},{4,16},{8,28},{12,24},{16,8},{20,12},{24,0},{28,4},{1,21},{... | collective-permute-start | bytes 7077896 | tf_op jit(solution)/shard_map/ppermute | solution.py:539
  532.5 80.5 %collective-permute-start.42 = (bf16[192,2048]{1,0:T(8,128)(2,1)}, bf16[192,2048]{1,0:T(8,128)(2,1)}, u32[]{:S(2)}, u32[]{:S(2)}) collective-permute-start(bf16[192,2048]{1,0:T(8,128)(2,1)} %slice_bitcast_fusion.4), channel_id=1, source_target_pairs={{0,1},{1,0},{2,3},{3,2},{4,5},{5,4},{6,7},{7,6},{8,9},{9,8},{10,11... | collective-permute-start | bytes 2359304 | tf_op jit(solution)/shard_map/ppermute | solution.py:531
  538.1 50.8 %collective-permute-start.51 = (bf16[2,192,768]{2,1,0:T(8,128)(2,1)}, bf16[2,192,768]{2,1,0:T(8,128)(2,1)S(1)}, u32[]{:S(2)}, u32[]{:S(2)}) collective-permute-start(bf16[2,192,768]{2,1,0:T(8,128)(2,1)} %bitcast.107), channel_id=1, source_target_pairs={{0,1},{1,0},{2,3},{3,2},{4,5},{5,4},{6,7},{7,6},{8,9},{9,8},{10,11... | collective-permute-start | bytes 1769480 | tf_op jit(solution)/shard_map/ppermute | solution.py:531
  610.6 23.0 %collective-permute-start.46 = (bf16[2,192,768]{2,1,0:T(8,128)(2,1)S(1)}, bf16[2,192,768]{2,1,0:T(8,128)(2,1)S(1)}, u32[]{:S(2)}, u32[]{:S(2)}) collective-permute-start(bf16[2,192,768]{2,1,0:T(8,128)(2,1)S(1)} %bitcast.235), channel_id=1, source_target_pairs={{0,1},{1,0},{2,3},{3,2},{4,5},{5,4},{6,7},{7,6},{8,9},{9,8},{10,11... | collective-permute-start | bytes 1769480 | tf_op jit(solution)/shard_map/ppermute | solution.py:531
  614.4 47.9 %collective-permute-start.43 = (bf16[192,2048]{1,0:T(8,128)(2,1)S(1)}, bf16[192,2048]{1,0:T(8,128)(2,1)}, u32[]{:S(2)}, u32[]{:S(2)}) collective-permute-start(bf16[192,2048]{1,0:T(8,128)(2,1)S(1)} %fusion.18), channel_id=1, source_target_pairs={{0,0},{1,1},{2,16},{3,17},{16,2},{17,3},{18,18},{19,19},{4,4},{5,5... | collective-permute-start | bytes 2359304 | tf_op jit(solution)/shard_map/ppermute | solution.py:628
  616.9 43.5 %collective-permute-start.40 = (bf16[192,1024]{1,0:T(8,128)(2,1)}, bf16[192,1024]{1,0:T(8,128)(2,1)}, u32[]{:S(2)}, u32[]{:S(2)}) collective-permute-start(bf16[192,1024]{1,0:T(8,128)(2,1)} %fusion.24), channel_id=1, source_target_pairs={{0,0},{1,1},{2,16},{3,17},{16,2},{17,3},{18,18},{19,19},{4,4},{5,5... | collective-permute-start | bytes 1179656 | tf_op jit(solution)/shard_map/ppermute | solution.py:628
  633.7 24.0 %collective-permute-start.47 = (bf16[192,768]{1,0:T(8,128)(2,1)S(1)}, bf16[192,768]{1,0:T(8,128)(2,1)S(1)}, u32[]{:S(2)}, u32[]{:S(2)}) collective-permute-start(bf16[192,768]{1,0:T(8,128)(2,1)S(1)} %slice_bitcast_fusion.28), channel_id=1, source_target_pairs={{0,2},{1,3},{2,0},{3,1},{4,6},{5,7},{6,4},{7,5},{8,10},{9,11},{10,... | collective-permute-start | bytes 884744 | tf_op jit(solution)/shard_map/ppermute | solution.py:531
  (146 other events, 995.1 us)

commit v2 on v1

v2 whole, which is shorter than its diff:
```python
from functools import partial

import jax
import jax.numpy as jnp
from jax import lax
from jax.experimental import pallas as pl
from jax.experimental.pallas import tpu as pltpu
from jax.sharding import PartitionSpec as P

HEAD = 64
EPS = 1e-06
NEGATIVE = -1e30
BF = jnp.bfloat16
F32 = jnp.float32
MIB = 1 << 20


def mm(left, right, dims):
    return lax.dot_general(left, right, (dims, ((), ())), preferred_element_type=F32)


def nn(left, right):
    return mm(left, right, ((1,), (0,)))


def tn(left, right):
    return mm(left, right, ((0,), (0,)))


def nt(left, right):
    return mm(left, right, ((1,), (1,)))


def params(mib, axes=1):
    return pltpu.CompilerParams(
        dimension_semantics=("arbitrary",) * axes, vmem_limit_bytes=mib * MIB
    )


def whole(shape):
    return pl.BlockSpec(shape, lambda *_: (0,) * len(shape))


def scores_of(key, query, start, prefix, causal):
    scores = tn(key, query * jnp.asarray(HEAD**-0.5, BF))
    if causal:
        keys = lax.broadcasted_iota(jnp.int32, scores.shape, 0)
        rows = lax.broadcasted_iota(jnp.int32, scores.shape, 1) + start
        scores = jnp.where((keys <= rows) | (keys < prefix), scores, NEGATIVE)
    return scores


def attend_forward(info, query, key, value, causal):
    (q_arr, q_row, q_moves), (k_arr, k_row), (v_arr, v_row) = query, key, value
    tq = info["tq"]
    blocks = q_arr.shape[0]
    heads = info["heads"]
    tk = k_arr.shape[2]

    def body(s_ref, q_ref, k_ref, v_ref, o_ref, l_ref):
        scores = scores_of(k_ref[0], q_ref[0], s_ref[0] * tq, s_ref[1], causal)
        top = jnp.max(scores, axis=0, keepdims=True)
        weights = jnp.exp(scores - top)
        total = jnp.sum(weights, axis=0, keepdims=True)
        mixed = nn(v_ref[0], weights.astype(BF))
        o_ref[0] = (mixed / total).astype(BF)
        l_ref[0] = top + jnp.log(total)

    return pl.pallas_call(
        body,
        out_shape=(
            jax.ShapeDtypeStruct((blocks, heads * HEAD, tq), BF),
            jax.ShapeDtypeStruct((blocks * heads, 1, tq), F32),
        ),
        grid_spec=pltpu.PrefetchScalarGridSpec(
            num_scalar_prefetch=1,
            grid=(blocks, heads),
            in_specs=[
                pl.BlockSpec(
                    (1, HEAD, tq), lambda b, h, s: (b, q_row + h, s[0] if q_moves else 0)
                ),
                pl.BlockSpec((1, HEAD, tk), lambda b, h, s: (b, k_row + h, 0)),
                pl.BlockSpec((1, HEAD, tk), lambda b, h, s: (b, v_row + h, 0)),
            ],
            out_specs=(
                pl.BlockSpec((1, HEAD, tq), lambda b, h, s: (b, h, 0)),
                pl.BlockSpec((1, 1, tq), lambda b, h, s: (b * heads + h, 0, 0)),
            ),
        ),
        compiler_params=params(48, 2),
    )(info["scalars"], q_arr, k_arr, v_arr)


def attend_backward(info, query, key, value, incoming, totals, causal):
    (q_arr, q_row, q_moves), (k_arr, k_row), (v_arr, v_row) = query, key, value
    tq = info["tq"]
    blocks = q_arr.shape[0]
    heads = info["heads"]
    tk = k_arr.shape[2]

    def body(s_ref, q_ref, k_ref, v_ref, g_ref, l_ref, dq_ref, dk_ref, dv_ref):
        q = q_ref[0]
        scores = scores_of(k_ref[0], q, s_ref[0] * tq, s_ref[1], causal)
        weights = jnp.exp(scores - l_ref[0])
        dp = tn(v_ref[0], g_ref[0])
        inner = weights * dp
        centre = jnp.sum(inner, axis=0, keepdims=True)
        ds = (inner - weights * centre).astype(BF)
        dv_ref[0] = nt(g_ref[0], weights.astype(BF)).astype(BF)
        dq_ref[0] = (nn(k_ref[0], ds) * HEAD**-0.5).astype(BF)
        dk_ref[0] = (nt(q, ds) * HEAD**-0.5).astype(BF)

    return pl.pallas_call(
        body,
        out_shape=(
            jax.ShapeDtypeStruct((blocks, heads * HEAD, tq), BF),
            jax.ShapeDtypeStruct((blocks, heads * HEAD, tk), BF),
            jax.ShapeDtypeStruct((blocks, heads * HEAD, tk), BF),
        ),
        grid_spec=pltpu.PrefetchScalarGridSpec(
            num_scalar_prefetch=1,
            grid=(blocks, heads),
            in_specs=[
                pl.BlockSpec(
                    (1, HEAD, tq), lambda b, h, s: (b, q_row + h, s[0] if q_moves else 0)
                ),
                pl.BlockSpec((1, HEAD, tk), lambda b, h, s: (b, k_row + h, 0)),
                pl.BlockSpec((1, HEAD, tk), lambda b, h, s: (b, v_row + h, 0)),
                pl.BlockSpec((1, HEAD, tq), lambda b, h, s: (b, h, 0)),
                pl.BlockSpec((1, 1, tq), lambda b, h, s: (b * heads + h, 0, 0)),
            ],
            out_specs=(
                pl.BlockSpec((1, HEAD, tq), lambda b, h, s: (b, h, 0)),
                pl.BlockSpec((1, HEAD, tk), lambda b, h, s: (b, h, 0)),
                pl.BlockSpec((1, HEAD, tk), lambda b, h, s: (b, h, 0)),
            ),
        ),
        compiler_params=params(48, 2),
    )(info["scalars"], q_arr, k_arr, v_arr, incoming, totals)


GELU_A = 0.7978845608028654
GELU_B = 0.044715


def gelu_parts(gate):
    inner = jnp.tanh(GELU_A * (gate + GELU_B * gate * gate * gate))
    value = 0.5 * gate * (1.0 + inner)
    slope = 0.5 * (1.0 + inner) + 0.5 * gate * (1.0 - inner * inner) * (
        GELU_A * (1.0 + 3.0 * GELU_B * gate * gate)
    )
    return value, slope


def ff_forward(packs, normed):
    d, lanes = packs[0].shape
    wide = lanes // 3
    tokens = normed.shape[1]
    n = len(packs)

    def body(*refs):
        w_refs, x_ref, save_refs, out_ref = refs[:n], refs[n], refs[n + 1 : 2 * n + 1], refs[-1]
        for b, (w_ref, save_ref) in enumerate(zip(w_refs, save_refs)):
            both = tn(w_ref[:, : 2 * wide], x_ref[...])
            save_ref[...] = both.astype(BF)
            value, _ = gelu_parts(both[:wide])
            hidden = (value * both[wide:]).astype(BF)
            part = nn(w_ref[:, 2 * wide :], hidden)
            out_ref[...] = part if b == 0 else out_ref[...] + part

    return pl.pallas_call(
        body,
        out_shape=[jax.ShapeDtypeStruct((2 * wide, tokens), BF)] * n
        + [jax.ShapeDtypeStruct((d, tokens), F32)],
        compiler_params=params(48, 0),
    )(*packs, normed)


def ff_backward(order, packs, saved, normed, grad):
    d, lanes = packs[0].shape
    wide = lanes // 3
    tokens = normed.shape[1]
    n = len(packs)

    def body(s_ref, *refs):
        w_refs, save_refs = refs[:n], refs[n : 2 * n]
        x_ref, g_ref, dw_ref, out_ref = refs[2 * n :]
        for b, (w_ref, save_ref) in enumerate(zip(w_refs, save_refs)):
            dh = tn(w_ref[:, 2 * wide :], g_ref[...])
            gate, up = save_ref[:wide].astype(F32), save_ref[wide:].astype(F32)
            value, slope = gelu_parts(gate)
            hidden = (value * up).astype(BF)
            grads = jnp.concatenate(
                [(dh * up * slope).astype(BF), (dh * value).astype(BF)], axis=0
            )
            first = nt(x_ref[...], grads).astype(BF)
            second = nt(g_ref[...], hidden).astype(BF)
            dw_ref[s_ref[b], :, : 2 * wide] = first
            dw_ref[s_ref[b], :, 2 * wide :] = second
            part = nn(w_ref[:, : 2 * wide], grads)
            out_ref[...] = part if b == 0 else out_ref[...] + part

    return pl.pallas_call(
        body,
        out_shape=(
            jax.ShapeDtypeStruct((n, d, lanes), BF),
            jax.ShapeDtypeStruct((d, tokens), F32),
        ),
        grid_spec=pltpu.PrefetchScalarGridSpec(
            num_scalar_prefetch=1,
            grid=(1,),
            in_specs=[whole((d, lanes))] * n
            + [whole((2 * wide, tokens))] * n
            + [whole((d, tokens))] * 2,
            out_specs=(whole((n, d, lanes)), whole((d, tokens))),
        ),
        compiler_params=params(60),
    )(order, *packs, *saved, normed, grad)


def norm_in(parts, gain, tokens, tile=256):
    d = parts[0].shape[0]
    n = len(parts)

    def body(*refs):
        x_refs, g_ref, sum_ref, norm_ref, scale_ref = refs[:n], refs[n], *refs[n + 1 :]
        states = x_refs[0][...].astype(F32)
        if n > 1:
            rest = x_refs[1][...]
            for ref in x_refs[2:]:
                rest = rest + ref[...]
            states = states + rest
        scale = lax.rsqrt(jnp.mean(states * states, axis=0, keepdims=True) + EPS)
        sum_ref[...] = states
        scale_ref[...] = scale
        norm_ref[...] = (states * scale * g_ref[...]).astype(BF)

    spec = pl.BlockSpec((d, tile), lambda i: (0, i))
    return pl.pallas_call(
        body,
        grid=(tokens // tile,),
        in_specs=[spec] * n + [whole((d, 1))],
        out_specs=(spec, spec, pl.BlockSpec((1, tile), lambda i: (0, i))),
        out_shape=(
            jax.ShapeDtypeStruct((d, tokens), F32),
            jax.ShapeDtypeStruct((d, tokens), BF),
            jax.ShapeDtypeStruct((1, tokens), F32),
        ),
        compiler_params=params(40),
    )(*parts, gain)


def norm_out(scalars, states, gain, scale, incoming, before, place=False, tile=256):
    d, tokens = states.shape
    n = len(incoming)
    has = before is not None
    own_tiles = before.shape[1] // tile if has else 1

    def body(*refs):
        s_ref, x_ref, g_ref, r_ref = refs[:4]
        y_refs = refs[4 : 4 + n]
        b_ref = refs[4 + n] if has else None
        outs = refs[4 + n + has :]
        i = pl.program_id(0)
        states_now = x_ref[...].astype(F32)
        dy = y_refs[0][...].astype(F32)
        for ref in y_refs[1:]:
            dy = dy + ref[...].astype(F32)
        scale_now = r_ref[...]
        weighted = dy * g_ref[...]
        inner = jnp.mean(weighted * states_now, axis=0, keepdims=True)
        total = scale_now * weighted - states_now * (scale_now * scale_now * scale_now * inner)
        if has and place:
            here = (i // own_tiles == s_ref[0]) & (s_ref[2] == 0)
            total = total + b_ref[...] * jnp.where(here, 1.0, 0.0)
        elif has:
            total = total + b_ref[...]
        gain_grad = jnp.sum(dy * states_now * scale_now, axis=1, keepdims=True)
        low_ref, gain_ref = outs[-2:]
        if not place:
            outs[0][...] = total
        low_ref[...] = total.astype(BF)

        @pl.when(i == 0)
        def _():
            gain_ref[...] = gain_grad

        @pl.when(i > 0)
        def _():
            gain_ref[...] += gain_grad

    spec = pl.BlockSpec((d, tile), lambda i, s: (0, i))
    out_shape = [] if place else [jax.ShapeDtypeStruct((d, tokens), F32)]
    out_shape += [jax.ShapeDtypeStruct((d, tokens), BF), jax.ShapeDtypeStruct((d, 1), F32)]
    return pl.pallas_call(
        body,
        out_shape=out_shape,
        grid_spec=pltpu.PrefetchScalarGridSpec(
            num_scalar_prefetch=1,
            grid=(tokens // tile,),
            in_specs=[spec, whole((d, 1)), pl.BlockSpec((1, tile), lambda i, s: (0, i))]
            + [spec] * n
            + ([pl.BlockSpec((d, tile), lambda i, s: (0, i % own_tiles))] if has else []),
            out_specs=[spec] * (len(out_shape) - 1) + [whole((d, 1))],
        ),
        compiler_params=params(40),
    )(scalars, states, gain, scale, *incoming, *([before] if has else []))


def lane_block(lanes, low, high):
    if low // 256 == (high - 1) // 256 and lanes % 256 == 0:
        return 256, low // 256, low % 256
    return lanes, 0, low


def project(pack, normed, low, high):
    blocks, d, lanes = pack.shape
    tokens = normed.shape[1]
    size, index, at = lane_block(lanes, low, high)

    def body(w_ref, x_ref, o_ref):
        o_ref[0] = tn(w_ref[0, :, at : at + high - low], x_ref[...]).astype(BF)

    return pl.pallas_call(
        body,
        grid=(blocks,),
        in_specs=[pl.BlockSpec((1, d, size), lambda b: (b, 0, index)), whole((d, tokens))],
        out_specs=pl.BlockSpec((1, high - low, tokens), lambda b: (b, 0, 0)),
        out_shape=jax.ShapeDtypeStruct((blocks, high - low, tokens), BF),
        compiler_params=params(40),
    )(pack, normed)


def combine(pack, rows, low, high):
    blocks, d, lanes = pack.shape
    tokens = rows.shape[2]
    size, index, at = lane_block(lanes, low, high)

    def body(w_ref, x_ref, o_ref):
        part = nn(w_ref[0, :, at : at + high - low], x_ref[0])
        for b in range(1, blocks):
            part += nn(w_ref[b, :, at : at + high - low], x_ref[b])
        o_ref[...] = part

    return pl.pallas_call(
        body,
        grid=(1,),
        in_specs=[
            pl.BlockSpec((blocks, d, size), lambda b: (0, 0, index)),
            whole((blocks, high - low, tokens)),
        ],
        out_specs=whole((d, tokens)),
        out_shape=jax.ShapeDtypeStruct((d, tokens), F32),
        compiler_params=params(40),
    )(pack, rows)


def weight_grads(scalars, pairs, lanes):
    d = pairs[0][0].shape[0]
    n = len(pairs)
    lefts = [left for left, _ in pairs]
    rights = [right for _, right in pairs]

    def body(*refs):
        outs = refs[2 * n + 1 :]
        at = 0
        for left_ref, right_ref in zip(refs[1 : n + 1], refs[n + 1 : 2 * n + 1]):
            width = right_ref.shape[1]
            for b, out_ref in enumerate(outs):
                out_ref[:, at : at + width] = nt(left_ref[...], right_ref[b]).astype(BF)
            at += width

    def left_spec(left, right):
        tokens = right.shape[2]
        if left.shape[1] == tokens:
            return pl.BlockSpec((d, tokens), lambda b, s: (0, 0))
        return pl.BlockSpec((d, tokens), lambda b, s: (0, s[0]))

    return pl.pallas_call(
        body,
        out_shape=[jax.ShapeDtypeStruct((d, lanes), BF)] * 2,
        grid_spec=pltpu.PrefetchScalarGridSpec(
            num_scalar_prefetch=1,
            grid=(1,),
            in_specs=[left_spec(left, right) for left, right in pairs]
            + [whole(right.shape) for right in rights],
            out_specs=[whole((d, lanes))] * 2,
        ),
        compiler_params=params(48),
    )(scalars, *lefts, *rights)


def split_sum(parts):
    d, lanes = parts[0].shape
    size = d // 4
    n = len(parts)

    def body(*refs):
        for f, out_ref in enumerate(refs[n:]):
            rows = slice(f * size, (f + 1) * size)
            acc = refs[0][rows].astype(F32)
            for ref in refs[1:n]:
                acc += ref[rows].astype(F32)
            out_ref[...] = acc.astype(BF)

    return pl.pallas_call(
        body,
        out_shape=[jax.ShapeDtypeStruct((size, lanes), BF)] * 4,
        compiler_params=params(40, 0),
    )(*parts)


def source_grads(pack, own, own_low, wide, wide_low, place, width, kind):
    blocks, d, lanes = pack.shape
    tq = own.shape[2] if own is not None else 0
    n = len(wide)
    tokens = wide[0].shape[2]
    step = min(1024, tokens)

    def body(*refs):
        s_ref, w_ref = refs[0], refs[1]
        wide_refs = refs[2 : 2 + n]
        o_ref = refs[-1]
        acc = jnp.zeros((d, step), F32)
        for b in range(blocks):
            for at, ref in zip(wide_low, wide_refs):
                acc += nn(w_ref[b, :, at : at + width], ref[b])
        o_ref[...] = acc.astype(kind)
        if own is not None:
            own_ref = refs[2 + n]
            part = jnp.zeros((d, tq), F32)
            for b in range(blocks):
                part += nn(w_ref[b, :, own_low : own_low + width], own_ref[b])
            where = pl.ds(pl.multiple_of(s_ref[0] * tq, tq), tq)
            o_ref[:, where] += part.astype(kind)

    return pl.pallas_call(
        body,
        out_shape=jax.ShapeDtypeStruct((d, tokens), kind),
        grid_spec=pltpu.PrefetchScalarGridSpec(
            num_scalar_prefetch=1,
            grid=(tokens // step,),
            in_specs=[pl.BlockSpec((blocks, d, lanes), lambda i, s: (0, 0, 0))]
            + [pl.BlockSpec((blocks, width, step), lambda i, s: (0, 0, i))] * n
            + (
                [pl.BlockSpec((blocks, width, tq), lambda i, s: (0, 0, 0))]
                if own is not None
                else []
            ),
            out_specs=pl.BlockSpec((d, step), lambda i, s: (0, i)),
        ),
        compiler_params=params(40),
    )(place, pack, *wide, *([own] if own is not None else []))


VB = 512


def assemble(s_ref, own_ref, one_ref, two_ref, three_ref, out_ref):
    size = own_ref.shape[0]
    out_ref[:size] = own_ref[...]
    out_ref[pl.ds(pl.multiple_of((1 + s_ref[1]) * size, size), size), :] = one_ref[...]
    out_ref[pl.ds(pl.multiple_of((2 - s_ref[1]) * size, size), size), :] = two_ref[...]
    out_ref[3 * size :] = three_ref[...]


def table_specs(size):
    return [pl.BlockSpec((size, VB), lambda v, s: (0, v))] * 4


def vocab_forward(scalars, hidden, table, wanted):
    half_chunks, d, step = hidden[0].shape
    chunks = 2 * half_chunks
    own = table[0]
    size, width = own.shape
    parts = width // VB

    def body(s_ref, h0_ref, h1_ref, own_ref, one_ref, two_ref, three_ref, t_ref, e_ref, m_ref, st_ref, blk, flip):
        vb = pl.program_id(0)

        @pl.when(vb == 0)
        def _():
            st_ref[0] = jnp.full((chunks, step), NEGATIVE, F32)
            st_ref[1:] = jnp.zeros((2, chunks, step), F32)

        assemble(s_ref, own_ref, one_ref, two_ref, three_ref, blk)
        flip[...] = blk[...].T
        ids = lax.broadcasted_iota(jnp.int32, (VB, step), 0)

        def one_chunk(n, states, masked):
            logits = nn(flip[...], states)
            row = slice(n, n + 1)
            st_ref[2, row] += jnp.sum(
                jnp.where(ids == t_ref[row] - vb * VB, logits, 0.0), axis=0, keepdims=True
            )
            if masked:
                logits = jnp.where(ids < s_ref[0] - vb * VB, logits, NEGATIVE)
            before = st_ref[0, row]
            top = jnp.maximum(before, jnp.max(logits, axis=0, keepdims=True))
            exps = jnp.exp(logits - top)
            st_ref[1, row] = st_ref[1, row] * jnp.exp(before - top) + jnp.sum(
                exps, axis=0, keepdims=True
            )
            st_ref[0, row] = top
            m_ref[0, row] = top
            e_ref[n] = exps.astype(BF)

        def some(masked):
            for n in range(chunks):
                one_chunk(n, (h0_ref, h1_ref)[n // half_chunks][n % half_chunks], masked)

        inside = (vb + 1) * VB <= s_ref[0]
        pl.when(inside)(partial(some, False))
        pl.when(jnp.logical_not(inside))(partial(some, True))

    return pl.pallas_call(
        body,
        out_shape=(
            jax.ShapeDtypeStruct((chunks, width, step), BF),
            jax.ShapeDtypeStruct((parts, chunks, step), F32),
            jax.ShapeDtypeStruct((3, chunks, step), F32),
        ),
        grid_spec=pltpu.PrefetchScalarGridSpec(
            num_scalar_prefetch=1,
            grid=(parts,),
            in_specs=[whole((half_chunks, d, step))] * 2
            + table_specs(size)
            + [whole((chunks, step))],
            out_specs=(
                pl.BlockSpec((chunks, VB, step), lambda v, s: (0, v, 0)),
                pl.BlockSpec((1, chunks, step), lambda v, s: (v, 0, 0)),
                whole((3, chunks, step)),
            ),
            scratch_shapes=[pltpu.VMEM((d, VB), BF), pltpu.VMEM((VB, d), BF)],
        ),
        compiler_params=params(48),
    )(scalars, *hidden, *table, wanted)


def vocab_hidden_grad(scalars, exps, tops, logsum, first_row, table, wanted):
    chunks, width, step = exps.shape
    own = table[0]
    size = own.shape[0]
    d = 4 * size
    parts = width // VB

    def body(s_ref, e_ref, m_ref, l_ref, own_ref, one_ref, two_ref, three_ref, t_ref, g_ref, o_ref, p_ref, blk, acc):
        vb = pl.program_id(0)

        @pl.when(vb == 0)
        def _():
            acc[...] = jnp.zeros_like(acc)

        assemble(s_ref, own_ref, one_ref, two_ref, three_ref, blk)
        ids = lax.broadcasted_iota(jnp.int32, (VB, step), 0)

        for n in range(chunks):
            row, at = slice(n, n + 1), slice(first_row + n, first_row + n + 1)
            scale = jnp.exp(m_ref[0, row] - l_ref[at])
            probs = e_ref[n].astype(F32) * scale
            grads = jnp.where(ids == t_ref[row] - vb * VB, probs - 1.0, probs).astype(BF)
            g_ref[n] = grads
            acc[n] += nn(blk[...], grads)

        @pl.when(vb == parts - 1)
        def _():
            o_ref[...] = acc[: chunks // 2].astype(BF)
            p_ref[...] = acc[chunks // 2 :].astype(BF)

    return pl.pallas_call(
        body,
        out_shape=(
            jax.ShapeDtypeStruct((chunks, width, step), BF),
            jax.ShapeDtypeStruct((chunks // 2, d, step), BF),
            jax.ShapeDtypeStruct((chunks // 2, d, step), BF),
        ),
        grid_spec=pltpu.PrefetchScalarGridSpec(
            num_scalar_prefetch=1,
            grid=(parts,),
            in_specs=[
                pl.BlockSpec((chunks, VB, step), lambda v, s: (0, v, 0)),
                pl.BlockSpec((1, chunks, step), lambda v, s: (v, 0, 0)),
                whole(logsum.shape),
            ]
            + table_specs(size)
            + [whole((chunks, step))],
            out_specs=(
                pl.BlockSpec((chunks, VB, step), lambda v, s: (0, v, 0)),
                whole((chunks // 2, d, step)),
                whole((chunks // 2, d, step)),
            ),
            scratch_shapes=[pltpu.VMEM((d, VB), BF), pltpu.VMEM((chunks, d, step), F32)],
        ),
        input_output_aliases={1: 0},
        compiler_params=params(56),
    )(scalars, exps, tops, logsum, *table, wanted)


def vocab_table_grad(places, hidden, grads):
    per, d, step = hidden[0].shape
    chunks, width, _ = grads[0].shape
    unit = d // 8
    parts = width // VB
    nh, ng = len(hidden), len(grads)

    def body(*refs):
        s_ref, h_refs, g_refs, o_ref = refs[0], refs[1 : 1 + nh], refs[1 + nh : -1], refs[-1]
        acc = None
        for n in range(nh * per):
            part = nt(h_refs[n // per][n % per], g_refs[n // chunks][n % chunks])
            acc = part if acc is None else acc + part
        for u in range(8):
            spot = pl.ds(pl.multiple_of(s_ref[u] * unit, unit), unit)
            o_ref[spot, :] = acc[u * unit : (u + 1) * unit].astype(BF)

    return pl.pallas_call(
        body,
        out_shape=jax.ShapeDtypeStruct((d, width), BF),
        grid_spec=pltpu.PrefetchScalarGridSpec(
            num_scalar_prefetch=1,
            grid=(parts,),
            in_specs=[whole((per, d, step))] * nh
            + [pl.BlockSpec((chunks, VB, step), lambda v, s: (0, v, 0))] * ng,
            out_specs=pl.BlockSpec((d, VB), lambda v, s: (0, v)),
        ),
        compiler_params=params(48),
    )(places, *hidden, *grads)


def merge_core(mine, other):
    def body(a_ref, b_ref, o_ref):
        for i in range(8):
            row, far = slice(i, i + 1), slice(i ^ 2, (i ^ 2) + 1)
            top = jnp.maximum(a_ref[0, row], b_ref[0, far])
            o_ref[0, row] = top
            o_ref[1, row] = a_ref[1, row] * jnp.exp(a_ref[0, row] - top) + b_ref[
                1, far
            ] * jnp.exp(b_ref[0, far] - top)
            o_ref[2, row] = a_ref[2, row] + b_ref[2, far]

    return pl.pallas_call(
        body,
        out_shape=jax.ShapeDtypeStruct(mine.shape, F32),
        compiler_params=params(16, 0),
    )(mine, other)


def merge_chips(spots, items):
    step = items[0].shape[2]
    flips = (0, 4, 1, 5)

    def body(s_ref, *refs):
        log_ref, loss_ref, rows = refs[-3:]
        for i in range(8):
            at = [slice(i ^ f, (i ^ f) + 1) for f in flips]
            top = refs[0][0, at[0]]
            for ref, row in zip(refs[1:4], at[1:]):
                top = jnp.maximum(top, ref[0, row])
            total = jnp.zeros((1, step), F32)
            picked = jnp.zeros((1, step), F32)
            for ref, row in zip(refs[:4], at):
                total += ref[1, row] * jnp.exp(ref[0, row] - top)
                picked += ref[2, row]
            logsum = top + jnp.log(total)
            log_ref[at[0]] = logsum
            rows[i] = logsum - picked
        for n in range(4):
            loss_ref[n] = rows[s_ref[n]]

    return pl.pallas_call(
        body,
        out_shape=(
            jax.ShapeDtypeStruct((8, step), F32),
            jax.ShapeDtypeStruct((4, 1, step), F32),
        ),
        grid_spec=pltpu.PrefetchScalarGridSpec(
            num_scalar_prefetch=1,
            grid=(1,),
            in_specs=[whole(items[0].shape)] * 4,
            out_specs=(whole((8, step)), whole((4, 1, step))),
            scratch_shapes=[pltpu.VMEM((8, 1, step), F32)],
        ),
        compiler_params=params(16),
    )(spots, *items)


class Moves:
    def __init__(self, dp):
        self.dp = dp

    def core(self, x):
        return lax.ppermute(x, "dp", [(i, i ^ 1) for i in range(self.dp)])

    def col(self, x, bit):
        return lax.ppermute(x, "col", [(i, i ^ bit) for i in range(4)])

    def cols(self, x, bit, core):
        perm = []
        for i in range(core, self.dp, 2):
            for c in range(4):
                perm.append((i * 4 + c, i * 4 + (c ^ bit)))
        return lax.ppermute(x, ("dp", "col"), perm)

    def row(self, x, bit):
        return lax.ppermute(x, "row", [(i, i ^ bit) for i in range(4)])

    def rows(self, x, pairs):
        perm = []
        for i in range(self.dp):
            for r in range(4):
                if i % 2 in pairs:
                    flip, bit = pairs[i % 2]
                    perm.append((i * 4 + r, (i ^ flip) * 4 + (r ^ bit)))
        return lax.ppermute(x, ("dp", "row"), perm)

    def spread(self, x, turn, back=False):
        perm = []
        for i in range(self.dp):
            for c in range(4):
                dest = (i - i % 2 + c // 2) * 4 + 2 * (i % 2) + (c % 2 ^ turn)
                perm.append((dest, i * 4 + c) if back else (i * 4 + c, dest))
        return lax.ppermute(x, ("dp", "col"), perm)


STEP_ONE = {0: (0, 1), 1: (0, 2)}
STEP_TWO = {0: (1, 2), 1: (1, 1)}
STEP_TWO_BACK = {0: (1, 1), 1: (1, 2)}
SAME_TWO = {0: (0, 2), 1: (0, 1)}


def same(bit):
    return {0: (0, bit), 1: (0, bit)}


def tie(*xs):
    return lax.optimization_barrier(xs)


def plus(a, b, kind=BF):
    return (a.astype(F32) + b.astype(F32)).astype(kind)


def local(
    inputs,
    encoder,
    prefix,
    targets,
    gain_self,
    w_query,
    w_key,
    w_value,
    w_attn_out,
    gain_cross,
    w_cross_query,
    w_cross_key,
    w_cross_value,
    w_cross_out,
    gain_ff,
    w_gate,
    w_up,
    w_ff_out,
    gain_final,
    embed_table,
    *,
    dp,
):
    move = Moves(dp)
    core = lax.axis_index("dp") % 2
    row = lax.axis_index("row")
    col = lax.axis_index("col")
    first_core = core == 0
    side = col // 2
    half = col % 2
    block = inputs.shape[0]
    d = 4 * block
    seq = inputs.shape[1]
    tq = seq // 2
    tc = tq // 2
    heads = w_query.shape[1] // HEAD
    hw = heads * HEAD
    ff_half = w_gate.shape[1] // 2
    vocab = embed_table.shape[1]
    width = -(-vocab // (2 * VB)) * VB
    mine = side == core
    pick = jnp.where

    def settle(got):
        other = move.core(got)
        near, far = pick(mine, got, other), pick(mine, other, got)
        return jnp.concatenate([near[0], far[0], near[1], far[1]], axis=0)

    def hand_back(parts):
        hi = [pick(mine, parts[0], parts[1]), pick(mine, parts[2], parts[3])]
        return [move.spread(hi[0], 0, True), move.spread(hi[1], 1, True)]

    def in_order(got):
        return pick(
            half == 0,
            jnp.concatenate([got[0], got[1]], axis=1),
            jnp.concatenate([got[1], got[0]], axis=1),
        )

    def fold_core(partial_sum):
        blocks4 = partial_sum.reshape(4, block, -1)
        near = jnp.stack([blocks4[0], blocks4[2]])
        far = jnp.stack([blocks4[1], blocks4[3]])
        return pick(mine, near, far), move.core(pick(mine, far, near))

    def fold_out(keep, got):
        return [move.spread(plus(keep[n], got[n]), n, True) for n in range(2)]

    def z_sum(parts, cores):
        own, two, one, three = split_sum(parts)
        send = [(two, 2), (one, 1), (three, 3)]
        if cores is None:
            return [own] + [move.col(x, bit) for x, bit in send]
        return [own] + [move.cols(x, bit, cores) for x, bit in send]

    def total(parts):
        return sum(x.astype(F32) for x in parts)

    def swap_bits(n):
        return n // 2 + 2 * (n % 2)

    other_targets = move.core(targets)
    near, far = pick(mine, targets, other_targets), pick(mine, other_targets, targets)

    def target_chunks(lo):
        out = []
        for which in (core, 1 - core):
            for seq_targets in (near, far):
                out.append(lax.dynamic_slice_in_dim(seq_targets, lo * tq + which * tc, tc, 0))
        wanted = jnp.stack(out) - col * vocab
        return jnp.where((wanted >= 0) & (wanted < vocab), wanted - core * width, -1)

    want_near, want_far = target_chunks(half), target_chunks(1 - half)
    valid = jnp.where(first_core, width, vocab - width)
    vocab_scalars = jnp.stack([valid, core]).astype(jnp.int32)
    chip = jnp.where(mine, 0, 1)
    spots = []
    for lo in range(2):
        for h in range(2):
            spots.append((half ^ lo) * 4 + (core ^ h) * 2 + chip)
    spots = jnp.stack(spots).astype(jnp.int32)
    own_places = jnp.stack([row, row ^ (1 + core), row ^ (2 - core), row ^ 3]).astype(jnp.int32)
    places = []
    for unit in range(8):
        e = 2 * (row ^ (unit // 2)) + unit % 2
        places.append(e % 4 * 2 + e // 4)
    places = jnp.stack(places).astype(jnp.int32)

    pack_self = jnp.concatenate([w_query, w_key, w_value, w_attn_out.T], axis=1)
    pack_cross = jnp.concatenate([w_cross_query, w_cross_key, w_cross_value, w_cross_out.T], axis=1)
    sc_own = pick(first_core, pack_self, pack_cross)
    sc_own, embed_table = tie(sc_own, embed_table)
    padded = jnp.pad(embed_table, ((0, 0), (0, 2 * width - vocab)))
    table_own = pick(first_core, padded[:, :width], padded[:, width:])
    pack_ff = [
        jnp.concatenate([w[:, s : s + ff_half] for w in (w_gate, w_up, w_ff_out)], axis=1)
        for s in (0, ff_half)
    ]
    ff_own = pick(first_core, *pack_ff)

    columns = [gain_self, gain_cross, gain_ff, gain_final]
    tops = [lax.reduce_precision(g, 8, 7) for g in columns]
    columns = tops + [g - t for g, t in zip(columns, tops)]
    high = (prefix // 256).astype(F32)
    columns += [jnp.broadcast_to(high, (block,)), jnp.broadcast_to(prefix - high * 256, (block,))]
    extras = jnp.pad(jnp.stack(columns, axis=1).astype(BF), ((0, 0), (0, 128 - len(columns))))
    x_in = jnp.concatenate([inputs, extras], axis=1)

    sc_got = [move.col(sc_own, bit) for bit in (2, 1, 3)]
    table_one = move.rows(table_own, STEP_ONE)
    table_two = move.rows(table_own, SAME_TWO)
    sc, x_in, ff_own, want_near, want_far, spots, places, own_places, table_one, table_two = tie(
        jnp.concatenate([sc_own, *sc_got]), x_in, ff_own, want_near, want_far, spots, places, own_places, table_one, table_two
    )
    sc_row = move.rows(sc, STEP_ONE)
    x_got = [move.spread(x_in, 0), move.spread(x_in, 1)]
    x_near, x_far, sc_row, sc, ff_own = tie(*x_got, sc_row, sc, ff_own)
    sc_one = move.rows(sc, STEP_TWO)
    sc_two = move.rows(sc_row, STEP_TWO)
    ff_got = [move.col(ff_own, bit) for bit in (2, 1, 3)]
    states_low = settle(jnp.stack([x_near, x_far]))
    small = states_low[:, seq : seq + 16].astype(F32)
    g_self, g_cross, g_ff, g_final = (small[:, n : n + 1] + small[:, n + 4 : n + 5] for n in range(4))
    length = lax.dynamic_slice(small, (swap_bits(col ^ row) * block, 8), (1, 2))
    length = (length[0, :1] * 256 + length[0, 1:]).astype(jnp.int32)
    scalars = jnp.concatenate([half[None], length, core[None]]).astype(jnp.int32)
    info = {"tq": tq, "heads": heads, "scalars": scalars}
    states_all, normed_all, scale_all = norm_in([states_low], g_self, seq)
    states_own = lax.dynamic_slice_in_dim(states_low, half * tq, tq, 1)
    own_blocks = jnp.stack([sc, sc_row])
    normed_all, states_own, own_blocks, scalars, ff_own, *ff_got = tie(
        normed_all, states_own, own_blocks, scalars, ff_own, *ff_got
    )
    ff, enc_in = tie(jnp.concatenate([ff_own, *ff_got]), encoder)
    enc_zero = move.spread(enc_in, 0)
    other_blocks = jnp.stack([sc_one, sc_two])
    ws = pick(first_core, own_blocks, other_blocks)
    wc = pick(first_core, other_blocks, own_blocks)

    qkv = project(ws, normed_all, 0, 3 * hw)
    self_args = ((qkv, 0, True), (qkv, heads), (qkv, 2 * heads))
    qkv, ff = tie(qkv, ff)
    self_args = ((qkv, 0, True), (qkv, heads), (qkv, 2 * heads))
    ff_row = move.rows(ff, STEP_ONE)
    ff_one = move.rows(ff, SAME_TWO)
    attended, totals_self = attend_forward(info, *self_args, True)
    attended, enc_zero, enc_in = tie(attended, enc_zero, enc_in)
    enc_one = move.spread(enc_in, 1)
    branch = combine(ws, attended, 3 * hw, 4 * hw)
    first, normed_cross, scale_cross = norm_in([states_own, branch, move.core(branch)], g_cross, tq)


    cq = project(wc, normed_cross, 0, hw)
    cq, enc_one, ff_row, ff_one = tie(cq, enc_one, ff_row, ff_one)
    ff_two = move.rows(ff_row, SAME_TWO)
    enc_all = settle(jnp.stack([enc_zero, enc_one]))
    ckv = project(wc, enc_all, hw, 3 * hw)
    cross_args = ((cq, 0, False), (ckv, 0), (ckv, heads))
    crossed, totals_cross = attend_forward(info, *cross_args, False)
    crossed, ff_two, table_one = tie(crossed, ff_two, table_one)
    table_three = move.rows(table_one, SAME_TWO)
    branch = combine(wc, crossed, 3 * hw, 4 * hw)
    second, normed_ff, scale_ff = norm_in([first, branch, move.core(branch)], g_ff, tq)

    wf = (ff, ff_row, ff_one, ff_two)
    *saved, branch = ff_forward(wf, normed_ff)
    third, normed_final, scale_final = norm_in([second, branch, move.core(branch)], g_final, tq)

    def reorder(x, index):
        parts = x.reshape(4, block, x.shape[-1])
        return jnp.concatenate(
            [lax.dynamic_index_in_dim(parts, i, 0, keepdims=False) for i in index], axis=0
        )

    piece = lax.dynamic_slice_in_dim(normed_final, core * tc, tc, 1)
    piece = reorder(piece, [swap_bits(col ^ row ^ s) for s in range(4)])
    near_pieces, table_three = tie(jnp.stack([piece, move.col(piece, 2)]), table_three)
    table = (table_own, table_one, table_two, table_three)
    far_pieces = move.col(near_pieces, 1)
    hidden_near = (near_pieces, move.core(near_pieces))
    exps_near, tops_near, stats_near = vocab_forward(
        vocab_scalars, hidden_near, table, want_near
    )
    far_pieces, stats_near, out_low = tie(far_pieces, stats_near, third.astype(BF))
    hidden_far = (far_pieces, move.core(far_pieces))
    out_got = hand_back(out_low.reshape(4, block, tq))
    exps_far, tops_far, stats_far = vocab_forward(vocab_scalars, hidden_far, table, want_far)
    stats_far, *out_got = tie(stats_far, *out_got)

    stats = jnp.concatenate([stats_near, stats_far], axis=1)
    stats = merge_core(stats, move.core(stats))
    items = [stats] + [move.col(stats, bit) for bit in (1, 2, 3)]
    logsum, loss = merge_chips(spots, items)
    loss = loss.reshape(seq)

    grads_far, own_far, oth_far = vocab_hidden_grad(
        vocab_scalars, exps_far, tops_far, logsum, 4, table, want_far
    )
    part_far, exps_near = tie(plus(own_far, move.core(oth_far)), exps_near)
    come_far = move.col(part_far, 1)
    grads_near, own_near, oth_near = vocab_hidden_grad(
        vocab_scalars, exps_near, tops_near, logsum, 0, table, want_near
    )
    part = plus(own_near, move.core(oth_near), F32) + come_far.astype(F32)
    part_last, grads_near = tie(part[1].astype(BF), grads_near)
    come_last = move.col(part_last, 2)
    grad_table = vocab_table_grad(
        places, (*hidden_near, *hidden_far), (grads_near, grads_far)
    )
    if dp == 2:
        table_sum = lax.psum_scatter(grad_table, "row", scatter_dimension=0, tiled=True)
    come_last, _ = tie(come_last, grad_table)
    part = plus(part[0], come_last)
    part = reorder(part, [col ^ row ^ swap_bits(n) for n in range(4)])
    other = move.core(part)
    grad_normed = jnp.concatenate(
        [pick(first_core, part, other), pick(first_core, other, part)], axis=1
    )

    grad_third, low, gg_final = norm_out(
        scalars, third, g_final, scale_final, [grad_normed], None
    )
    ff_grads, partial_normed = ff_backward(own_places, wf, saved, normed_ff, low)
    ff_sum = lax.psum_scatter(ff_grads.reshape(4 * d, -1), "row", scatter_dimension=0, tiled=True)
    grad_second, low, gg_ff = norm_out(
        scalars, second, g_ff, scale_ff, [partial_normed, move.core(partial_normed)], grad_third
    )
    grad_crossed = project(wc, low, 3 * hw, 4 * hw)
    dcq, dck, dcv = attend_backward(info, *cross_args, grad_crossed, totals_cross, False)
    partial_normed = combine(wc, dcq, 0, hw)
    partial_other = move.core(partial_normed)
    dck, partial_normed = tie(dck, partial_normed)
    grad_enc = source_grads(wc, None, 0, (dck, dcv), (hw, 2 * hw), scalars, hw, BF)
    partial_other, grad_enc = tie(partial_other, grad_enc)
    grad_first, low_self, gg_cross = norm_out(
        scalars, first, g_cross, scale_cross, [partial_normed, partial_other], grad_second
    )
    enc_keep, enc_come = fold_core(grad_enc)
    enc_keep, enc_come, low_self, normed_cross = tie(enc_keep, enc_come, low_self, normed_cross)
    enc_come = fold_out(enc_keep, enc_come)
    cross_zero, cross_one = weight_grads(
        scalars, [(normed_cross, dcq), (enc_all, dck), (enc_all, dcv), (low, crossed)], 4 * hw
    )
    cross_zero, cross_one, low_self = tie(cross_zero, cross_one, low_self)
    cross_come = [
        move.rows(cross_zero, {0: (1, 1)}),
        move.rows(cross_one, {0: (1, 3)}),
        move.rows(cross_one, {1: (0, 2)}),
    ]

    grad_attended = project(ws, low_self, 3 * hw, 4 * hw)
    dq, dk, dv = attend_backward(info, *self_args, grad_attended, totals_self, True)
    dq, dk, ff_sum = tie(dq, dk, ff_sum)
    self_zero, self_one = weight_grads(
        scalars, [(normed_all, dq), (normed_all, dk), (normed_all, dv), (low_self, attended)], 4 * hw
    )
    self_come = [
        move.rows(self_one, {0: (0, 1)}),
        move.rows(self_zero, {1: (1, 2)}),
        move.rows(self_one, {1: (1, 3)}),
    ]
    dk, self_zero, ff_sum = tie(dk, self_zero, ff_sum)
    ff_parts = [ff_sum[p * block : (p + 1) * block] for p in range(4)]
    ff_parts[1:] = [move.col(x, bit) for x, bit in zip(ff_parts[1:], (2, 1, 3))]
    partial_normed = source_grads(ws, dq, 0, (dk, dv), (hw, 2 * hw), scalars, hw, F32)
    partial_normed, *cross_come = tie(partial_normed, *cross_come)
    cross_parts = z_sum([cross_zero, *cross_come], 1)
    partial_normed, cross_own = tie(partial_normed, cross_parts[0])
    grad_states, gg_self = norm_out(
        scalars, states_all, g_self, scale_all, [partial_normed], grad_first, True
    )
    once = jnp.where(first_core, 1.0, 0.0)
    gain_columns = jnp.concatenate([gg_self, gg_cross * once, gg_ff * once, gg_final * once], axis=1)
    gain_columns = jnp.pad(gain_columns.astype(BF), ((0, 0), (0, 124)))
    grad_states = jnp.concatenate([grad_states, gain_columns], axis=1)
    grad_states, *enc_come = tie(grad_states, *enc_come)
    in_keep, in_come = fold_core(grad_states)
    in_come = fold_out(in_keep, in_come)
    in_come[0], cross_parts[1:], ff_parts, self_come = tie(
        in_come[0], cross_parts[1:], ff_parts, self_come
    )
    self_parts = z_sum([self_zero, *self_come], 0)
    in_come = in_come[0].astype(F32) + in_come[1].astype(F32)
    in_come, self_own = tie(in_come, self_parts[0])
    packed = in_come[:, seq : seq + 4].T
    if dp == 2:
        come = [move.row(packed, bit) for bit in (1, 2, 3)]
        packed, come, self_parts[1:], table_sum = tie(packed, come, self_parts[1:], table_sum)
        packed = packed + come[0] + come[1] + come[2]
        packed = packed + move.core(packed)
    else:
        packed = lax.psum(packed, ("dp", "row"))

    grad_encoder = enc_come[0].astype(F32) + enc_come[1].astype(F32)
    grad_inputs = in_come[:, :seq]
    sum_self = total([self_own, *self_parts[1:]])
    sum_cross = total([cross_own, *cross_parts[1:]])
    sum_ff = total(ff_parts)

    if dp == 2:
        cut = table_sum.reshape(2, d // 8, width)
        keep, got = pick(first_core, cut[0], cut[1]), move.core(pick(first_core, cut[1], cut[0]))
        table_sum = jnp.concatenate(
            [pick(first_core, keep, got), pick(first_core, got, keep)[:, : vocab - width]], axis=1
        ).astype(F32)
    else:
        full = grad_table.reshape(4, 2, d // 8, width).transpose(1, 0, 2, 3).reshape(d, width)
        blank = jnp.zeros_like(full)
        full = pick(
            first_core,
            jnp.concatenate([full, blank], axis=1),
            jnp.concatenate([blank, full], axis=1),
        )[:, :vocab]
        table_sum = lax.psum_scatter(
            full, ("dp", "row"), scatter_dimension=0, tiled=True
        ).astype(F32)

    def flip_last(x):
        return jnp.concatenate([x[:, :-hw], x[:, -hw:].T], axis=1)

    both = jnp.concatenate(
        [flip_last(pick(first_core, sum_self, sum_cross)), sum_ff], axis=1
    )
    if dp == 2:
        rows_half = block // 2
        keep = pick(first_core, both[:rows_half], both[rows_half:])
        got = move.core(pick(first_core, both[rows_half:], both[:rows_half]))
        lower, upper = pick(first_core, keep, got), pick(first_core, got, keep)
    else:
        both = jnp.concatenate([pick(first_core, both, 0.0), pick(first_core, 0.0, both)], axis=1)
        both = lax.psum_scatter(both, "dp", scatter_dimension=0, tiled=True)
        lower, upper = jnp.split(both, 2, axis=1)
    out_ff0, out_ff1 = lower[:, 4 * hw :], upper[:, 4 * hw :]

    def ff_part(n):
        sl = slice(n * ff_half, (n + 1) * ff_half)
        return jnp.concatenate([out_ff0[:, sl], out_ff1[:, sl]], axis=1)

    return (
        in_order(out_got),
        loss,
        grad_inputs,
        grad_encoder,
        packed[0],
        *(lower[:, n * hw : (n + 1) * hw] for n in range(4)),
        packed[1],
        *(upper[:, n * hw : (n + 1) * hw] for n in range(4)),
        packed[2],
        ff_part(0),
        ff_part(1),
        ff_part(2),
        packed[3],
        table_sum,
    )


def solution(mesh):
    return jax.shard_map(
        partial(local, dp=mesh.shape["dp"]),
        mesh=mesh,
        in_specs=(
            P("col", ("dp", "row")),
            P("col", ("dp", "row")),
            P(("dp", "col")),
            P(("dp", "row")),
            P("col"),
            P("col", "row"),
            P("col", "row"),
            P("col", "row"),
            P("row", "col"),
            P("col"),
            P("col", "row"),
            P("col", "row"),
            P("col", "row"),
            P("row", "col"),
            P("col"),
            P("col", "row"),
            P("col", "row"),
            P("col", "row"),
            P("col"),
            P("row", "col"),
        ),
        out_specs=(
            P("col", ("dp", "row")),
            P(("dp", "row")),
            P("col", ("dp", "row")),
            P("col", ("dp", "row")),
            P("col"),
            P(("col", "dp"), "row"),
            P(("col", "dp"), "row"),
            P(("col", "dp"), "row"),
            P(("row", "dp"), "col"),
            P("col"),
            P(("col", "dp"), "row"),
            P(("col", "dp"), "row"),
            P(("col", "dp"), "row"),
            P(("row", "dp"), "col"),
            P("col"),
            P(("col", "dp"), "row"),
            P(("col", "dp"), "row"),
            P(("col", "dp"), "row"),
            P("col"),
            P(("dp", "row"), "col"),
        ),
        check_vma=False,
    )
```

time: 675 us -> 631 us (0.935)
  other arithmetic: 110 us -> 44.3 us
  blocking collectives: 50.1 us -> 0 us
  starting transfers between devices: 77.1 us -> 110 us
  Pallas kernels: 199 us -> 216 us
  between operations: 2.85 us -> 18.2 us
  local copies, waits for them, and re-layouts: 42.9 us -> 52.7 us
    ppermute x19 -> x16, waiting for transfers between devices: 162 us -> 92.7 us  [col(): return lax.ppermute(x, 'col', [(i, i ^ bit) for i in range(4)])]
    psum x1 -> x0, blocking collectives: 50.1 us -> none  [local(): packed = lax.psum(packed, ('dp', 'row', 'col'))]
    ppermute x12 -> x15, waiting for transfers between devices: 14.6 us -> 52.4 us  [rows(): return lax.ppermute(x, ('dp', 'row'), perm)]
    convert_element_type x26 -> x7, other arithmetic: 37.9 us -> 10.7 us  [the longest x4 7.18 us: plus(): return (a.astype(F32) + b.astype(F32)).astype(kind)]
    pallas_call x12 -> x24, Pallas kernels: 44.7 us -> 70.7 us  [the longest x2 16.9 us: weight_grads(): pl.pallas_call(body, out_shape=[jax.ShapeDtypeStruct((d, lanes), BF)] * 2...]
    unnamed x257 -> x272, local copies, waits for them, and re-layouts: 16.3 us -> 39.2 us
    ppermute x3 -> x9, starting transfers between devices: 7.89 us -> 27 us  [the longest x6 24.2 us: cols(): return lax.ppermute(x, ('dp', 'col'), perm)]
    ppermute x17 -> x19, starting transfers between devices: 4.2 us -> 22 us  [core(): return lax.ppermute(x, 'dp', [(i, i ^ 1) for i in range(self.dp)])]
  transfers between devices with their start and end apart: 57 -> 71, of which waited for: 19 -> 34; matrix products, arithmetic and copies ran while one was open for 19% -> 7% of each run, Pallas kernels for 18% -> 26%
where the time goes in v2:
time: 631 us; the launch traced here: 624 us
  Pallas kernels  216 us (34%)
  waiting for transfers between devices  183 us (29%)
  starting transfers between devices  110 us (17%)
  local copies, waits for them, and re-layouts  52.7 us (8%)
  other arithmetic  44.3 us (7%)
  between operations  18.2 us (3%)
    ppermute x16, waiting for transfers between devices, col(): return lax.ppermute(x, 'col', [(i, i ^ bit) for i in range(4)])  92.7 us
    ppermute x15, waiting for transfers between devices, rows(): return lax.ppermute(x, ('dp', 'row'), perm)  52.4 us
    unnamed x272, local copies, waits for them, and re-layouts  39.2 us
    pallas_call x2, Pallas kernels, vocab_forward(): pl.pallas_call(body, out_shape=(jax.ShapeDtypeStruct((chunks, width, step...  33.8 us
    pallas_call x2, Pallas kernels, attend_backward(): pl.pallas_call(body, out_shape=(jax.ShapeDtypeStruct((blocks, heads * HEA...  33.3 us
    pallas_call x2, Pallas kernels, vocab_hidden_grad(): pl.pallas_call(body, out_shape=(jax.ShapeDtypeStruct((chunks, width, step...  30.7 us
    ppermute x6, starting transfers between devices, cols(): return lax.ppermute(x, ('dp', 'col'), perm)  24.2 us
    ppermute x19, waiting for transfers between devices, core(): return lax.ppermute(x, 'dp', [(i, i ^ 1) for i in range(self.dp)])  23.1 us
  transfers between devices with their start and end apart: 71, of which 34 were waited for; matrix products, arithmetic and copies ran while one was open for 7% of the time, Pallas kernels for 26%

profile of v2, /device:TPU:0, one launch (start us, length us, event | category | flops | bytes accessed | tf_op | source)
XLA Modules:
  0.0 623.6 jit_solution(4506323380064575273)
XLA Ops:
  10.7 5.1 collective-permute-start.2
  29.3 14.6 %collective-permute-done = bf16[192,768]{1,0:T(8,128)(2,1)S(1)} collective-permute-done((bf16[192,768]{1,0:T(8,128)(2,1)S(1)}, bf16[192,768]{1,0:T(8,128)(2,1)S(1)}, u32[]{:S(2)}, u32[]{:S(2)}) %collective-permute-start) | collective-permute-done | bytes 294944 | tf_op jit(solution)/shard_map/ppermute | solution.py:695
  45.0 10.3 %collective-permute-done.5.two_ref = bf16[192,4096]{1,0:T(8,128)(2,1)S(1)} collective-permute-done((bf16[192,4096]{1,0:T(8,128)(2,1)S(1)}, bf16[192,4096]{1,0:T(8,128)(2,1)S(1)}, u32[]{:S(2)}, u32[]{:S(2)}) %collective-permute-start.5) | collective-permute-done | bytes 1572896 | tf_op jit(solution)/shard_map/ppermute | solution.py:714
  58.4 10.6 %collective-permute-done.7 = bf16[192,1152]{1,0:T(8,128)(2,1)S(1)} collective-permute-done((bf16[192,1152]{1,0:T(8,128)(2,1)S(1)}, bf16[192,1152]{1,0:T(8,128)(2,1)S(1)}, u32[]{:S(2)}, u32[]{:S(2)}) %collective-permute-start.7) | collective-permute-done | bytes 442400 | tf_op jit(solution)/shard_map/ppermute | solution.py:722
  72.9 7.9 %collective-permute-start.9 = (bf16[2,192,1152]{2,1,0:T(8,128)(2,1)}, bf16[2,192,1152]{2,1,0:T(8,128)(2,1)}, u32[]{:S(2)}, u32[]{:S(2)}) collective-permute-start(bf16[2,192,1152]{2,1,0:T(8,128)(2,1)} %pad_maximum_fusion.10), channel_id=1, source_target_pairs={{0,16},{16,0},{1,17},{17,1},{2,18},{18,2},{3,19},{19,3},{4,20},{20... | collective-permute-start | bytes 2654216 | tf_op jit(solution)/shard_map/ppermute | solution.py:692
  100.8 6.7 %collective-permute-done.10 = bf16[192,768]{1,0:T(8,128)(2,1)S(1)} collective-permute-done((bf16[192,768]{1,0:T(8,128)(2,1)}, bf16[192,768]{1,0:T(8,128)(2,1)S(1)}, u32[]{:S(2)}, u32[]{:S(2)}) %collective-permute-start.10) | collective-permute-done | bytes 294944 | tf_op jit(solution)/shard_map/ppermute | solution.py:695
  116.2 8.0 %shard_map.349 = (bf16[2,192,512]{2,1,0:T(8,128)(2,1)S(1)}, f32[6,1,512]{2,1,0:T(1,128)S(1)}) custom-call(s32[3]{0:T(128)S(1)} %pad_add_fusion.3.s_ref.refs_0_, bf16[2,576,1024]{2,1,0:T(8,128)(2,1)S(1)} %shard_map.348.q_ref.k_ref.v_ref, bf16[2,576,1024]{2,1,0:T(8,128)(2,1)S(1)} %shard_map.348.q_ref.k_ref.v_ref, ...), custom_call_target="tpu_custom_call" | custom-call | tf_op jit(solution)/shard_map/pallas_call | solution.py:69
  125.2 7.0 %collective-permute-start.16 = (f32[768,512]{1,0:T(8,128)S(1)}, f32[768,512]{1,0:T(8,128)S(1)}, u32[]{:S(2)}, u32[]{:S(2)}) collective-permute-start(f32[768,512]{1,0:T(8,128)S(1)} %shard_map.350.refs_1_), channel_id=1, source_target_pairs={{0,16},{16,0},{1,17},{17,1},{2,18},{18,2},{3,19},{19,3},{4,20},{20... | collective-permute-start | bytes 4718600 | tf_op jit(solution)/shard_map/ppermute | solution.py:692
  137.4 22.7 %collective-permute-done.19.refs_2_ = bf16[768,768]{1,0:T(8,128)(2,1)S(1)} collective-permute-done((bf16[768,768]{1,0:T(8,128)(2,1)S(1)}, bf16[768,768]{1,0:T(8,128)(2,1)S(1)}, u32[]{:S(2)}, u32[]{:S(2)}) %collective-permute-start.19) | collective-permute-done | bytes 1179680 | tf_op jit(solution)/shard_map/ppermute | solution.py:714
  169.1 13.5 %shard_map.354 = (bf16[2,192,512]{2,1,0:T(8,128)(2,1)S(1)}, f32[6,1,512]{2,1,0:T(1,128)S(1)}) custom-call(s32[3]{0:T(128)S(1)} %pad_add_fusion.3.s_ref.refs_0_, bf16[2,192,512]{2,1,0:T(8,128)(2,1)S(1)} %shard_map.352.q_ref, bf16[2,384,2048]{2,1,0:T(8,128)(2,1)S(1)} %shard_map.353.k_ref.v_ref, bf16[2,384,2048]{2,1,0:T(8,128)(2,1)S(1)} %shard_map.353.k_ref.v_ref), custom_call_target="tpu_custom_call" | custom-call | tf_op jit(solution)/shard_map/pallas_call | solution.py:69
  189.2 6.5 %shard_map.357 = (bf16[512,512]{1,0:T(8,128)(2,1)S(1)}, bf16[512,512]{1,0:T(8,128)(2,1)S(1)}, bf16[512,512]{1,0:T(8,128)(2,1)S(1)}, bf16[512,512]{1,0:T(8,128)(2,1)S(1)}, f32[768,512]{1,0:T(8,128)}) custom-call(bf16[768,768]{1,0:T(8,128)(2,1)S(1)} %pad_maximum_fusion.9.refs_0_, bf16[768,768]{1,0:T(8,128)(2,1)S(1)} %collective-permute-done.18.refs_1_, ...), custom_call_target="tpu_custom_call" | custom-call | tf_op jit(solution)/shard_map/pallas_call | solution.py:171
  209.3 18.8 %collective-permute-done.24 = bf16[768,256]{1,0:T(8,128)(2,1)S(1)} collective-permute-done((bf16[768,256]{1,0:T(8,128)(2,1)S(1)}, bf16[768,256]{1,0:T(8,128)(2,1)S(1)}, u32[]{:S(2)}, u32[]{:S(2)}) %collective-permute-start.24) | collective-permute-done | bytes 393248 | tf_op jit(solution)/shard_map/ppermute | solution.py:695
  230.7 16.9 %shard_map.359 = (bf16[4,4096,256]{2,1,0:T(8,128)(2,1)}, f32[8,4,256]{2,1,0:T(4,128)S(1)}, f32[3,4,256]{2,1,0:T(4,128)S(1)}) custom-call(s32[2]{0:T(128)S(1)} %pad_add_fusion.s_ref, bf16[2,768,256]{2,1,0:T(8,128)(2,1)S(1)} %pad_maximum_fusion.13.h0_ref.refs_1_, bf16[2,768,256]{2,1,0:T(8,128)(2,1)} %collective-permute-done.27.h1_ref.refs_2_, ...), custom_call_target="tpu_custom_call" | custom-call | tf_op jit(solution)/shard_map/pallas_call | solution.py:516
  250.9 16.9 %shard_map.360 = (bf16[4,4096,256]{2,1,0:T(8,128)(2,1)}, f32[8,4,256]{2,1,0:T(4,128)S(1)}, f32[3,4,256]{2,1,0:T(4,128)S(1)}) custom-call(s32[2]{0:T(128)S(1)} %pad_add_fusion.s_ref, bf16[2,768,256]{2,1,0:T(8,128)(2,1)} %collective-permute-done.26.h0_ref.refs_3_, bf16[2,768,256]{2,1,0:T(8,128)(2,1)S(1)} %collective-permute-done.28.h1_ref.refs_4_, ...), custom_call_target="tpu_custom_call" | custom-call | tf_op jit(solution)/shard_map/pallas_call | solution.py:516
  280.7 15.3 %shard_map.363 = (bf16[4,4096,256]{2,1,0:T(8,128)(2,1)}, bf16[2,768,256]{2,1,0:T(8,128)(2,1)}, bf16[2,768,256]{2,1,0:T(8,128)(2,1)}) custom-call(s32[2]{0:T(128)} %copy-done.86, bf16[4,4096,256]{2,1,0:T(8,128)(2,1)} %get-tuple-element.252.e_ref, f32[8,4,256]{2,1,0:T(4,128)} %copy-done.80, f32[8,256]{1,0:T(8,128)} %copy-done.81, ...), custom_call_target="tpu_custom_call", output_to_operand_aliasing={{0}: (1, {})} | custom-call | tf_op jit(solution)/shard_map/pallas_call | solution.py:570
  299.9 15.3 %shard_map.364 = (bf16[4,4096,256]{2,1,0:T(8,128)(2,1)}, bf16[2,768,256]{2,1,0:T(8,128)(2,1)}, bf16[2,768,256]{2,1,0:T(8,128)(2,1)}) custom-call(s32[2]{0:T(128)} %copy-done.86, bf16[4,4096,256]{2,1,0:T(8,128)(2,1)} %get-tuple-element.258.e_ref, f32[8,4,256]{2,1,0:T(4,128)} %copy-done.79, f32[8,256]{1,0:T(8,128)} %copy-done.81, ...), custom_call_target="tpu_custom_call", output_to_operand_aliasing={{0}: (1, {})} | custom-call | tf_op jit(solution)/shard_map/pallas_call | solution.py:570
  317.8 17.5 %collective-permute-done.37 = bf16[2,768,256]{2,1,0:T(8,128)(2,1)S(1)} collective-permute-done((bf16[2,768,256]{2,1,0:T(8,128)(2,1)S(1)}, bf16[2,768,256]{2,1,0:T(8,128)(2,1)S(1)}, u32[]{:S(2)}, u32[]{:S(2)}) %collective-permute-start.37) | collective-permute-done | bytes 786464 | tf_op jit(solution)/shard_map/ppermute | solution.py:695
  342.6 18.3 %shard_map.365 = bf16[768,4096]{1,0:T(8,128)(2,1)} custom-call(s32[8]{0:T(128)S(1)} %copy-done.92, bf16[2,768,256]{2,1,0:T(8,128)(2,1)S(1)} %pad_maximum_fusion.13.h0_ref.refs_1_, bf16[2,768,256]{2,1,0:T(8,128)(2,1)} %collective-permute-done.27.h1_ref.refs_2_, bf16[2,768,256]{2,1,0:T(8,128)(2,1)} %collective-permute-done.26.h0_ref.refs_3_, ...), custom_call_target="tpu_custom_call" | custom-call | tf_op jit(solution)/shard_map/pallas_call | solution.py:616
  369.3 12.7 %shard_map.367 = (bf16[4,768,768]{2,1,0:T(8,128)(2,1)}, f32[768,512]{1,0:T(8,128)}) custom-call(s32[4]{0:T(128)} %get-tuple-element.246.s_ref, bf16[768,768]{1,0:T(8,128)(2,1)} %copy-done.10, bf16[768,768]{1,0:T(8,128)(2,1)} %copy-done.22, bf16[768,768]{1,0:T(8,128)(2,1)} %copy-done.98, bf16[768,768]{1,0:T(8,128)(2,1)} %collective-permute-done.21.refs_3_, ...), custom_call_target="tpu_custom_call" | custom-call | tf_op jit(solution)/shard_map/pallas_call | solution.py:203
  395.0 21.1 %shard_map.370 = (bf16[2,192,512]{2,1,0:T(8,128)(2,1)S(1)}, bf16[2,192,2048]{2,1,0:T(8,128)(2,1)S(1)}, bf16[2,192,2048]{2,1,0:T(8,128)(2,1)S(1)}) custom-call(s32[3]{0:T(128)S(1)} %pad_add_fusion.3.s_ref.refs_0_, bf16[2,192,512]{2,1,0:T(8,128)(2,1)S(1)} %copy-done.32, bf16[2,384,2048]{2,1,0:T(8,128)(2,1)} %copy-done.2, bf16[2,384,2048]{2,1,0:T(8,128)(2,1)} %copy-done.2, ...), custom_call_target="tpu_custom_call" | custom-call | tf_op jit(solution)/shard_map/pallas_call | solution.py:113
  435.2 10.4 %shard_map.374 = (bf16[768,768]{1,0:T(8,128)(2,1)}, bf16[768,768]{1,0:T(8,128)(2,1)}) custom-call(s32[3]{0:T(128)S(1)} %pad_add_fusion.3.s_ref.refs_0_, bf16[768,512]{1,0:T(8,128)(2,1)S(1)} %copy-done.36, bf16[768,2048]{1,0:T(8,128)(2,1)} %copy-done.6, bf16[768,2048]{1,0:T(8,128)(2,1)} %copy-done.6, bf16[768,512]{1,0:T(8,128)(2,1)S(1)} %get-tuple-element.272.x_ref.refs_4_, ...), custom_call_target="tpu_custom_call" | custom-call | tf_op jit(solution)/shard_map/pallas_call | solution.py:379
  458.8 7.4 %collective-permute-start.46 = (bf16[192,2048]{1,0:T(8,128)(2,1)}, bf16[192,2048]{1,0:T(8,128)(2,1)}, u32[]{:S(2)}, u32[]{:S(2)}) collective-permute-start(bf16[192,2048]{1,0:T(8,128)(2,1)} %get-tuple-element.359), channel_id=1, source_target_pairs={{0,0},{1,1},{16,2},{17,3},{2,16},{3,17},{18,18},{19,19},{4,4},{5,5... | collective-permute-start | bytes 2359304 | tf_op jit(solution)/shard_map/ppermute | solution.py:722
  469.0 12.2 %shard_map.376 = (bf16[2,192,512]{2,1,0:T(8,128)(2,1)S(1)}, bf16[2,192,1024]{2,1,0:T(8,128)(2,1)S(1)}, bf16[2,192,1024]{2,1,0:T(8,128)(2,1)S(1)}) custom-call(s32[3]{0:T(128)S(1)} %pad_add_fusion.3.s_ref.refs_0_, bf16[2,576,1024]{2,1,0:T(8,128)(2,1)S(1)} %shard_map.348.q_ref.k_ref.v_ref, bf16[2,576,1024]{2,1,0:T(8,128)(2,1)S(1)} %shard_map.348.q_ref.k_ref.v_ref, ...), custom_call_target="tpu_custom_call" | custom-call | tf_op jit(solution)/shard_map/pallas_call | solution.py:113
  487.1 6.6 %shard_map.377 = (bf16[768,768]{1,0:T(8,128)(2,1)S(1)}, bf16[768,768]{1,0:T(8,128)(2,1)}) custom-call(s32[3]{0:T(128)S(1)} %pad_add_fusion.3.s_ref.refs_0_, bf16[768,1024]{1,0:T(8,128)(2,1)} %copy-done.9, bf16[768,1024]{1,0:T(8,128)(2,1)} %copy-done.9, bf16[768,1024]{1,0:T(8,128)(2,1)} %copy-done.9, bf16[768,512]{1,0:T(8,128)(2,1)S(1)} %copy-done.41, ...), custom_call_target="tpu_custom_call" | custom-call | tf_op jit(solution)/shard_map/pallas_call | solution.py:379
  496.4 8.6 %collective-permute-done.43.refs_1_ = bf16[768,768]{1,0:T(8,128)(2,1)} collective-permute-done((bf16[768,768]{1,0:T(8,128)(2,1)}, bf16[768,768]{1,0:T(8,128)(2,1)}, u32[]{:S(2)}, u32[]{:S(2)}) %collective-permute-start.43) | collective-permute-done | bytes 1179680 | tf_op jit(solution)/shard_map/ppermute | solution.py:714
  522.0 6.8 %collective-permute-done.55 = bf16[192,768]{1,0:T(8,128)(2,1)S(1)} collective-permute-done((bf16[192,768]{1,0:T(8,128)(2,1)S(1)}, bf16[192,768]{1,0:T(8,128)(2,1)S(1)}, u32[]{:S(2)}, u32[]{:S(2)}) %collective-permute-start.55) | collective-permute-done | bytes 294944 | tf_op jit(solution)/shard_map/ppermute | solution.py:695
  530.1 6.0 collective-permute-done.54
  537.3 12.5 %collective-permute-done.53 = bf16[192,768]{1,0:T(8,128)(2,1)S(1)} collective-permute-done((bf16[192,768]{1,0:T(8,128)(2,1)S(1)}, bf16[192,768]{1,0:T(8,128)(2,1)S(1)}, u32[]{:S(2)}, u32[]{:S(2)}) %collective-permute-start.53) | collective-permute-done | bytes 294944 | tf_op jit(solution)/shard_map/ppermute | solution.py:695
  554.9 5.0 collective-permute-start.49
  562.7 5.5 collective-permute-done.56.refs_1_
  570.1 14.6 %collective-permute-start.63 = (bf16[192,768]{1,0:T(8,128)(2,1)S(1)}, bf16[192,768]{1,0:T(8,128)(2,1)S(1)}, u32[]{:S(2)}, u32[]{:S(2)}) collective-permute-start(bf16[192,768]{1,0:T(8,128)(2,1)S(1)} %get-tuple-element.330), channel_id=1, source_target_pairs={{0,2},{1,3},{2,0},{3,1},{4,6},{5,7},{6,4},{7,5},{8,10},{9,11},{10,... | collective-permute-start | bytes 884744 | tf_op jit(solution)/shard_map/ppermute | solution.py:702
  584.6 5.5 collective-permute-start.64
  (523 shorter events, 238.5 us)
Async XLA Ops:
  7.2 476.6 %reduce-scatter.3.cloned.1.call-start = ((), (), s32[]{:S(2)}) async-start(), calls=%async_computation.2 | async-start | bytes 5898240 | tf_op jit(solution)/shard_map/reduce_scatter | solution.py:987
  18.2 37.1 %collective-permute-start.5 = (bf16[192,4096]{1,0:T(8,128)(2,1)S(1)}, bf16[192,4096]{1,0:T(8,128)(2,1)S(1)}, u32[]{:S(2)}, u32[]{:S(2)}) collective-permute-start(bf16[192,4096]{1,0:T(8,128)(2,1)S(1)} %fusion.own_ref), channel_id=1, source_target_pairs={{0,8},{4,12},{8,0},{12,4},{16,20},{20,16},{24,28},{28,24},{1,9},{5... | collective-permute-start | bytes 4718600 | tf_op jit(solution)/shard_map/ppermute | solution.py:714
  19.8 35.6 %collective-permute-start.4 = (bf16[192,4096]{1,0:T(8,128)(2,1)S(1)}, bf16[192,4096]{1,0:T(8,128)(2,1)}, u32[]{:S(2)}, u32[]{:S(2)}) collective-permute-start(bf16[192,4096]{1,0:T(8,128)(2,1)S(1)} %fusion.own_ref), channel_id=1, source_target_pairs={{0,4},{4,0},{8,12},{12,8},{16,24},{20,28},{24,16},{28,20},{1,5},{5... | collective-permute-start | bytes 4718600 | tf_op jit(solution)/shard_map/ppermute | solution.py:714
  81.7 19.1 %collective-permute-start.11 = (bf16[192,768]{1,0:T(8,128)(2,1)}, bf16[192,768]{1,0:T(8,128)(2,1)S(1)}, u32[]{:S(2)}, u32[]{:S(2)}) collective-permute-start(bf16[192,768]{1,0:T(8,128)(2,1)} %maximum_select_fusion.2), channel_id=1, source_target_pairs={{0,1},{1,0},{2,3},{3,2},{4,5},{5,4},{6,7},{7,6},{8,9},{9,8},{10,11... | collective-permute-start | bytes 884744 | tf_op jit(solution)/shard_map/ppermute | solution.py:695
  81.7 25.8 %collective-permute-start.10 = (bf16[192,768]{1,0:T(8,128)(2,1)}, bf16[192,768]{1,0:T(8,128)(2,1)S(1)}, u32[]{:S(2)}, u32[]{:S(2)}) collective-permute-start(bf16[192,768]{1,0:T(8,128)(2,1)} %maximum_select_fusion.2), channel_id=1, source_target_pairs={{0,2},{1,3},{2,0},{3,1},{4,6},{5,7},{6,4},{7,5},{8,10},{9,11},{10,... | collective-permute-start | bytes 884744 | tf_op jit(solution)/shard_map/ppermute | solution.py:695
  85.3 25.6 %collective-permute-start.13 = (bf16[768,768]{1,0:T(8,128)(2,1)S(1)}, bf16[768,768]{1,0:T(8,128)(2,1)S(1)}, u32[]{:S(2)}, u32[]{:S(2)}) collective-permute-start(bf16[768,768]{1,0:T(8,128)(2,1)S(1)} %copy-done.97), channel_id=1, source_target_pairs={{0,24},{4,28},{8,16},{12,20},{16,4},{20,0},{24,12},{28,8},{1,25},{... | collective-permute-start | bytes 3538952 | tf_op jit(solution)/shard_map/ppermute | solution.py:714
  87.0 26.6 %collective-permute-start.14 = (bf16[768,768]{1,0:T(8,128)(2,1)S(1)}, bf16[768,768]{1,0:T(8,128)(2,1)S(1)}, u32[]{:S(2)}, u32[]{:S(2)}) collective-permute-start(bf16[768,768]{1,0:T(8,128)(2,1)S(1)} %copy-done.108), channel_id=1, source_target_pairs={{0,24},{4,28},{8,16},{12,20},{16,4},{20,0},{24,12},{28,8},{1,25},{... | collective-permute-start | bytes 3538952 | tf_op jit(solution)/shard_map/ppermute | solution.py:714
  132.2 27.9 %collective-permute-start.19 = (bf16[768,768]{1,0:T(8,128)(2,1)S(1)}, bf16[768,768]{1,0:T(8,128)(2,1)S(1)}, u32[]{:S(2)}, u32[]{:S(2)}) collective-permute-start(bf16[768,768]{1,0:T(8,128)(2,1)S(1)} %pad_maximum_fusion.9.refs_0_), channel_id=1, source_target_pairs={{0,8},{4,12},{8,0},{12,4},{16,20},{20,16},{24,28},{28,24},{1,9},{5... | collective-permute-start | bytes 3538952 | tf_op jit(solution)/shard_map/ppermute | solution.py:714
  132.7 27.5 %collective-permute-start.18 = (bf16[768,768]{1,0:T(8,128)(2,1)S(1)}, bf16[768,768]{1,0:T(8,128)(2,1)S(1)}, u32[]{:S(2)}, u32[]{:S(2)}) collective-permute-start(bf16[768,768]{1,0:T(8,128)(2,1)S(1)} %pad_maximum_fusion.9.refs_0_), channel_id=1, source_target_pairs={{0,4},{4,0},{8,12},{12,8},{16,24},{20,28},{24,16},{28,20},{1,5},{5... | collective-permute-start | bytes 3538952 | tf_op jit(solution)/shard_map/ppermute | solution.py:714
  132.7 27.4 %collective-permute-start.17 = (bf16[192,2048]{1,0:T(8,128)(2,1)}, bf16[192,2048]{1,0:T(8,128)(2,1)S(1)}, u32[]{:S(2)}, u32[]{:S(2)}) collective-permute-start(bf16[192,2048]{1,0:T(8,128)(2,1)} %param.21), channel_id=1, source_target_pairs={{0,1},{1,0},{2,17},{3,16},{16,3},{17,2},{18,19},{19,18},{4,5},{5,4... | collective-permute-start | bytes 2359304 | tf_op jit(solution)/shard_map/ppermute | solution.py:722
  161.1 21.5 %collective-permute-start.21 = (bf16[768,768]{1,0:T(8,128)(2,1)S(1)}, bf16[768,768]{1,0:T(8,128)(2,1)}, u32[]{:S(2)}, u32[]{:S(2)}) collective-permute-start(bf16[768,768]{1,0:T(8,128)(2,1)S(1)} %collective-permute-done.18.refs_1_), channel_id=1, source_target_pairs={{0,8},{4,12},{8,0},{12,4},{16,20},{20,16},{24,28},{28,24},{1,9},{5... | collective-permute-start | bytes 3538952 | tf_op jit(solution)/shard_map/ppermute | solution.py:714
  199.1 29.2 %collective-permute-start.25 = (bf16[192,4096]{1,0:T(8,128)(2,1)}, bf16[192,4096]{1,0:T(8,128)(2,1)}, u32[]{:S(2)}, u32[]{:S(2)}) collective-permute-start(bf16[192,4096]{1,0:T(8,128)(2,1)} %collective-permute-done.4.one_ref), channel_id=1, source_target_pairs={{0,8},{4,12},{8,0},{12,4},{16,20},{20,16},{24,28},{28,24},{1,9},{5... | collective-permute-start | bytes 4718600 | tf_op jit(solution)/shard_map/ppermute | solution.py:714
  208.9 19.2 %collective-permute-start.24 = (bf16[768,256]{1,0:T(8,128)(2,1)S(1)}, bf16[768,256]{1,0:T(8,128)(2,1)S(1)}, u32[]{:S(2)}, u32[]{:S(2)}) collective-permute-start(bf16[768,256]{1,0:T(8,128)(2,1)S(1)} %get-tuple-element.415), channel_id=1, source_target_pairs={{0,2},{1,3},{2,0},{3,1},{4,6},{5,7},{6,4},{7,5},{8,10},{9,11},{10,... | collective-permute-start | bytes 1179656 | tf_op jit(solution)/shard_map/ppermute | solution.py:695
  228.3 20.0 %collective-permute-start.26 = (bf16[2,768,256]{2,1,0:T(8,128)(2,1)S(1)}, bf16[2,768,256]{2,1,0:T(8,128)(2,1)}, u32[]{:S(2)}, u32[]{:S(2)}) collective-permute-start(bf16[2,768,256]{2,1,0:T(8,128)(2,1)S(1)} %pad_maximum_fusion.13.h0_ref.refs_1_), channel_id=1, source_target_pairs={{0,1},{1,0},{2,3},{3,2},{4,5},{5,4},{6,7},{7,6},{8,9},{9,8},{10,11... | collective-permute-start | bytes 2359304 | tf_op jit(solution)/shard_map/ppermute | solution.py:695
  248.4 19.4 %collective-permute-start.30 = (bf16[192,512]{1,0:T(8,128)(2,1)S(1)}, bf16[192,512]{1,0:T(8,128)(2,1)S(1)}, u32[]{:S(2)}, u32[]{:S(2)}) collective-permute-start(bf16[192,512]{1,0:T(8,128)(2,1)S(1)} %get-tuple-element.394), channel_id=1, source_target_pairs={{1,0},{0,1},{17,2},{16,3},{3,16},{2,17},{19,18},{18,19},{5,4},{4,5... | collective-permute-start | bytes 589832 | tf_op jit(solution)/shard_map/ppermute | solution.py:722
  315.5 19.8 %collective-permute-start.37 = (bf16[2,768,256]{2,1,0:T(8,128)(2,1)S(1)}, bf16[2,768,256]{2,1,0:T(8,128)(2,1)S(1)}, u32[]{:S(2)}, u32[]{:S(2)}) collective-permute-start(bf16[2,768,256]{2,1,0:T(8,128)(2,1)S(1)} %add_convert_fusion.2), channel_id=1, source_target_pairs={{0,1},{1,0},{2,3},{3,2},{4,5},{5,4},{6,7},{7,6},{8,9},{9,8},{10,11... | collective-permute-start | bytes 2359304 | tf_op jit(solution)/shard_map/ppermute | solution.py:695
  339.7 21.2 %collective-permute-start.38 = (bf16[768,256]{1,0:T(8,128)(2,1)}, bf16[768,256]{1,0:T(8,128)(2,1)}, u32[]{:S(2)}, u32[]{:S(2)}) collective-permute-start(bf16[768,256]{1,0:T(8,128)(2,1)} %fusion.9), channel_id=1, source_target_pairs={{0,2},{1,3},{2,0},{3,1},{4,6},{5,7},{6,4},{7,5},{8,10},{9,11},{10,... | collective-permute-start | bytes 1179656 | tf_op jit(solution)/shard_map/ppermute | solution.py:695
  382.0 222.4 %reduce-scatter.5.cloned.1.call-start = ((), (), s32[]{:S(2)}) async-start(), calls=%async_computation.3 | async-start | bytes 7864320 | tf_op jit(solution)/shard_map/reduce_scatter | solution.py:974
  445.6 59.4 %collective-permute-start.45 = (bf16[768,768]{1,0:T(8,128)(2,1)}, bf16[768,768]{1,0:T(8,128)(2,1)}, u32[]{:S(2)}, u32[]{:S(2)}) collective-permute-start(bf16[768,768]{1,0:T(8,128)(2,1)} %get-tuple-element.300), channel_id=1, source_target_pairs={{16,24},{20,28},{24,16},{28,20},{17,25},{21,29},{25,17},{29,21},{1... | collective-permute-start | bytes 3538952 | tf_op jit(solution)/shard_map/ppermute | solution.py:714
  447.3 57.8 %collective-permute-start.44 = (bf16[768,768]{1,0:T(8,128)(2,1)}, bf16[768,768]{1,0:T(8,128)(2,1)}, u32[]{:S(2)}, u32[]{:S(2)}) collective-permute-start(bf16[768,768]{1,0:T(8,128)(2,1)} %get-tuple-element.300), channel_id=1, source_target_pairs={{0,28},{4,24},{8,20},{12,16},{1,29},{5,25},{9,21},{13,17},{2,30},{... | collective-permute-start | bytes 3538952 | tf_op jit(solution)/shard_map/ppermute | solution.py:714
  451.6 53.4 %collective-permute-start.43 = (bf16[768,768]{1,0:T(8,128)(2,1)}, bf16[768,768]{1,0:T(8,128)(2,1)}, u32[]{:S(2)}, u32[]{:S(2)}) collective-permute-start(bf16[768,768]{1,0:T(8,128)(2,1)} %get-tuple-element.299.refs_0_), channel_id=1, source_target_pairs={{0,20},{4,16},{8,28},{12,24},{1,21},{5,17},{9,29},{13,25},{2,22},{... | collective-permute-start | bytes 3538952 | tf_op jit(solution)/shard_map/ppermute | solution.py:714
  458.0 55.2 %collective-permute-start.47 = (bf16[192,2048]{1,0:T(8,128)(2,1)}, bf16[192,2048]{1,0:T(8,128)(2,1)}, u32[]{:S(2)}, u32[]{:S(2)}) collective-permute-start(bf16[192,2048]{1,0:T(8,128)(2,1)} %get-tuple-element.358), channel_id=1, source_target_pairs={{1,0},{0,1},{17,2},{16,3},{3,16},{2,17},{19,18},{18,19},{5,4},{4,5... | collective-permute-start | bytes 2359304 | tf_op jit(solution)/shard_map/ppermute | solution.py:722
  458.8 54.4 %collective-permute-start.46 = (bf16[192,2048]{1,0:T(8,128)(2,1)}, bf16[192,2048]{1,0:T(8,128)(2,1)}, u32[]{:S(2)}, u32[]{:S(2)}) collective-permute-start(bf16[192,2048]{1,0:T(8,128)(2,1)} %get-tuple-element.359), channel_id=1, source_target_pairs={{0,0},{1,1},{16,2},{17,3},{2,16},{3,17},{18,18},{19,19},{4,4},{5,5... | collective-permute-start | bytes 2359304 | tf_op jit(solution)/shard_map/ppermute | solution.py:722
  513.6 39.4 %collective-permute-start.48 = (bf16[2,192,1152]{2,1,0:T(8,128)(2,1)S(1)}, bf16[2,192,1152]{2,1,0:T(8,128)(2,1)S(1)}, u32[]{:S(2)}, u32[]{:S(2)}) collective-permute-start(bf16[2,192,1152]{2,1,0:T(8,128)(2,1)S(1)} %get-tuple-element.373), channel_id=1, source_target_pairs={{0,16},{16,0},{1,17},{17,1},{2,18},{18,2},{3,19},{19,3},{4,20},{20... | collective-permute-start | bytes 2654216 | tf_op jit(solution)/shard_map/ppermute | solution.py:692
  520.2 29.6 %collective-permute-start.53 = (bf16[192,768]{1,0:T(8,128)(2,1)S(1)}, bf16[192,768]{1,0:T(8,128)(2,1)S(1)}, u32[]{:S(2)}, u32[]{:S(2)}) collective-permute-start(bf16[192,768]{1,0:T(8,128)(2,1)S(1)} %get-tuple-element.386), channel_id=1, source_target_pairs={{0,2},{1,3},{2,0},{3,1},{4,6},{5,7},{6,4},{7,5},{8,10},{9,11},{10,... | collective-permute-start | bytes 884744 | tf_op jit(solution)/shard_map/ppermute | solution.py:695
  521.3 31.0 %collective-permute-start.50 = (bf16[192,768]{1,0:T(8,128)(2,1)S(1)}, bf16[192,768]{1,0:T(8,128)(2,1)S(1)}, u32[]{:S(2)}, u32[]{:S(2)}) collective-permute-start(bf16[192,768]{1,0:T(8,128)(2,1)S(1)} %get-tuple-element.316), channel_id=1, source_target_pairs={{16,18},{17,19},{18,16},{19,17},{20,22},{21,23},{22,20},{23,21},{2... | collective-permute-start | bytes 884744 | tf_op jit(solution)/shard_map/ppermute | solution.py:702
  528.8 33.9 %collective-permute-start.57 = (bf16[768,768]{1,0:T(8,128)(2,1)S(1)}, bf16[768,768]{1,0:T(8,128)(2,1)S(1)}, u32[]{:S(2)}, u32[]{:S(2)}) collective-permute-start(bf16[768,768]{1,0:T(8,128)(2,1)S(1)} %get-tuple-element.322.refs_0_), channel_id=1, source_target_pairs={{16,8},{20,12},{24,0},{28,4},{17,9},{21,13},{25,1},{29,5},{18,10},... | collective-permute-start | bytes 3538952 | tf_op jit(solution)/shard_map/ppermute | solution.py:714
  536.0 26.7 %collective-permute-start.58 = (bf16[768,768]{1,0:T(8,128)(2,1)}, bf16[768,768]{1,0:T(8,128)(2,1)S(1)}, u32[]{:S(2)}, u32[]{:S(2)}) collective-permute-start(bf16[768,768]{1,0:T(8,128)(2,1)} %get-tuple-element.320), channel_id=1, source_target_pairs={{16,12},{20,8},{24,4},{28,0},{17,13},{21,9},{25,5},{29,1},{18,14},... | collective-permute-start | bytes 3538952 | tf_op jit(solution)/shard_map/ppermute | solution.py:714
  549.8 18.4 %collective-permute-start.56 = (bf16[768,768]{1,0:T(8,128)(2,1)}, bf16[768,768]{1,0:T(8,128)(2,1)}, u32[]{:S(2)}, u32[]{:S(2)}) collective-permute-start(bf16[768,768]{1,0:T(8,128)(2,1)} %get-tuple-element.320), channel_id=1, source_target_pairs={{0,4},{4,0},{8,12},{12,8},{1,5},{5,1},{9,13},{13,9},{2,6},{6,2},{1... | collective-permute-start | bytes 3538952 | tf_op jit(solution)/shard_map/ppermute | solution.py:714
  560.6 31.6 %collective-permute-start.59 = (bf16[192,1152]{1,0:T(8,128)(2,1)}, bf16[192,1152]{1,0:T(8,128)(2,1)}, u32[]{:S(2)}, u32[]{:S(2)}) collective-permute-start(bf16[192,1152]{1,0:T(8,128)(2,1)} %get-tuple-element.371), channel_id=1, source_target_pairs={{1,0},{0,1},{17,2},{16,3},{3,16},{2,17},{19,18},{18,19},{5,4},{4,5... | collective-permute-start | bytes 1327112 | tf_op jit(solution)/shard_map/ppermute | solution.py:722
  570.1 33.7 %collective-permute-start.63 = (bf16[192,768]{1,0:T(8,128)(2,1)S(1)}, bf16[192,768]{1,0:T(8,128)(2,1)S(1)}, u32[]{:S(2)}, u32[]{:S(2)}) collective-permute-start(bf16[192,768]{1,0:T(8,128)(2,1)S(1)} %get-tuple-element.330), channel_id=1, source_target_pairs={{0,2},{1,3},{2,0},{3,1},{4,6},{5,7},{6,4},{7,5},{8,10},{9,11},{10,... | collective-permute-start | bytes 884744 | tf_op jit(solution)/shard_map/ppermute | solution.py:702
  584.6 19.1 %collective-permute-start.64 = (bf16[192,768]{1,0:T(8,128)(2,1)S(1)}, bf16[192,768]{1,0:T(8,128)(2,1)S(1)}, u32[]{:S(2)}, u32[]{:S(2)}) collective-permute-start(bf16[192,768]{1,0:T(8,128)(2,1)S(1)} %get-tuple-element.331), channel_id=1, source_target_pairs={{0,1},{1,0},{2,3},{3,2},{4,5},{5,4},{6,7},{7,6},{8,9},{9,8},{10,11... | collective-permute-start | bytes 884744 | tf_op jit(solution)/shard_map/ppermute | solution.py:702
  (174 other events, 2013.6 us)
Sparse Core Ops, SparseCore 0:
  382.1 54.3 reduce-scatter.2
  439.5 95.1 reduce-scatter.4

commit v3 on v2

--- a/solution.py
+++ b/solution.py
@@ -181,6 +181,7 @@
     wide = lanes // 3
     tokens = normed.shape[1]
     n = len(packs)
+    size = d // 4
 
     def body(s_ref, *refs):
         w_refs, save_refs = refs[:n], refs[n : 2 * n]
@@ -195,8 +196,10 @@
             )
             first = nt(x_ref[...], grads).astype(BF)
             second = nt(g_ref[...], hidden).astype(BF)
-            dw_ref[s_ref[b], :, : 2 * wide] = first
-            dw_ref[s_ref[b], :, 2 * wide :] = second
+            for p in range(4):
+                at = pl.ds(pl.multiple_of(s_ref[4 + p] * size, size), size)
+                dw_ref[s_ref[b], at, : 2 * wide] = first[p * size : (p + 1) * size]
+                dw_ref[s_ref[b], at, 2 * wide :] = second[p * size : (p + 1) * size]
             part = nn(w_ref[:, : 2 * wide], grads)
             out_ref[...] = part if b == 0 else out_ref[...] + part
 
@@ -822,18 +825,6 @@
     def swap_bits(n):
         return n // 2 + 2 * (n % 2)
 
-    other_targets = move.core(targets)
-    near, far = pick(mine, targets, other_targets), pick(mine, other_targets, targets)
-
-    def target_chunks(lo):
-        out = []
-        for which in (core, 1 - core):
-            for seq_targets in (near, far):
-                out.append(lax.dynamic_slice_in_dim(seq_targets, lo * tq + which * tc, tc, 0))
-        wanted = jnp.stack(out) - col * vocab
-        return jnp.where((wanted >= 0) & (wanted < vocab), wanted - core * width, -1)
-
-    want_near, want_far = target_chunks(half), target_chunks(1 - half)
     valid = jnp.where(first_core, width, vocab - width)
     vocab_scalars = jnp.stack([valid, core]).astype(jnp.int32)
     chip = jnp.where(mine, 0, 1)
@@ -842,7 +833,9 @@
         for h in range(2):
             spots.append((half ^ lo) * 4 + (core ^ h) * 2 + chip)
     spots = jnp.stack(spots).astype(jnp.int32)
-    own_places = jnp.stack([row, row ^ (1 + core), row ^ (2 - core), row ^ 3]).astype(jnp.int32)
+    own_places = [row, row ^ (1 + core), row ^ (2 - core), row ^ 3]
+    own_places += [col ^ swap_bits(p) for p in range(4)]
+    own_places = jnp.stack(own_places).astype(jnp.int32)
     places = []
     for unit in range(8):
         e = 2 * (row ^ (unit // 2)) + unit % 2
@@ -872,15 +865,30 @@
     sc_got = [move.col(sc_own, bit) for bit in (2, 1, 3)]
     table_one = move.rows(table_own, STEP_ONE)
     table_two = move.rows(table_own, SAME_TWO)
-    sc, x_in, ff_own, want_near, want_far, spots, places, own_places, table_one, table_two = tie(
-        jnp.concatenate([sc_own, *sc_got]), x_in, ff_own, want_near, want_far, spots, places, own_places, table_one, table_two
-    )
+    sc, x_in, ff_own, targets, spots, places, own_places = tie(
+        jnp.concatenate([sc_own, *sc_got]), x_in, ff_own, targets, spots, places, own_places
+    )
+    other_targets = move.core(targets)
+    near, far = pick(mine, targets, other_targets), pick(mine, other_targets, targets)
+
+    def target_chunks(lo):
+        out = []
+        for which in (core, 1 - core):
+            for seq_targets in (near, far):
+                out.append(lax.dynamic_slice_in_dim(seq_targets, lo * tq + which * tc, tc, 0))
+        wanted = jnp.stack(out) - col * vocab
+        return jnp.where((wanted >= 0) & (wanted < vocab), wanted - core * width, -1)
+
+    want_near, want_far = target_chunks(half), target_chunks(1 - half)
     sc_row = move.rows(sc, STEP_ONE)
     x_got = [move.spread(x_in, 0), move.spread(x_in, 1)]
-    x_near, x_far, sc_row, sc, ff_own = tie(*x_got, sc_row, sc, ff_own)
+    x_near, x_far, sc_row, sc, ff_own, table_one, table_two, enc_in = tie(
+        *x_got, sc_row, sc, ff_own, table_one, table_two, encoder
+    )
     sc_one = move.rows(sc, STEP_TWO)
     sc_two = move.rows(sc_row, STEP_TWO)
-    ff_got = [move.col(ff_own, bit) for bit in (2, 1, 3)]
+    ff_far = move.col(ff_own, 2)
+    enc_zero = move.spread(enc_in, 0)
     states_low = settle(jnp.stack([x_near, x_far]))
     small = states_low[:, seq : seq + 16].astype(F32)
     g_self, g_cross, g_ff, g_final = (small[:, n : n + 1] + small[:, n + 4 : n + 5] for n in range(4))
@@ -891,33 +899,33 @@
     states_all, normed_all, scale_all = norm_in([states_low], g_self, seq)
     states_own = lax.dynamic_slice_in_dim(states_low, half * tq, tq, 1)
     own_blocks = jnp.stack([sc, sc_row])
-    normed_all, states_own, own_blocks, scalars, ff_own, *ff_got = tie(
-        normed_all, states_own, own_blocks, scalars, ff_own, *ff_got
-    )
-    ff, enc_in = tie(jnp.concatenate([ff_own, *ff_got]), encoder)
-    enc_zero = move.spread(enc_in, 0)
+    normed_all, states_own, own_blocks, scalars, ff_own, want_near, want_far, ff_far, enc_zero, enc_in = tie(
+        normed_all, states_own, own_blocks, scalars, ff_own, want_near, want_far, ff_far, enc_zero, enc_in
+    )
+    ff = jnp.concatenate([ff_own, ff_far])
+    ff_got = move.col(ff, 1)
+    enc_one = move.spread(enc_in, 1)
     other_blocks = jnp.stack([sc_one, sc_two])
     ws = pick(first_core, own_blocks, other_blocks)
     wc = pick(first_core, other_blocks, own_blocks)
 
     qkv = project(ws, normed_all, 0, 3 * hw)
     self_args = ((qkv, 0, True), (qkv, heads), (qkv, 2 * heads))
-    qkv, ff = tie(qkv, ff)
     self_args = ((qkv, 0, True), (qkv, heads), (qkv, 2 * heads))
+    attended, totals_self = attend_forward(info, *self_args, True)
+    attended, enc_one, ff, ff_got = tie(attended, enc_one, ff, ff_got)
+    ff = jnp.concatenate([ff, ff_got])
     ff_row = move.rows(ff, STEP_ONE)
     ff_one = move.rows(ff, SAME_TWO)
-    attended, totals_self = attend_forward(info, *self_args, True)
-    attended, enc_zero, enc_in = tie(attended, enc_zero, enc_in)
-    enc_one = move.spread(enc_in, 1)
+    enc_all = settle(jnp.stack([enc_zero, enc_one]))
     branch = combine(ws, attended, 3 * hw, 4 * hw)
     first, normed_cross, scale_cross = norm_in([states_own, branch, move.core(branch)], g_cross, tq)
 
 
     cq = project(wc, normed_cross, 0, hw)
-    cq, enc_one, ff_row, ff_one = tie(cq, enc_one, ff_row, ff_one)
+    ckv = project(wc, enc_all, hw, 3 * hw)
+    cq, ckv, ff_row, ff_one = tie(cq, ckv, ff_row, ff_one)
     ff_two = move.rows(ff_row, SAME_TWO)
-    enc_all = settle(jnp.stack([enc_zero, enc_one]))
-    ckv = project(wc, enc_all, hw, 3 * hw)
     cross_args = ((cq, 0, False), (ckv, 0), (ckv, heads))
     crossed, totals_cross = attend_forward(info, *cross_args, False)
     crossed, ff_two, table_one = tie(crossed, ff_two, table_one)
@@ -970,9 +978,9 @@
     grad_table = vocab_table_grad(
         places, (*hidden_near, *hidden_far), (grads_near, grads_far)
     )
+    come_last, grad_table = tie(come_last, grad_table)
     if dp == 2:
         table_sum = lax.psum_scatter(grad_table, "row", scatter_dimension=0, tiled=True)
-    come_last, _ = tie(come_last, grad_table)
     part = plus(part[0], come_last)
     part = reorder(part, [col ^ row ^ swap_bits(n) for n in range(4)])
     other = move.core(part)
@@ -1013,7 +1021,9 @@
 
     grad_attended = project(ws, low_self, 3 * hw, 4 * hw)
     dq, dk, dv = attend_backward(info, *self_args, grad_attended, totals_self, True)
-    dq, dk, ff_sum = tie(dq, dk, ff_sum)
+    if dp == 2:
+        dq, table_sum = tie(dq, table_sum)
+    dq, dk, cross_come = tie(dq, dk, cross_come)
     self_zero, self_one = weight_grads(
         scalars, [(normed_all, dq), (normed_all, dk), (normed_all, dv), (low_self, attended)], 4 * hw
     )
@@ -1023,12 +1033,14 @@
         move.rows(self_one, {1: (1, 3)}),
     ]
     dk, self_zero, ff_sum = tie(dk, self_zero, ff_sum)
-    ff_parts = [ff_sum[p * block : (p + 1) * block] for p in range(4)]
-    ff_parts[1:] = [move.col(x, bit) for x, bit in zip(ff_parts[1:], (2, 1, 3))]
+    sum_ff = lax.psum_scatter(ff_sum, "col", scatter_dimension=0, tiled=True)
+    cross_sum = [cross_zero, *cross_come]
+    cut = d // 2
+    cross_send = total([x[cut:] for x in cross_sum]).astype(BF)
+    cross_keep = total([x[:cut] for x in cross_sum]).astype(BF)
+    cross_got = move.cols(cross_send, 1, 1)
+    dk, cross_keep = tie(dk, cross_keep)
     partial_normed = source_grads(ws, dq, 0, (dk, dv), (hw, 2 * hw), scalars, hw, F32)
-    partial_normed, *cross_come = tie(partial_normed, *cross_come)
-    cross_parts = z_sum([cross_zero, *cross_come], 1)
-    partial_normed, cross_own = tie(partial_normed, cross_parts[0])
     grad_states, gg_self = norm_out(
         scalars, states_all, g_self, scale_all, [partial_normed], grad_first, True
     )
@@ -1036,19 +1048,18 @@
     gain_columns = jnp.concatenate([gg_self, gg_cross * once, gg_ff * once, gg_final * once], axis=1)
     gain_columns = jnp.pad(gain_columns.astype(BF), ((0, 0), (0, 124)))
     grad_states = jnp.concatenate([grad_states, gain_columns], axis=1)
-    grad_states, *enc_come = tie(grad_states, *enc_come)
+    grad_states, enc_come, self_come, cross_got = tie(grad_states, enc_come, self_come, cross_got)
     in_keep, in_come = fold_core(grad_states)
     in_come = fold_out(in_keep, in_come)
-    in_come[0], cross_parts[1:], ff_parts, self_come = tie(
-        in_come[0], cross_parts[1:], ff_parts, self_come
-    )
     self_parts = z_sum([self_zero, *self_come], 0)
+    cross_sum = plus(cross_keep, cross_got)
+    cross_got = move.cols(cross_sum[block:], 2, 1)
     in_come = in_come[0].astype(F32) + in_come[1].astype(F32)
     in_come, self_own = tie(in_come, self_parts[0])
     packed = in_come[:, seq : seq + 4].T
     if dp == 2:
         come = [move.row(packed, bit) for bit in (1, 2, 3)]
-        packed, come, self_parts[1:], table_sum = tie(packed, come, self_parts[1:], table_sum)
+        packed, come, self_parts[1:], sum_ff = tie(packed, come, self_parts[1:], sum_ff)
         packed = packed + come[0] + come[1] + come[2]
         packed = packed + move.core(packed)
     else:
@@ -1057,8 +1068,8 @@
     grad_encoder = enc_come[0].astype(F32) + enc_come[1].astype(F32)
     grad_inputs = in_come[:, :seq]
     sum_self = total([self_own, *self_parts[1:]])
-    sum_cross = total([cross_own, *cross_parts[1:]])
-    sum_ff = total(ff_parts)
+    sum_cross = cross_sum[:block].astype(F32) + cross_got.astype(F32)
+    sum_ff = sum_ff.astype(F32)
 
     if dp == 2:
         cut = table_sum.reshape(2, d // 8, width)

time: 631 us -> 615 us (0.975)
  waiting for transfers between devices: 183 us -> 170 us
  starting transfers between devices: 110 us -> 99.2 us
    ppermute x6 -> x5, waiting for transfers between devices: 0.02 us -> 13.5 us  [cols(): return lax.ppermute(x, ('dp', 'col'), perm)]
    ppermute x15, waiting for transfers between devices: 52.4 us -> 40.2 us  [rows(): return lax.ppermute(x, ('dp', 'row'), perm)]
    ppermute x19, starting transfers between devices: 22 us -> 11.1 us  [core(): return lax.ppermute(x, 'dp', [(i, i ^ 1) for i in range(self.dp)])]
    ppermute x16 -> x12, waiting for transfers between devices: 92.7 us -> 81.9 us  [col(): return lax.ppermute(x, 'col', [(i, i ^ bit) for i in range(4)])]
    ppermute x15, starting transfers between devices: 18.6 us -> 27.7 us  [rows(): return lax.ppermute(x, ('dp', 'row'), perm)]
    unnamed x272 -> x240, local copies, waits for them, and re-layouts: 39.2 us -> 45.6 us
    ppermute x16 -> x12, starting transfers between devices: 22.2 us -> 18.2 us  [col(): return lax.ppermute(x, 'col', [(i, i ^ bit) for i in range(4)])]
    ppermute x6 -> x5, starting transfers between devices: 24.2 us -> 23.5 us  [cols(): return lax.ppermute(x, ('dp', 'col'), perm)]
  transfers between devices with their start and end apart: 71 -> 67, of which waited for: 34 -> 33; matrix products, arithmetic and copies ran while one was open for 7% -> 7% of each run, Pallas kernels for 26% -> 29%
where the time goes in v3:
time: 615 us; the launch traced here: 608 us
  Pallas kernels  216 us (35%)
  waiting for transfers between devices  170 us (28%)
  starting transfers between devices  99.2 us (16%)
  local copies, waits for them, and re-layouts  58.2 us (9%)
  other arithmetic  47 us (8%)
  between operations  18.1 us (3%)
    ppermute x12, waiting for transfers between devices, col(): return lax.ppermute(x, 'col', [(i, i ^ bit) for i in range(4)])  81.9 us
    unnamed x240, local copies, waits for them, and re-layouts  45.6 us
    ppermute x15, waiting for transfers between devices, rows(): return lax.ppermute(x, ('dp', 'row'), perm)  40.2 us
    pallas_call x2, Pallas kernels, vocab_forward(): pl.pallas_call(body, out_shape=(jax.ShapeDtypeStruct((chunks, width, step...  33.9 us
    pallas_call x2, Pallas kernels, attend_backward(): pl.pallas_call(body, out_shape=(jax.ShapeDtypeStruct((blocks, heads * HEA...  33.2 us
    pallas_call x2, Pallas kernels, vocab_hidden_grad(): pl.pallas_call(body, out_shape=(jax.ShapeDtypeStruct((chunks, width, step...  30.7 us
    ppermute x15, starting transfers between devices, rows(): return lax.ppermute(x, ('dp', 'row'), perm)  27.7 us
    ppermute x5, starting transfers between devices, cols(): return lax.ppermute(x, ('dp', 'col'), perm)  23.5 us
  transfers between devices with their start and end apart: 67, of which 33 were waited for; matrix products, arithmetic and copies ran while one was open for 7% of the time, Pallas kernels for 29%

profile of v3, /device:TPU:0, one launch (start us, length us, event | category | flops | bytes accessed | tf_op | source)
XLA Modules:
  0.0 608.3 jit_solution(13294766065676113858)
XLA Ops:
  10.7 5.1 collective-permute-start.2
  30.4 10.7 %collective-permute-done = bf16[192,768]{1,0:T(8,128)(2,1)} collective-permute-done((bf16[192,768]{1,0:T(8,128)(2,1)S(1)}, bf16[192,768]{1,0:T(8,128)(2,1)}, u32[]{:S(2)}, u32[]{:S(2)}) %collective-permute-start) | collective-permute-done | bytes 294944 | tf_op jit(solution)/shard_map/ppermute | solution.py:698
  44.5 12.9 %collective-permute-done.4 = bf16[192,1152]{1,0:T(8,128)(2,1)S(1)} collective-permute-done((bf16[192,1152]{1,0:T(8,128)(2,1)S(1)}, bf16[192,1152]{1,0:T(8,128)(2,1)S(1)}, u32[]{:S(2)}, u32[]{:S(2)}) %collective-permute-start.4) | collective-permute-done | bytes 442400 | tf_op jit(solution)/shard_map/ppermute | solution.py:725
  57.4 9.7 %collective-permute-done.5 = bf16[768,768]{1,0:T(8,128)(2,1)S(1)} collective-permute-done((bf16[768,768]{1,0:T(8,128)(2,1)S(1)}, bf16[768,768]{1,0:T(8,128)(2,1)S(1)}, u32[]{:S(2)}, u32[]{:S(2)}) %collective-permute-start.5) | collective-permute-done | bytes 1179680 | tf_op jit(solution)/shard_map/ppermute | solution.py:717
  86.9 9.6 %collective-permute-done.10 = bf16[192,768]{1,0:T(8,128)(2,1)S(1)} collective-permute-done((bf16[192,768]{1,0:T(8,128)(2,1)S(1)}, bf16[192,768]{1,0:T(8,128)(2,1)S(1)}, u32[]{:S(2)}, u32[]{:S(2)}) %collective-permute-start.10) | collective-permute-done | bytes 294944 | tf_op jit(solution)/shard_map/ppermute | solution.py:698
  98.7 5.5 collective-permute-done.13
  106.8 8.0 %shard_map.349 = (bf16[2,192,512]{2,1,0:T(8,128)(2,1)S(1)}, f32[6,1,512]{2,1,0:T(1,128)S(1)}) custom-call(s32[3]{0:T(128)S(1)} %pad_add_fusion.2.s_ref.refs_0_, bf16[2,576,1024]{2,1,0:T(8,128)(2,1)S(1)} %shard_map.348.q_ref.k_ref.v_ref, bf16[2,576,1024]{2,1,0:T(8,128)(2,1)S(1)} %shard_map.348.q_ref.k_ref.v_ref, ...), custom_call_target="tpu_custom_call" | custom-call | tf_op jit(solution)/shard_map/pallas_call | solution.py:69
  114.9 19.6 %collective-permute-done.15 = bf16[384,768]{1,0:T(8,128)(2,1)S(1)} collective-permute-done((bf16[384,768]{1,0:T(8,128)(2,1)S(1)}, bf16[384,768]{1,0:T(8,128)(2,1)S(1)}, u32[]{:S(2)}, u32[]{:S(2)}) %collective-permute-start.15) | collective-permute-done | bytes 589856 | tf_op jit(solution)/shard_map/ppermute | solution.py:698
  146.1 18.1 %collective-permute-done.19.refs_2_ = bf16[768,768]{1,0:T(8,128)(2,1)S(1)} collective-permute-done((bf16[768,768]{1,0:T(8,128)(2,1)S(1)}, bf16[768,768]{1,0:T(8,128)(2,1)S(1)}, u32[]{:S(2)}, u32[]{:S(2)}) %collective-permute-start.19) | collective-permute-done | bytes 1179680 | tf_op jit(solution)/shard_map/ppermute | solution.py:717
  165.8 13.5 %shard_map.354 = (bf16[2,192,512]{2,1,0:T(8,128)(2,1)S(1)}, f32[6,1,512]{2,1,0:T(1,128)S(1)}) custom-call(s32[3]{0:T(128)S(1)} %pad_add_fusion.2.s_ref.refs_0_, bf16[2,192,512]{2,1,0:T(8,128)(2,1)S(1)} %shard_map.352.q_ref, bf16[2,384,2048]{2,1,0:T(8,128)(2,1)S(1)} %shard_map.353.k_ref.v_ref, bf16[2,384,2048]{2,1,0:T(8,128)(2,1)S(1)} %shard_map.353.k_ref.v_ref), custom_call_target="tpu_custom_call" | custom-call | tf_op jit(solution)/shard_map/pallas_call | solution.py:69
  186.3 7.0 %shard_map.357 = (bf16[512,512]{1,0:T(8,128)(2,1)S(1)}, bf16[512,512]{1,0:T(8,128)(2,1)S(1)}, bf16[512,512]{1,0:T(8,128)(2,1)S(1)}, bf16[512,512]{1,0:T(8,128)(2,1)S(1)}, f32[768,512]{1,0:T(8,128)}) custom-call(bf16[768,768]{1,0:T(8,128)(2,1)S(1)} %constant_dynamic-update-slice_fusion.2.refs_0_, bf16[768,768]{1,0:T(8,128)(2,1)S(1)} %collective-permute-done.18.refs_1_, ...), custom_call_target="tpu_custom_call" | custom-call | tf_op jit(solution)/shard_map/pallas_call | solution.py:171
  207.8 19.1 %collective-permute-done.23 = bf16[768,256]{1,0:T(8,128)(2,1)S(1)} collective-permute-done((bf16[768,256]{1,0:T(8,128)(2,1)S(1)}, bf16[768,256]{1,0:T(8,128)(2,1)S(1)}, u32[]{:S(2)}, u32[]{:S(2)}) %collective-permute-start.23) | collective-permute-done | bytes 393248 | tf_op jit(solution)/shard_map/ppermute | solution.py:698
  229.5 16.8 %shard_map.359 = (bf16[4,4096,256]{2,1,0:T(8,128)(2,1)}, f32[8,4,256]{2,1,0:T(4,128)S(1)}, f32[3,4,256]{2,1,0:T(4,128)S(1)}) custom-call(s32[2]{0:T(128)S(1)} %pad_add_fusion.s_ref, bf16[2,768,256]{2,1,0:T(8,128)(2,1)S(1)} %pad_maximum_fusion.12.h0_ref.refs_1_, bf16[2,768,256]{2,1,0:T(8,128)(2,1)} %collective-permute-done.26.h1_ref.refs_2_, ...), custom_call_target="tpu_custom_call" | custom-call | tf_op jit(solution)/shard_map/pallas_call | solution.py:519
  249.7 17.1 %shard_map.360 = (bf16[4,4096,256]{2,1,0:T(8,128)(2,1)}, f32[8,4,256]{2,1,0:T(4,128)S(1)}, f32[3,4,256]{2,1,0:T(4,128)S(1)}) custom-call(s32[2]{0:T(128)S(1)} %pad_add_fusion.s_ref, bf16[2,768,256]{2,1,0:T(8,128)(2,1)} %collective-permute-done.25.h0_ref.refs_3_, bf16[2,768,256]{2,1,0:T(8,128)(2,1)S(1)} %collective-permute-done.27.h1_ref.refs_4_, ...), custom_call_target="tpu_custom_call" | custom-call | tf_op jit(solution)/shard_map/pallas_call | solution.py:519
  279.2 15.4 %shard_map.363 = (bf16[4,4096,256]{2,1,0:T(8,128)(2,1)}, bf16[2,768,256]{2,1,0:T(8,128)(2,1)}, bf16[2,768,256]{2,1,0:T(8,128)(2,1)}) custom-call(s32[2]{0:T(128)} %copy-done.83, bf16[4,4096,256]{2,1,0:T(8,128)(2,1)} %get-tuple-element.240.e_ref, f32[8,4,256]{2,1,0:T(4,128)} %copy-done.79, f32[8,256]{1,0:T(8,128)} %copy-done.80, ...), custom_call_target="tpu_custom_call", output_to_operand_aliasing={{0}: (1, {})} | custom-call | tf_op jit(solution)/shard_map/pallas_call | solution.py:573
  298.5 15.4 %shard_map.364 = (bf16[4,4096,256]{2,1,0:T(8,128)(2,1)}, bf16[2,768,256]{2,1,0:T(8,128)(2,1)}, bf16[2,768,256]{2,1,0:T(8,128)(2,1)}) custom-call(s32[2]{0:T(128)} %copy-done.83, bf16[4,4096,256]{2,1,0:T(8,128)(2,1)} %get-tuple-element.246.e_ref, f32[8,4,256]{2,1,0:T(4,128)} %copy-done.78, f32[8,256]{1,0:T(8,128)} %copy-done.80, ...), custom_call_target="tpu_custom_call", output_to_operand_aliasing={{0}: (1, {})} | custom-call | tf_op jit(solution)/shard_map/pallas_call | solution.py:573
  316.4 17.5 %collective-permute-done.36 = bf16[2,768,256]{2,1,0:T(8,128)(2,1)S(1)} collective-permute-done((bf16[2,768,256]{2,1,0:T(8,128)(2,1)S(1)}, bf16[2,768,256]{2,1,0:T(8,128)(2,1)S(1)}, u32[]{:S(2)}, u32[]{:S(2)}) %collective-permute-start.36) | collective-permute-done | bytes 786464 | tf_op jit(solution)/shard_map/ppermute | solution.py:698
  340.0 18.3 %shard_map.365 = bf16[768,4096]{1,0:T(8,128)(2,1)} custom-call(s32[8]{0:T(128)S(1)} %stack.226.refs_0_, bf16[2,768,256]{2,1,0:T(8,128)(2,1)S(1)} %pad_maximum_fusion.12.h0_ref.refs_1_, bf16[2,768,256]{2,1,0:T(8,128)(2,1)} %collective-permute-done.26.h1_ref.refs_2_, bf16[2,768,256]{2,1,0:T(8,128)(2,1)} %collective-permute-done.25.h0_ref.refs_3_, ...), custom_call_target="tpu_custom_call" | custom-call | tf_op jit(solution)/shard_map/pallas_call | solution.py:619
  367.4 12.8 %shard_map.367 = (bf16[4,768,768]{2,1,0:T(8,128)(2,1)}, f32[768,512]{1,0:T(8,128)}) custom-call(s32[8]{0:T(128)} %stack.235.s_ref, bf16[768,768]{1,0:T(8,128)(2,1)} %copy-done.12, bf16[768,768]{1,0:T(8,128)(2,1)} %copy-done.24, bf16[768,768]{1,0:T(8,128)(2,1)} %copy-done.96, bf16[768,768]{1,0:T(8,128)(2,1)} %collective-permute-done.20.refs_3_, ...), custom_call_target="tpu_custom_call" | custom-call | tf_op jit(solution)/shard_map/pallas_call | solution.py:206
  393.2 21.0 %shard_map.370 = (bf16[2,192,512]{2,1,0:T(8,128)(2,1)S(1)}, bf16[2,192,2048]{2,1,0:T(8,128)(2,1)S(1)}, bf16[2,192,2048]{2,1,0:T(8,128)(2,1)S(1)}) custom-call(s32[3]{0:T(128)S(1)} %pad_add_fusion.2.s_ref.refs_0_, bf16[2,192,512]{2,1,0:T(8,128)(2,1)S(1)} %copy-done.34, bf16[2,384,2048]{2,1,0:T(8,128)(2,1)} %copy-done.2, bf16[2,384,2048]{2,1,0:T(8,128)(2,1)} %copy-done.2, ...), custom_call_target="tpu_custom_call" | custom-call | tf_op jit(solution)/shard_map/pallas_call | solution.py:113
  416.0 4.6 shard_map.372
  436.1 10.9 %shard_map.374 = (bf16[768,768]{1,0:T(8,128)(2,1)}, bf16[768,768]{1,0:T(8,128)(2,1)}) custom-call(s32[3]{0:T(128)S(1)} %pad_add_fusion.2.s_ref.refs_0_, bf16[768,512]{1,0:T(8,128)(2,1)S(1)} %copy-done.36, bf16[768,2048]{1,0:T(8,128)(2,1)} %copy-done.6, bf16[768,2048]{1,0:T(8,128)(2,1)} %copy-done.6, bf16[768,512]{1,0:T(8,128)(2,1)S(1)} %get-tuple-element.260.x_ref.refs_4_, ...), custom_call_target="tpu_custom_call" | custom-call | tf_op jit(solution)/shard_map/pallas_call | solution.py:382
  448.7 4.9 collective-permute-start.43
  463.0 7.4 %collective-permute-start.45 = (bf16[192,2048]{1,0:T(8,128)(2,1)}, bf16[192,2048]{1,0:T(8,128)(2,1)}, u32[]{:S(2)}, u32[]{:S(2)}) collective-permute-start(bf16[192,2048]{1,0:T(8,128)(2,1)} %get-tuple-element.339), channel_id=1, source_target_pairs={{0,0},{1,1},{16,2},{17,3},{2,16},{3,17},{18,18},{19,19},{4,4},{5,5... | collective-permute-start | bytes 2359304 | tf_op jit(solution)/shard_map/ppermute | solution.py:725
  470.4 12.2 %shard_map.376 = (bf16[2,192,512]{2,1,0:T(8,128)(2,1)S(1)}, bf16[2,192,1024]{2,1,0:T(8,128)(2,1)S(1)}, bf16[2,192,1024]{2,1,0:T(8,128)(2,1)S(1)}) custom-call(s32[3]{0:T(128)S(1)} %pad_add_fusion.2.s_ref.refs_0_, bf16[2,576,1024]{2,1,0:T(8,128)(2,1)S(1)} %shard_map.348.q_ref.k_ref.v_ref, bf16[2,576,1024]{2,1,0:T(8,128)(2,1)S(1)} %shard_map.348.q_ref.k_ref.v_ref, ...), custom_call_target="tpu_custom_call" | custom-call | tf_op jit(solution)/shard_map/pallas_call | solution.py:113
  491.0 6.9 %shard_map.377 = (bf16[768,768]{1,0:T(8,128)(2,1)}, bf16[768,768]{1,0:T(8,128)(2,1)}) custom-call(s32[3]{0:T(128)S(1)} %pad_add_fusion.2.s_ref.refs_0_, bf16[768,1024]{1,0:T(8,128)(2,1)} %copy-done.9, bf16[768,1024]{1,0:T(8,128)(2,1)} %copy-done.9, bf16[768,1024]{1,0:T(8,128)(2,1)} %copy-done.9, bf16[768,512]{1,0:T(8,128)(2,1)S(1)} %copy-done.41, ...), custom_call_target="tpu_custom_call" | custom-call | tf_op jit(solution)/shard_map/pallas_call | solution.py:382
  503.0 4.0 add_convert_fusion.4
  522.8 4.0 shard_map.379
  528.2 5.1 collective-permute-start.63
  547.2 6.7 %collective-permute-start.57 = (bf16[192,768]{1,0:T(8,128)(2,1)S(1)}, bf16[192,768]{1,0:T(8,128)(2,1)S(1)}, u32[]{:S(2)}, u32[]{:S(2)}) collective-permute-start(bf16[192,768]{1,0:T(8,128)(2,1)S(1)} %get-tuple-element.312), channel_id=1, source_target_pairs={{0,2},{1,3},{2,0},{3,1},{4,6},{5,7},{6,4},{7,5},{8,10},{9,11},{10,... | collective-permute-start | bytes 884744 | tf_op jit(solution)/shard_map/ppermute | solution.py:705
  557.8 10.7 %collective-permute-start.59 = (bf16[192,768]{1,0:T(8,128)(2,1)S(1)}, bf16[192,768]{1,0:T(8,128)(2,1)}, u32[]{:S(2)}, u32[]{:S(2)}) collective-permute-start(bf16[192,768]{1,0:T(8,128)(2,1)S(1)} %get-tuple-element.314), channel_id=1, source_target_pairs={{0,3},{1,2},{2,1},{3,0},{4,7},{5,6},{6,5},{7,4},{8,11},{9,10},{10,... | collective-permute-start | bytes 884744 | tf_op jit(solution)/shard_map/ppermute | solution.py:705
  569.9 13.5 %collective-permute-done.57 = bf16[192,768]{1,0:T(8,128)(2,1)S(1)} collective-permute-done((bf16[192,768]{1,0:T(8,128)(2,1)S(1)}, bf16[192,768]{1,0:T(8,128)(2,1)S(1)}, u32[]{:S(2)}, u32[]{:S(2)}) %collective-permute-start.57) | collective-permute-done | bytes 294944 | tf_op jit(solution)/shard_map/ppermute | solution.py:705
  (486 shorter events, 226.2 us)
Async XLA Ops:
  7.2 478.0 %reduce-scatter.4.cloned.1.call-start = ((), (), s32[]{:S(2)}) async-start(), calls=%async_computation.3 | async-start | bytes 7864320 | tf_op jit(solution)/shard_map/reduce_scatter | solution.py:983
  15.8 25.2 %collective-permute-start = (bf16[192,768]{1,0:T(8,128)(2,1)S(1)}, bf16[192,768]{1,0:T(8,128)(2,1)}, u32[]{:S(2)}, u32[]{:S(2)}) collective-permute-start(bf16[192,768]{1,0:T(8,128)(2,1)S(1)} %maximum_select_fusion.1), channel_id=1, source_target_pairs={{0,2},{1,3},{2,0},{3,1},{4,6},{5,7},{6,4},{7,5},{8,10},{9,11},{10,... | collective-permute-start | bytes 884744 | tf_op jit(solution)/shard_map/ppermute | solution.py:698
  18.9 48.3 %collective-permute-start.7 = (bf16[192,4096]{1,0:T(8,128)(2,1)S(1)}, bf16[192,4096]{1,0:T(8,128)(2,1)S(1)}, u32[]{:S(2)}, u32[]{:S(2)}) collective-permute-start(bf16[192,4096]{1,0:T(8,128)(2,1)S(1)} %fusion.own_ref), channel_id=1, source_target_pairs={{0,8},{4,12},{8,0},{12,4},{16,20},{20,16},{24,28},{28,24},{1,9},{5... | collective-permute-start | bytes 4718600 | tf_op jit(solution)/shard_map/ppermute | solution.py:717
  20.6 46.6 %collective-permute-start.6 = (bf16[192,4096]{1,0:T(8,128)(2,1)S(1)}, bf16[192,4096]{1,0:T(8,128)(2,1)}, u32[]{:S(2)}, u32[]{:S(2)}) collective-permute-start(bf16[192,4096]{1,0:T(8,128)(2,1)S(1)} %fusion.own_ref), channel_id=1, source_target_pairs={{0,4},{4,0},{8,12},{12,8},{16,24},{20,28},{24,16},{28,20},{1,5},{5... | collective-permute-start | bytes 4718600 | tf_op jit(solution)/shard_map/ppermute | solution.py:717
  42.3 24.9 %collective-permute-start.5 = (bf16[768,768]{1,0:T(8,128)(2,1)S(1)}, bf16[768,768]{1,0:T(8,128)(2,1)S(1)}, u32[]{:S(2)}, u32[]{:S(2)}) collective-permute-start(bf16[768,768]{1,0:T(8,128)(2,1)S(1)} %pad_maximum_fusion.8), channel_id=1, source_target_pairs={{0,4},{4,0},{8,12},{12,8},{16,24},{20,28},{24,16},{28,20},{1,5},{5... | collective-permute-start | bytes 3538952 | tf_op jit(solution)/shard_map/ppermute | solution.py:717
  71.5 25.0 %collective-permute-start.10 = (bf16[192,768]{1,0:T(8,128)(2,1)S(1)}, bf16[192,768]{1,0:T(8,128)(2,1)S(1)}, u32[]{:S(2)}, u32[]{:S(2)}) collective-permute-start(bf16[192,768]{1,0:T(8,128)(2,1)S(1)} %copy-done.104), channel_id=1, source_target_pairs={{0,2},{1,3},{2,0},{3,1},{4,6},{5,7},{6,4},{7,5},{8,10},{9,11},{10,... | collective-permute-start | bytes 884744 | tf_op jit(solution)/shard_map/ppermute | solution.py:698
  73.9 22.6 %collective-permute-start.11 = (bf16[192,2048]{1,0:T(8,128)(2,1)}, bf16[192,2048]{1,0:T(8,128)(2,1)S(1)}, u32[]{:S(2)}, u32[]{:S(2)}) collective-permute-start(bf16[192,2048]{1,0:T(8,128)(2,1)} %param.21), channel_id=1, source_target_pairs={{0,0},{1,1},{2,16},{3,17},{16,2},{17,3},{18,18},{19,19},{4,4},{5,5... | collective-permute-start | bytes 2359304 | tf_op jit(solution)/shard_map/ppermute | solution.py:725
  75.7 23.0 %collective-permute-start.12 = (bf16[768,768]{1,0:T(8,128)(2,1)S(1)}, bf16[768,768]{1,0:T(8,128)(2,1)S(1)}, u32[]{:S(2)}, u32[]{:S(2)}) collective-permute-start(bf16[768,768]{1,0:T(8,128)(2,1)S(1)} %copy-done.95), channel_id=1, source_target_pairs={{0,24},{4,28},{8,16},{12,20},{16,4},{20,0},{24,12},{28,8},{1,25},{... | collective-permute-start | bytes 3538952 | tf_op jit(solution)/shard_map/ppermute | solution.py:717
  77.7 26.5 %collective-permute-start.13 = (bf16[768,768]{1,0:T(8,128)(2,1)}, bf16[768,768]{1,0:T(8,128)(2,1)S(1)}, u32[]{:S(2)}, u32[]{:S(2)}) collective-permute-start(bf16[768,768]{1,0:T(8,128)(2,1)} %copy-done.105), channel_id=1, source_target_pairs={{0,24},{4,28},{8,16},{12,20},{16,4},{20,0},{24,12},{28,8},{1,25},{... | collective-permute-start | bytes 3538952 | tf_op jit(solution)/shard_map/ppermute | solution.py:717
  96.5 37.9 %collective-permute-start.14 = (bf16[192,2048]{1,0:T(8,128)(2,1)}, bf16[192,2048]{1,0:T(8,128)(2,1)S(1)}, u32[]{:S(2)}, u32[]{:S(2)}) collective-permute-start(bf16[192,2048]{1,0:T(8,128)(2,1)} %param.21), channel_id=1, source_target_pairs={{0,1},{1,0},{2,17},{3,16},{16,3},{17,2},{18,19},{19,18},{4,5},{5,4... | collective-permute-start | bytes 2359304 | tf_op jit(solution)/shard_map/ppermute | solution.py:725
  97.0 37.4 %collective-permute-start.15 = (bf16[384,768]{1,0:T(8,128)(2,1)S(1)}, bf16[384,768]{1,0:T(8,128)(2,1)S(1)}, u32[]{:S(2)}, u32[]{:S(2)}) collective-permute-start(bf16[384,768]{1,0:T(8,128)(2,1)S(1)} %constant_dynamic-update-slice_fusion), channel_id=1, source_target_pairs={{0,1},{1,0},{2,3},{3,2},{4,5},{5,4},{6,7},{7,6},{8,9},{9,8},{10,11... | collective-permute-start | bytes 1769480 | tf_op jit(solution)/shard_map/ppermute | solution.py:698
  136.0 28.3 %collective-permute-start.19 = (bf16[768,768]{1,0:T(8,128)(2,1)S(1)}, bf16[768,768]{1,0:T(8,128)(2,1)S(1)}, u32[]{:S(2)}, u32[]{:S(2)}) collective-permute-start(bf16[768,768]{1,0:T(8,128)(2,1)S(1)} %constant_dynamic-update-slice_fusion.2.refs_0_), channel_id=1, source_target_pairs={{0,8},{4,12},{8,0},{12,4},{16,20},{20,16},{24,28},{28,24},{1,9},{5... | collective-permute-start | bytes 3538952 | tf_op jit(solution)/shard_map/ppermute | solution.py:717
  137.5 26.7 %collective-permute-start.18 = (bf16[768,768]{1,0:T(8,128)(2,1)S(1)}, bf16[768,768]{1,0:T(8,128)(2,1)S(1)}, u32[]{:S(2)}, u32[]{:S(2)}) collective-permute-start(bf16[768,768]{1,0:T(8,128)(2,1)S(1)} %constant_dynamic-update-slice_fusion.2.refs_0_), channel_id=1, source_target_pairs={{0,4},{4,0},{8,12},{12,8},{16,24},{20,28},{24,16},{28,20},{1,5},{5... | collective-permute-start | bytes 3538952 | tf_op jit(solution)/shard_map/ppermute | solution.py:717
  196.7 30.3 %collective-permute-start.24 = (bf16[192,4096]{1,0:T(8,128)(2,1)}, bf16[192,4096]{1,0:T(8,128)(2,1)}, u32[]{:S(2)}, u32[]{:S(2)}) collective-permute-start(bf16[192,4096]{1,0:T(8,128)(2,1)} %collective-permute-done.6.one_ref), channel_id=1, source_target_pairs={{0,8},{4,12},{8,0},{12,4},{16,20},{20,16},{24,28},{28,24},{1,9},{5... | collective-permute-start | bytes 4718600 | tf_op jit(solution)/shard_map/ppermute | solution.py:717
  206.4 20.5 %collective-permute-start.23 = (bf16[768,256]{1,0:T(8,128)(2,1)S(1)}, bf16[768,256]{1,0:T(8,128)(2,1)S(1)}, u32[]{:S(2)}, u32[]{:S(2)}) collective-permute-start(bf16[768,256]{1,0:T(8,128)(2,1)S(1)} %get-tuple-element.391), channel_id=1, source_target_pairs={{0,2},{1,3},{2,0},{3,1},{4,6},{5,7},{6,4},{7,5},{8,10},{9,11},{10,... | collective-permute-start | bytes 1179656 | tf_op jit(solution)/shard_map/ppermute | solution.py:698
  338.3 20.2 %collective-permute-start.37 = (bf16[768,256]{1,0:T(8,128)(2,1)}, bf16[768,256]{1,0:T(8,128)(2,1)}, u32[]{:S(2)}, u32[]{:S(2)}) collective-permute-start(bf16[768,256]{1,0:T(8,128)(2,1)} %fusion.9), channel_id=1, source_target_pairs={{0,2},{1,3},{2,0},{3,1},{4,6},{5,7},{6,4},{7,5},{8,10},{9,11},{10,... | collective-permute-start | bytes 1179656 | tf_op jit(solution)/shard_map/ppermute | solution.py:698
  358.6 152.4 %reduce-scatter.6.cloned.1.call-start = ((), (), s32[]{:S(2)}) async-start(), calls=%async_computation.4 | async-start | bytes 5898240 | tf_op jit(solution)/shard_map/reduce_scatter | solution.py:995
  380.2 207.9 %reduce-scatter.8.cloned.1.call-start = ((), (), s32[]{:S(2)}) async-start(), calls=%async_computation.5 | async-start | bytes 1474560 | tf_op jit(solution)/shard_map/reduce_scatter | solution.py:1036
  447.0 40.7 %collective-permute-start.44 = (bf16[768,768]{1,0:T(8,128)(2,1)}, bf16[768,768]{1,0:T(8,128)(2,1)}, u32[]{:S(2)}, u32[]{:S(2)}) collective-permute-start(bf16[768,768]{1,0:T(8,128)(2,1)} %get-tuple-element.283), channel_id=1, source_target_pairs={{16,24},{20,28},{24,16},{28,20},{17,25},{21,29},{25,17},{29,21},{1... | collective-permute-start | bytes 3538952 | tf_op jit(solution)/shard_map/ppermute | solution.py:717
  448.7 39.0 %collective-permute-start.43 = (bf16[768,768]{1,0:T(8,128)(2,1)}, bf16[768,768]{1,0:T(8,128)(2,1)}, u32[]{:S(2)}, u32[]{:S(2)}) collective-permute-start(bf16[768,768]{1,0:T(8,128)(2,1)} %get-tuple-element.283), channel_id=1, source_target_pairs={{0,28},{4,24},{8,20},{12,16},{1,29},{5,25},{9,21},{13,17},{2,30},{... | collective-permute-start | bytes 3538952 | tf_op jit(solution)/shard_map/ppermute | solution.py:717
  453.6 34.1 %collective-permute-start.42 = (bf16[768,768]{1,0:T(8,128)(2,1)}, bf16[768,768]{1,0:T(8,128)(2,1)}, u32[]{:S(2)}, u32[]{:S(2)}) collective-permute-start(bf16[768,768]{1,0:T(8,128)(2,1)} %get-tuple-element.282), channel_id=1, source_target_pairs={{0,20},{4,16},{8,28},{12,24},{1,21},{5,17},{9,29},{13,25},{2,22},{... | collective-permute-start | bytes 3538952 | tf_op jit(solution)/shard_map/ppermute | solution.py:717
  459.9 48.8 %collective-permute-start.46 = (bf16[192,2048]{1,0:T(8,128)(2,1)}, bf16[192,2048]{1,0:T(8,128)(2,1)}, u32[]{:S(2)}, u32[]{:S(2)}) collective-permute-start(bf16[192,2048]{1,0:T(8,128)(2,1)} %get-tuple-element.338), channel_id=1, source_target_pairs={{1,0},{0,1},{17,2},{16,3},{3,16},{2,17},{19,18},{18,19},{5,4},{4,5... | collective-permute-start | bytes 2359304 | tf_op jit(solution)/shard_map/ppermute | solution.py:725
  463.0 64.3 %collective-permute-start.45 = (bf16[192,2048]{1,0:T(8,128)(2,1)}, bf16[192,2048]{1,0:T(8,128)(2,1)}, u32[]{:S(2)}, u32[]{:S(2)}) collective-permute-start(bf16[192,2048]{1,0:T(8,128)(2,1)} %get-tuple-element.339), channel_id=1, source_target_pairs={{0,0},{1,1},{16,2},{17,3},{2,16},{3,17},{18,18},{19,19},{4,4},{5,5... | collective-permute-start | bytes 2359304 | tf_op jit(solution)/shard_map/ppermute | solution.py:725
  497.9 38.6 %collective-permute-start.49 = (bf16[768,768]{1,0:T(8,128)(2,1)}, bf16[768,768]{1,0:T(8,128)(2,1)}, u32[]{:S(2)}, u32[]{:S(2)}) collective-permute-start(bf16[768,768]{1,0:T(8,128)(2,1)} %get-tuple-element.302), channel_id=1, source_target_pairs={{16,12},{20,8},{24,4},{28,0},{17,13},{21,9},{25,5},{29,1},{18,14},... | collective-permute-start | bytes 3538952 | tf_op jit(solution)/shard_map/ppermute | solution.py:717
  499.3 37.2 %collective-permute-start.47 = (bf16[768,768]{1,0:T(8,128)(2,1)}, bf16[768,768]{1,0:T(8,128)(2,1)}, u32[]{:S(2)}, u32[]{:S(2)}) collective-permute-start(bf16[768,768]{1,0:T(8,128)(2,1)} %get-tuple-element.302), channel_id=1, source_target_pairs={{0,4},{4,0},{8,12},{12,8},{1,5},{5,1},{9,13},{13,9},{2,6},{6,2},{1... | collective-permute-start | bytes 3538952 | tf_op jit(solution)/shard_map/ppermute | solution.py:717
  507.1 26.3 %collective-permute-start.50 = (bf16[384,768]{1,0:T(8,128)(2,1)}, bf16[384,768]{1,0:T(8,128)(2,1)}, u32[]{:S(2)}, u32[]{:S(2)}) collective-permute-start(bf16[384,768]{1,0:T(8,128)(2,1)} %get-tuple-element.334), channel_id=1, source_target_pairs={{16,17},{17,16},{18,19},{19,18},{20,21},{21,20},{22,23},{23,22},{2... | collective-permute-start | bytes 1769480 | tf_op jit(solution)/shard_map/ppermute | solution.py:705
  508.7 27.8 %collective-permute-start.48 = (bf16[768,768]{1,0:T(8,128)(2,1)}, bf16[768,768]{1,0:T(8,128)(2,1)}, u32[]{:S(2)}, u32[]{:S(2)}) collective-permute-start(bf16[768,768]{1,0:T(8,128)(2,1)} %get-tuple-element.304.refs_0_), channel_id=1, source_target_pairs={{16,8},{20,12},{24,0},{28,4},{17,9},{21,13},{25,1},{29,5},{18,10},... | collective-permute-start | bytes 3538952 | tf_op jit(solution)/shard_map/ppermute | solution.py:717
  540.4 28.1 %collective-permute-start.53 = (bf16[192,1152]{1,0:T(8,128)(2,1)S(1)}, bf16[192,1152]{1,0:T(8,128)(2,1)S(1)}, u32[]{:S(2)}, u32[]{:S(2)}) collective-permute-start(bf16[192,1152]{1,0:T(8,128)(2,1)S(1)} %get-tuple-element.351), channel_id=1, source_target_pairs={{1,0},{0,1},{17,2},{16,3},{3,16},{2,17},{19,18},{18,19},{5,4},{4,5... | collective-permute-start | bytes 1327112 | tf_op jit(solution)/shard_map/ppermute | solution.py:725
  543.6 45.9 %collective-permute-start.61 = (bf16[192,768]{1,0:T(8,128)(2,1)}, bf16[192,768]{1,0:T(8,128)(2,1)S(1)}, u32[]{:S(2)}, u32[]{:S(2)}) collective-permute-start(bf16[192,768]{1,0:T(8,128)(2,1)} %slice.421), channel_id=1, source_target_pairs={{16,18},{17,19},{18,16},{19,17},{20,22},{21,23},{22,20},{23,21},{2... | collective-permute-start | bytes 884744 | tf_op jit(solution)/shard_map/ppermute | solution.py:705
  547.2 36.1 %collective-permute-start.57 = (bf16[192,768]{1,0:T(8,128)(2,1)S(1)}, bf16[192,768]{1,0:T(8,128)(2,1)S(1)}, u32[]{:S(2)}, u32[]{:S(2)}) collective-permute-start(bf16[192,768]{1,0:T(8,128)(2,1)S(1)} %get-tuple-element.312), channel_id=1, source_target_pairs={{0,2},{1,3},{2,0},{3,1},{4,6},{5,7},{6,4},{7,5},{8,10},{9,11},{10,... | collective-permute-start | bytes 884744 | tf_op jit(solution)/shard_map/ppermute | solution.py:705
  553.9 30.9 %collective-permute-start.58 = (bf16[192,768]{1,0:T(8,128)(2,1)S(1)}, bf16[192,768]{1,0:T(8,128)(2,1)S(1)}, u32[]{:S(2)}, u32[]{:S(2)}) collective-permute-start(bf16[192,768]{1,0:T(8,128)(2,1)S(1)} %get-tuple-element.313), channel_id=1, source_target_pairs={{0,1},{1,0},{2,3},{3,2},{4,5},{5,4},{6,7},{7,6},{8,9},{9,8},{10,11... | collective-permute-start | bytes 884744 | tf_op jit(solution)/shard_map/ppermute | solution.py:705
  557.8 30.3 %collective-permute-start.59 = (bf16[192,768]{1,0:T(8,128)(2,1)S(1)}, bf16[192,768]{1,0:T(8,128)(2,1)}, u32[]{:S(2)}, u32[]{:S(2)}) collective-permute-start(bf16[192,768]{1,0:T(8,128)(2,1)S(1)} %get-tuple-element.314), channel_id=1, source_target_pairs={{0,3},{1,2},{2,1},{3,0},{4,7},{5,6},{6,5},{7,4},{8,11},{9,10},{10,... | collective-permute-start | bytes 884744 | tf_op jit(solution)/shard_map/ppermute | solution.py:705
  (153 other events, 1761.1 us)
Sparse Core Ops, SparseCore 0:
  358.7 68.8 reduce-scatter.3
  430.6 79.0 reduce-scatter.5
  517.7 35.3 reduce-scatter.7

commit v4 on v3

--- a/solution.py
+++ b/solution.py
@@ -882,12 +882,15 @@
     want_near, want_far = target_chunks(half), target_chunks(1 - half)
     sc_row = move.rows(sc, STEP_ONE)
     x_got = [move.spread(x_in, 0), move.spread(x_in, 1)]
-    x_near, x_far, sc_row, sc, ff_own, table_one, table_two, enc_in = tie(
-        *x_got, sc_row, sc, ff_own, table_one, table_two, encoder
+    x_near, x_far, ff_own = tie(*x_got, ff_own)
+    ff_far = move.col(ff_own, 2)
+    x_near, x_far, sc_row, sc, ff_own, ff_far, table_one, table_two, enc_in = tie(
+        x_near, x_far, sc_row, sc, ff_own, ff_far, table_one, table_two, encoder
     )
     sc_one = move.rows(sc, STEP_TWO)
     sc_two = move.rows(sc_row, STEP_TWO)
-    ff_far = move.col(ff_own, 2)
+    ff = jnp.concatenate([ff_own, ff_far])
+    ff_got = move.col(ff, 1)
     enc_zero = move.spread(enc_in, 0)
     states_low = settle(jnp.stack([x_near, x_far]))
     small = states_low[:, seq : seq + 16].astype(F32)
@@ -899,11 +902,11 @@
     states_all, normed_all, scale_all = norm_in([states_low], g_self, seq)
     states_own = lax.dynamic_slice_in_dim(states_low, half * tq, tq, 1)
     own_blocks = jnp.stack([sc, sc_row])
-    normed_all, states_own, own_blocks, scalars, ff_own, want_near, want_far, ff_far, enc_zero, enc_in = tie(
-        normed_all, states_own, own_blocks, scalars, ff_own, want_near, want_far, ff_far, enc_zero, enc_in
-    )
-    ff = jnp.concatenate([ff_own, ff_far])
-    ff_got = move.col(ff, 1)
+    normed_all, states_own, own_blocks, scalars, want_near, want_far, ff, ff_got, enc_zero, enc_in = tie(
+        normed_all, states_own, own_blocks, scalars, want_near, want_far, ff, ff_got, enc_zero, enc_in
+    )
+    ff = jnp.concatenate([ff, ff_got])
+    ff_row = move.rows(ff, STEP_ONE)
     enc_one = move.spread(enc_in, 1)
     other_blocks = jnp.stack([sc_one, sc_two])
     ws = pick(first_core, own_blocks, other_blocks)
@@ -913,9 +916,7 @@
     self_args = ((qkv, 0, True), (qkv, heads), (qkv, 2 * heads))
     self_args = ((qkv, 0, True), (qkv, heads), (qkv, 2 * heads))
     attended, totals_self = attend_forward(info, *self_args, True)
-    attended, enc_one, ff, ff_got = tie(attended, enc_one, ff, ff_got)
-    ff = jnp.concatenate([ff, ff_got])
-    ff_row = move.rows(ff, STEP_ONE)
+    attended, enc_one, ff, ff_row = tie(attended, enc_one, ff, ff_row)
     ff_one = move.rows(ff, SAME_TWO)
     enc_all = settle(jnp.stack([enc_zero, enc_one]))
     branch = combine(ws, attended, 3 * hw, 4 * hw)

time: 615 us -> 599 us (0.974)
  waiting for transfers between devices: 170 us -> 145 us
    ppermute x15, waiting for transfers between devices: 40.2 us -> 26.2 us  [rows(): return lax.ppermute(x, ('dp', 'row'), perm)]
    ppermute x12, waiting for transfers between devices: 81.9 us -> 73.6 us  [col(): return lax.ppermute(x, 'col', [(i, i ^ bit) for i in range(4)])]
    unnamed x240 -> x238, local copies, waits for them, and re-layouts: 45.6 us -> 49.1 us
  transfers between devices with their start and end apart: 67 -> 67, of which waited for: 33 -> 31; matrix products, arithmetic and copies ran while one was open for 7% -> 9% of each run, Pallas kernels for 29% -> 29%
where the time goes in v4:
time: 599 us; the launch traced here: 593 us
  Pallas kernels  216 us (36%)
  waiting for transfers between devices  145 us (24%)
  starting transfers between devices  104 us (17%)
  local copies, waits for them, and re-layouts  61.1 us (10%)
  other arithmetic  49.4 us (8%)
  between operations  18 us (3%)
    ppermute x12, waiting for transfers between devices, col(): return lax.ppermute(x, 'col', [(i, i ^ bit) for i in range(4)])  73.6 us
    unnamed x238, local copies, waits for them, and re-layouts  49.1 us
    pallas_call x2, Pallas kernels, vocab_forward(): pl.pallas_call(body, out_shape=(jax.ShapeDtypeStruct((chunks, width, step...  33.9 us
    pallas_call x2, Pallas kernels, attend_backward(): pl.pallas_call(body, out_shape=(jax.ShapeDtypeStruct((blocks, heads * HEA...  33.3 us
    ppermute x15, starting transfers between devices, rows(): return lax.ppermute(x, ('dp', 'row'), perm)  32.1 us
    pallas_call x2, Pallas kernels, vocab_hidden_grad(): pl.pallas_call(body, out_shape=(jax.ShapeDtypeStruct((chunks, width, step...  30.7 us
    ppermute x15, waiting for transfers between devices, rows(): return lax.ppermute(x, ('dp', 'row'), perm)  26.2 us
    ppermute x5, starting transfers between devices, cols(): return lax.ppermute(x, ('dp', 'col'), perm)  23.6 us
  transfers between devices with their start and end apart: 67, of which 31 were waited for; matrix products, arithmetic and copies ran while one was open for 9% of the time, Pallas kernels for 29%

profile of v4, /device:TPU:0, one launch (start us, length us, event | category | flops | bytes accessed | tf_op | source)
XLA Modules:
  0.0 593.2 jit_solution(14493765976192837758)
XLA Ops:
  10.7 5.1 collective-permute-start.2
  30.4 10.7 %collective-permute-done = bf16[192,768]{1,0:T(8,128)(2,1)} collective-permute-done((bf16[192,768]{1,0:T(8,128)(2,1)S(1)}, bf16[192,768]{1,0:T(8,128)(2,1)}, u32[]{:S(2)}, u32[]{:S(2)}) %collective-permute-start) | collective-permute-done | bytes 294944 | tf_op jit(solution)/shard_map/ppermute | solution.py:698
  46.1 12.3 %collective-permute-done.4 = bf16[192,1152]{1,0:T(8,128)(2,1)} collective-permute-done((bf16[192,1152]{1,0:T(8,128)(2,1)S(1)}, bf16[192,1152]{1,0:T(8,128)(2,1)}, u32[]{:S(2)}, u32[]{:S(2)}) %collective-permute-start.4) | collective-permute-done | bytes 442400 | tf_op jit(solution)/shard_map/ppermute | solution.py:725
  58.4 6.4 %collective-permute-start.6 = (bf16[192,768]{1,0:T(8,128)(2,1)}, bf16[192,768]{1,0:T(8,128)(2,1)S(1)}, u32[]{:S(2)}, u32[]{:S(2)}) collective-permute-start(bf16[192,768]{1,0:T(8,128)(2,1)} %maximum_select_fusion.2), channel_id=1, source_target_pairs={{0,2},{1,3},{2,0},{3,1},{4,6},{5,7},{6,4},{7,5},{8,10},{9,11},{10,... | collective-permute-start | bytes 884744 | tf_op jit(solution)/shard_map/ppermute | solution.py:698
  65.3 12.9 %collective-permute-done.6 = bf16[192,768]{1,0:T(8,128)(2,1)S(1)} collective-permute-done((bf16[192,768]{1,0:T(8,128)(2,1)}, bf16[192,768]{1,0:T(8,128)(2,1)S(1)}, u32[]{:S(2)}, u32[]{:S(2)}) %collective-permute-start.6) | collective-permute-done | bytes 294944 | tf_op jit(solution)/shard_map/ppermute | solution.py:698
  83.0 4.4 collective-permute-start.13
  97.1 8.8 %collective-permute-done.11 = bf16[384,768]{1,0:T(8,128)(2,1)S(1)} collective-permute-done((bf16[384,768]{1,0:T(8,128)(2,1)S(1)}, bf16[384,768]{1,0:T(8,128)(2,1)S(1)}, u32[]{:S(2)}, u32[]{:S(2)}) %collective-permute-start.11) | collective-permute-done | bytes 589856 | tf_op jit(solution)/shard_map/ppermute | solution.py:698
  107.1 14.5 %collective-permute-done.14 = bf16[768,768]{1,0:T(8,128)(2,1)S(1)} collective-permute-done((bf16[768,768]{1,0:T(8,128)(2,1)}, bf16[768,768]{1,0:T(8,128)(2,1)S(1)}, u32[]{:S(2)}, u32[]{:S(2)}) %collective-permute-start.14) | collective-permute-done | bytes 1179680 | tf_op jit(solution)/shard_map/ppermute | solution.py:717
  126.8 8.1 %shard_map.349 = (bf16[2,192,512]{2,1,0:T(8,128)(2,1)S(1)}, f32[6,1,512]{2,1,0:T(1,128)S(1)}) custom-call(s32[3]{0:T(128)S(1)} %pad_add_fusion.2.s_ref.refs_0_, bf16[2,576,1024]{2,1,0:T(8,128)(2,1)S(1)} %shard_map.348.q_ref.k_ref.v_ref, bf16[2,576,1024]{2,1,0:T(8,128)(2,1)S(1)} %shard_map.348.q_ref.k_ref.v_ref, ...), custom_call_target="tpu_custom_call" | custom-call | tf_op jit(solution)/shard_map/pallas_call | solution.py:69
  147.5 5.3 collective-permute-done.19.refs_2_
  154.8 13.5 %shard_map.354 = (bf16[2,192,512]{2,1,0:T(8,128)(2,1)S(1)}, f32[6,1,512]{2,1,0:T(1,128)S(1)}) custom-call(s32[3]{0:T(128)S(1)} %pad_add_fusion.2.s_ref.refs_0_, bf16[2,192,512]{2,1,0:T(8,128)(2,1)S(1)} %shard_map.352.q_ref, bf16[2,384,2048]{2,1,0:T(8,128)(2,1)S(1)} %shard_map.353.k_ref.v_ref, bf16[2,384,2048]{2,1,0:T(8,128)(2,1)S(1)} %shard_map.353.k_ref.v_ref), custom_call_target="tpu_custom_call" | custom-call | tf_op jit(solution)/shard_map/pallas_call | solution.py:69
  175.9 6.5 %shard_map.357 = (bf16[512,512]{1,0:T(8,128)(2,1)S(1)}, bf16[512,512]{1,0:T(8,128)(2,1)S(1)}, bf16[512,512]{1,0:T(8,128)(2,1)S(1)}, bf16[512,512]{1,0:T(8,128)(2,1)S(1)}, f32[768,512]{1,0:T(8,128)}) custom-call(bf16[768,768]{1,0:T(8,128)(2,1)S(1)} %constant_dynamic-update-slice_fusion.2.refs_0_, bf16[768,768]{1,0:T(8,128)(2,1)S(1)} %collective-permute-done.16.refs_1_, ...), custom_call_target="tpu_custom_call" | custom-call | tf_op jit(solution)/shard_map/pallas_call | solution.py:171
  194.6 18.7 %collective-permute-done.23 = bf16[768,256]{1,0:T(8,128)(2,1)S(1)} collective-permute-done((bf16[768,256]{1,0:T(8,128)(2,1)S(1)}, bf16[768,256]{1,0:T(8,128)(2,1)S(1)}, u32[]{:S(2)}, u32[]{:S(2)}) %collective-permute-start.23) | collective-permute-done | bytes 393248 | tf_op jit(solution)/shard_map/ppermute | solution.py:698
  215.8 16.8 %shard_map.359 = (bf16[4,4096,256]{2,1,0:T(8,128)(2,1)}, f32[8,4,256]{2,1,0:T(4,128)S(1)}, f32[3,4,256]{2,1,0:T(4,128)S(1)}) custom-call(s32[2]{0:T(128)S(1)} %pad_add_fusion.s_ref, bf16[2,768,256]{2,1,0:T(8,128)(2,1)S(1)} %pad_maximum_fusion.12.h0_ref.refs_1_, bf16[2,768,256]{2,1,0:T(8,128)(2,1)} %collective-permute-done.26.h1_ref.refs_2_, ...), custom_call_target="tpu_custom_call" | custom-call | tf_op jit(solution)/shard_map/pallas_call | solution.py:519
  236.0 17.1 %shard_map.360 = (bf16[4,4096,256]{2,1,0:T(8,128)(2,1)}, f32[8,4,256]{2,1,0:T(4,128)S(1)}, f32[3,4,256]{2,1,0:T(4,128)S(1)}) custom-call(s32[2]{0:T(128)S(1)} %pad_add_fusion.s_ref, bf16[2,768,256]{2,1,0:T(8,128)(2,1)} %collective-permute-done.25.h0_ref.refs_3_, bf16[2,768,256]{2,1,0:T(8,128)(2,1)S(1)} %collective-permute-done.27.h1_ref.refs_4_, ...), custom_call_target="tpu_custom_call" | custom-call | tf_op jit(solution)/shard_map/pallas_call | solution.py:519
  265.7 15.3 %shard_map.363 = (bf16[4,4096,256]{2,1,0:T(8,128)(2,1)}, bf16[2,768,256]{2,1,0:T(8,128)(2,1)}, bf16[2,768,256]{2,1,0:T(8,128)(2,1)}) custom-call(s32[2]{0:T(128)} %copy-done.83, bf16[4,4096,256]{2,1,0:T(8,128)(2,1)} %get-tuple-element.248.e_ref, f32[8,4,256]{2,1,0:T(4,128)} %copy-done.77, f32[8,256]{1,0:T(8,128)} %copy-done.78, ...), custom_call_target="tpu_custom_call", output_to_operand_aliasing={{0}: (1, {})} | custom-call | tf_op jit(solution)/shard_map/pallas_call | solution.py:573
  284.9 15.4 %shard_map.364 = (bf16[4,4096,256]{2,1,0:T(8,128)(2,1)}, bf16[2,768,256]{2,1,0:T(8,128)(2,1)}, bf16[2,768,256]{2,1,0:T(8,128)(2,1)}) custom-call(s32[2]{0:T(128)} %copy-done.83, bf16[4,4096,256]{2,1,0:T(8,128)(2,1)} %get-tuple-element.254.e_ref, f32[8,4,256]{2,1,0:T(4,128)} %copy-done.76, f32[8,256]{1,0:T(8,128)} %copy-done.78, ...), custom_call_target="tpu_custom_call", output_to_operand_aliasing={{0}: (1, {})} | custom-call | tf_op jit(solution)/shard_map/pallas_call | solution.py:573
  302.8 17.5 %collective-permute-done.36 = bf16[2,768,256]{2,1,0:T(8,128)(2,1)S(1)} collective-permute-done((bf16[2,768,256]{2,1,0:T(8,128)(2,1)S(1)}, bf16[2,768,256]{2,1,0:T(8,128)(2,1)S(1)}, u32[]{:S(2)}, u32[]{:S(2)}) %collective-permute-start.36) | collective-permute-done | bytes 786464 | tf_op jit(solution)/shard_map/ppermute | solution.py:698
  324.7 18.3 %shard_map.365 = bf16[768,4096]{1,0:T(8,128)(2,1)} custom-call(s32[8]{0:T(128)S(1)} %copy-done.89, bf16[2,768,256]{2,1,0:T(8,128)(2,1)S(1)} %pad_maximum_fusion.12.h0_ref.refs_1_, bf16[2,768,256]{2,1,0:T(8,128)(2,1)} %collective-permute-done.26.h1_ref.refs_2_, bf16[2,768,256]{2,1,0:T(8,128)(2,1)} %collective-permute-done.25.h0_ref.refs_3_, ...), custom_call_target="tpu_custom_call" | custom-call | tf_op jit(solution)/shard_map/pallas_call | solution.py:619
  352.7 12.9 %shard_map.367 = (bf16[4,768,768]{2,1,0:T(8,128)(2,1)}, f32[768,512]{1,0:T(8,128)}) custom-call(s32[8]{0:T(128)} %stack.235.s_ref, bf16[768,768]{1,0:T(8,128)(2,1)} %copy-done.12, bf16[768,768]{1,0:T(8,128)(2,1)} %copy-done.24, bf16[768,768]{1,0:T(8,128)(2,1)} %copy-done.97, bf16[768,768]{1,0:T(8,128)(2,1)} %collective-permute-done.20.refs_3_, ...), custom_call_target="tpu_custom_call" | custom-call | tf_op jit(solution)/shard_map/pallas_call | solution.py:206
  378.0 21.0 %shard_map.370 = (bf16[2,192,512]{2,1,0:T(8,128)(2,1)S(1)}, bf16[2,192,2048]{2,1,0:T(8,128)(2,1)S(1)}, bf16[2,192,2048]{2,1,0:T(8,128)(2,1)S(1)}) custom-call(s32[3]{0:T(128)S(1)} %pad_add_fusion.2.s_ref.refs_0_, bf16[2,192,512]{2,1,0:T(8,128)(2,1)S(1)} %copy-done.32, bf16[2,384,2048]{2,1,0:T(8,128)(2,1)} %copy-done.2, bf16[2,384,2048]{2,1,0:T(8,128)(2,1)} %copy-done.2, ...), custom_call_target="tpu_custom_call" | custom-call | tf_op jit(solution)/shard_map/pallas_call | solution.py:113
  400.9 4.6 shard_map.372
  420.5 10.8 %shard_map.374 = (bf16[768,768]{1,0:T(8,128)(2,1)}, bf16[768,768]{1,0:T(8,128)(2,1)}) custom-call(s32[3]{0:T(128)S(1)} %pad_add_fusion.2.s_ref.refs_0_, bf16[768,512]{1,0:T(8,128)(2,1)S(1)} %copy-done.34, bf16[768,2048]{1,0:T(8,128)(2,1)} %copy-done.6, bf16[768,2048]{1,0:T(8,128)(2,1)} %copy-done.6, bf16[768,512]{1,0:T(8,128)(2,1)S(1)} %copy-done.36, ...), custom_call_target="tpu_custom_call" | custom-call | tf_op jit(solution)/shard_map/pallas_call | solution.py:382
  432.9 5.4 collective-permute-start.43
  447.5 7.4 %collective-permute-start.45 = (bf16[192,2048]{1,0:T(8,128)(2,1)}, bf16[192,2048]{1,0:T(8,128)(2,1)}, u32[]{:S(2)}, u32[]{:S(2)}) collective-permute-start(bf16[192,2048]{1,0:T(8,128)(2,1)} %get-tuple-element.347), channel_id=1, source_target_pairs={{0,0},{1,1},{16,2},{17,3},{2,16},{3,17},{18,18},{19,19},{4,4},{5,5... | collective-permute-start | bytes 2359304 | tf_op jit(solution)/shard_map/ppermute | solution.py:725
  454.9 12.3 %shard_map.376 = (bf16[2,192,512]{2,1,0:T(8,128)(2,1)S(1)}, bf16[2,192,1024]{2,1,0:T(8,128)(2,1)S(1)}, bf16[2,192,1024]{2,1,0:T(8,128)(2,1)S(1)}) custom-call(s32[3]{0:T(128)S(1)} %pad_add_fusion.2.s_ref.refs_0_, bf16[2,576,1024]{2,1,0:T(8,128)(2,1)S(1)} %shard_map.348.q_ref.k_ref.v_ref, bf16[2,576,1024]{2,1,0:T(8,128)(2,1)S(1)} %shard_map.348.q_ref.k_ref.v_ref, ...), custom_call_target="tpu_custom_call" | custom-call | tf_op jit(solution)/shard_map/pallas_call | solution.py:113
  475.6 7.1 %shard_map.377 = (bf16[768,768]{1,0:T(8,128)(2,1)}, bf16[768,768]{1,0:T(8,128)(2,1)}) custom-call(s32[3]{0:T(128)S(1)} %pad_add_fusion.2.s_ref.refs_0_, bf16[768,1024]{1,0:T(8,128)(2,1)} %copy-done.9, bf16[768,1024]{1,0:T(8,128)(2,1)} %copy-done.9, bf16[768,1024]{1,0:T(8,128)(2,1)} %copy-done.9, bf16[768,512]{1,0:T(8,128)(2,1)S(1)} %get-tuple-element.284.x_ref.refs_4_, ...), custom_call_target="tpu_custom_call" | custom-call | tf_op jit(solution)/shard_map/pallas_call | solution.py:382
  487.9 4.0 add_convert_fusion.4
  513.2 5.1 collective-permute-start.63
  532.1 6.8 %collective-permute-start.57 = (bf16[192,768]{1,0:T(8,128)(2,1)S(1)}, bf16[192,768]{1,0:T(8,128)(2,1)S(1)}, u32[]{:S(2)}, u32[]{:S(2)}) collective-permute-start(bf16[192,768]{1,0:T(8,128)(2,1)S(1)} %get-tuple-element.320), channel_id=1, source_target_pairs={{0,2},{1,3},{2,0},{3,1},{4,6},{5,7},{6,4},{7,5},{8,10},{9,11},{10,... | collective-permute-start | bytes 884744 | tf_op jit(solution)/shard_map/ppermute | solution.py:705
  542.7 10.7 %collective-permute-start.59 = (bf16[192,768]{1,0:T(8,128)(2,1)S(1)}, bf16[192,768]{1,0:T(8,128)(2,1)}, u32[]{:S(2)}, u32[]{:S(2)}) collective-permute-start(bf16[192,768]{1,0:T(8,128)(2,1)S(1)} %get-tuple-element.322), channel_id=1, source_target_pairs={{0,3},{1,2},{2,1},{3,0},{4,7},{5,6},{6,5},{7,4},{8,11},{9,10},{10,... | collective-permute-start | bytes 884744 | tf_op jit(solution)/shard_map/ppermute | solution.py:705
  554.8 13.4 %collective-permute-done.57 = bf16[192,768]{1,0:T(8,128)(2,1)S(1)} collective-permute-done((bf16[192,768]{1,0:T(8,128)(2,1)S(1)}, bf16[192,768]{1,0:T(8,128)(2,1)S(1)}, u32[]{:S(2)}, u32[]{:S(2)}) %collective-permute-start.57) | collective-permute-done | bytes 294944 | tf_op jit(solution)/shard_map/ppermute | solution.py:705
  (484 shorter events, 226.2 us)
Async XLA Ops:
  7.2 462.6 %reduce-scatter.4.cloned.1.call-start = ((), (), s32[]{:S(2)}) async-start(), calls=%async_computation.3 | async-start | bytes 7864320 | tf_op jit(solution)/shard_map/reduce_scatter | solution.py:984
  15.8 25.2 %collective-permute-start = (bf16[192,768]{1,0:T(8,128)(2,1)S(1)}, bf16[192,768]{1,0:T(8,128)(2,1)}, u32[]{:S(2)}, u32[]{:S(2)}) collective-permute-start(bf16[192,768]{1,0:T(8,128)(2,1)S(1)} %maximum_select_fusion.1), channel_id=1, source_target_pairs={{0,2},{1,3},{2,0},{3,1},{4,6},{5,7},{6,4},{7,5},{8,10},{9,11},{10,... | collective-permute-start | bytes 884744 | tf_op jit(solution)/shard_map/ppermute | solution.py:698
  18.9 59.3 %collective-permute-start.8 = (bf16[192,4096]{1,0:T(8,128)(2,1)S(1)}, bf16[192,4096]{1,0:T(8,128)(2,1)S(1)}, u32[]{:S(2)}, u32[]{:S(2)}) collective-permute-start(bf16[192,4096]{1,0:T(8,128)(2,1)S(1)} %fusion.own_ref), channel_id=1, source_target_pairs={{0,8},{4,12},{8,0},{12,4},{16,20},{20,16},{24,28},{28,24},{1,9},{5... | collective-permute-start | bytes 4718600 | tf_op jit(solution)/shard_map/ppermute | solution.py:717
  20.6 57.6 %collective-permute-start.7 = (bf16[192,4096]{1,0:T(8,128)(2,1)S(1)}, bf16[192,4096]{1,0:T(8,128)(2,1)}, u32[]{:S(2)}, u32[]{:S(2)}) collective-permute-start(bf16[192,4096]{1,0:T(8,128)(2,1)S(1)} %fusion.own_ref), channel_id=1, source_target_pairs={{0,4},{4,0},{8,12},{12,8},{16,24},{20,28},{24,16},{28,20},{1,5},{5... | collective-permute-start | bytes 4718600 | tf_op jit(solution)/shard_map/ppermute | solution.py:717
  43.2 34.9 %collective-permute-start.5 = (bf16[768,768]{1,0:T(8,128)(2,1)}, bf16[768,768]{1,0:T(8,128)(2,1)}, u32[]{:S(2)}, u32[]{:S(2)}) collective-permute-start(bf16[768,768]{1,0:T(8,128)(2,1)} %pad_maximum_fusion.8), channel_id=1, source_target_pairs={{0,4},{4,0},{8,12},{12,8},{16,24},{20,28},{24,16},{28,20},{1,5},{5... | collective-permute-start | bytes 3538952 | tf_op jit(solution)/shard_map/ppermute | solution.py:717
  58.4 19.7 %collective-permute-start.6 = (bf16[192,768]{1,0:T(8,128)(2,1)}, bf16[192,768]{1,0:T(8,128)(2,1)S(1)}, u32[]{:S(2)}, u32[]{:S(2)}) collective-permute-start(bf16[192,768]{1,0:T(8,128)(2,1)} %maximum_select_fusion.2), channel_id=1, source_target_pairs={{0,2},{1,3},{2,0},{3,1},{4,6},{5,7},{6,4},{7,5},{8,10},{9,11},{10,... | collective-permute-start | bytes 884744 | tf_op jit(solution)/shard_map/ppermute | solution.py:698
  82.2 23.8 %collective-permute-start.11 = (bf16[384,768]{1,0:T(8,128)(2,1)S(1)}, bf16[384,768]{1,0:T(8,128)(2,1)S(1)}, u32[]{:S(2)}, u32[]{:S(2)}) collective-permute-start(bf16[384,768]{1,0:T(8,128)(2,1)S(1)} %constant_dynamic-update-slice_fusion), channel_id=1, source_target_pairs={{0,1},{1,0},{2,3},{3,2},{4,5},{5,4},{6,7},{7,6},{8,9},{9,8},{10,11... | collective-permute-start | bytes 1769480 | tf_op jit(solution)/shard_map/ppermute | solution.py:698
  82.3 23.7 %collective-permute-start.12 = (bf16[192,2048]{1,0:T(8,128)(2,1)S(1)}, bf16[192,2048]{1,0:T(8,128)(2,1)S(1)}, u32[]{:S(2)}, u32[]{:S(2)}) collective-permute-start(bf16[192,2048]{1,0:T(8,128)(2,1)S(1)} %copy-done.116), channel_id=1, source_target_pairs={{0,0},{1,1},{2,16},{3,17},{16,2},{17,3},{18,18},{19,19},{4,4},{5,5... | collective-permute-start | bytes 2359304 | tf_op jit(solution)/shard_map/ppermute | solution.py:725
  83.0 24.1 %collective-permute-start.13 = (bf16[768,768]{1,0:T(8,128)(2,1)}, bf16[768,768]{1,0:T(8,128)(2,1)}, u32[]{:S(2)}, u32[]{:S(2)}) collective-permute-start(bf16[768,768]{1,0:T(8,128)(2,1)} %pad_maximum_fusion.8), channel_id=1, source_target_pairs={{0,24},{4,28},{8,16},{12,20},{16,4},{20,0},{24,12},{28,8},{1,25},{... | collective-permute-start | bytes 3538952 | tf_op jit(solution)/shard_map/ppermute | solution.py:717
  87.4 34.2 %collective-permute-start.14 = (bf16[768,768]{1,0:T(8,128)(2,1)}, bf16[768,768]{1,0:T(8,128)(2,1)S(1)}, u32[]{:S(2)}, u32[]{:S(2)}) collective-permute-start(bf16[768,768]{1,0:T(8,128)(2,1)} %collective-permute-done.5), channel_id=1, source_target_pairs={{0,24},{4,28},{8,16},{12,20},{16,4},{20,0},{24,12},{28,8},{1,25},{... | collective-permute-start | bytes 3538952 | tf_op jit(solution)/shard_map/ppermute | solution.py:717
  106.1 28.9 %collective-permute-start.16 = (bf16[768,768]{1,0:T(8,128)(2,1)S(1)}, bf16[768,768]{1,0:T(8,128)(2,1)S(1)}, u32[]{:S(2)}, u32[]{:S(2)}) collective-permute-start(bf16[768,768]{1,0:T(8,128)(2,1)S(1)} %constant_dynamic-update-slice_fusion.2.refs_0_), channel_id=1, source_target_pairs={{0,4},{4,0},{8,12},{12,8},{16,24},{20,28},{24,16},{28,20},{1,5},{5... | collective-permute-start | bytes 3538952 | tf_op jit(solution)/shard_map/ppermute | solution.py:717
  107.1 27.8 %collective-permute-start.15 = (bf16[192,2048]{1,0:T(8,128)(2,1)S(1)}, bf16[192,2048]{1,0:T(8,128)(2,1)S(1)}, u32[]{:S(2)}, u32[]{:S(2)}) collective-permute-start(bf16[192,2048]{1,0:T(8,128)(2,1)S(1)} %copy-done.116), channel_id=1, source_target_pairs={{0,1},{1,0},{2,17},{3,16},{16,3},{17,2},{18,19},{19,18},{4,5},{5,4... | collective-permute-start | bytes 2359304 | tf_op jit(solution)/shard_map/ppermute | solution.py:725
  185.8 27.6 %collective-permute-start.24 = (bf16[192,4096]{1,0:T(8,128)(2,1)}, bf16[192,4096]{1,0:T(8,128)(2,1)}, u32[]{:S(2)}, u32[]{:S(2)}) collective-permute-start(bf16[192,4096]{1,0:T(8,128)(2,1)} %collective-permute-done.7.one_ref), channel_id=1, source_target_pairs={{0,8},{4,12},{8,0},{12,4},{16,20},{20,16},{24,28},{28,24},{1,9},{5... | collective-permute-start | bytes 4718600 | tf_op jit(solution)/shard_map/ppermute | solution.py:717
  213.5 20.0 %collective-permute-start.25 = (bf16[2,768,256]{2,1,0:T(8,128)(2,1)S(1)}, bf16[2,768,256]{2,1,0:T(8,128)(2,1)}, u32[]{:S(2)}, u32[]{:S(2)}) collective-permute-start(bf16[2,768,256]{2,1,0:T(8,128)(2,1)S(1)} %pad_maximum_fusion.12.h0_ref.refs_1_), channel_id=1, source_target_pairs={{0,1},{1,0},{2,3},{3,2},{4,5},{5,4},{6,7},{7,6},{8,9},{9,8},{10,11... | collective-permute-start | bytes 2359304 | tf_op jit(solution)/shard_map/ppermute | solution.py:698
  300.5 19.8 %collective-permute-start.36 = (bf16[2,768,256]{2,1,0:T(8,128)(2,1)S(1)}, bf16[2,768,256]{2,1,0:T(8,128)(2,1)S(1)}, u32[]{:S(2)}, u32[]{:S(2)}) collective-permute-start(bf16[2,768,256]{2,1,0:T(8,128)(2,1)S(1)} %add_convert_fusion.2), channel_id=1, source_target_pairs={{0,1},{1,0},{2,3},{3,2},{4,5},{5,4},{6,7},{7,6},{8,9},{9,8},{10,11... | collective-permute-start | bytes 2359304 | tf_op jit(solution)/shard_map/ppermute | solution.py:698
  323.6 20.2 %collective-permute-start.37 = (bf16[768,256]{1,0:T(8,128)(2,1)}, bf16[768,256]{1,0:T(8,128)(2,1)}, u32[]{:S(2)}, u32[]{:S(2)}) collective-permute-start(bf16[768,256]{1,0:T(8,128)(2,1)} %fusion.9), channel_id=1, source_target_pairs={{0,2},{1,3},{2,0},{3,1},{4,6},{5,7},{6,4},{7,5},{8,10},{9,11},{10,... | collective-permute-start | bytes 1179656 | tf_op jit(solution)/shard_map/ppermute | solution.py:698
  343.9 151.9 %reduce-scatter.6.cloned.1.call-start = ((), (), s32[]{:S(2)}) async-start(), calls=%async_computation.4 | async-start | bytes 5898240 | tf_op jit(solution)/shard_map/reduce_scatter | solution.py:996
  365.6 207.3 %reduce-scatter.8.cloned.1.call-start = ((), (), s32[]{:S(2)}) async-start(), calls=%async_computation.5 | async-start | bytes 1474560 | tf_op jit(solution)/shard_map/reduce_scatter | solution.py:1037
  431.2 41.1 %collective-permute-start.44 = (bf16[768,768]{1,0:T(8,128)(2,1)}, bf16[768,768]{1,0:T(8,128)(2,1)}, u32[]{:S(2)}, u32[]{:S(2)}) collective-permute-start(bf16[768,768]{1,0:T(8,128)(2,1)} %get-tuple-element.291), channel_id=1, source_target_pairs={{16,24},{20,28},{24,16},{28,20},{17,25},{21,29},{25,17},{29,21},{1... | collective-permute-start | bytes 3538952 | tf_op jit(solution)/shard_map/ppermute | solution.py:717
  432.9 39.4 %collective-permute-start.43 = (bf16[768,768]{1,0:T(8,128)(2,1)}, bf16[768,768]{1,0:T(8,128)(2,1)}, u32[]{:S(2)}, u32[]{:S(2)}) collective-permute-start(bf16[768,768]{1,0:T(8,128)(2,1)} %get-tuple-element.291), channel_id=1, source_target_pairs={{0,28},{4,24},{8,20},{12,16},{1,29},{5,25},{9,21},{13,17},{2,30},{... | collective-permute-start | bytes 3538952 | tf_op jit(solution)/shard_map/ppermute | solution.py:717
  438.3 34.0 %collective-permute-start.42 = (bf16[768,768]{1,0:T(8,128)(2,1)}, bf16[768,768]{1,0:T(8,128)(2,1)}, u32[]{:S(2)}, u32[]{:S(2)}) collective-permute-start(bf16[768,768]{1,0:T(8,128)(2,1)} %get-tuple-element.290), channel_id=1, source_target_pairs={{0,20},{4,16},{8,28},{12,24},{1,21},{5,17},{9,29},{13,25},{2,22},{... | collective-permute-start | bytes 3538952 | tf_op jit(solution)/shard_map/ppermute | solution.py:717
  444.7 48.9 %collective-permute-start.46 = (bf16[192,2048]{1,0:T(8,128)(2,1)}, bf16[192,2048]{1,0:T(8,128)(2,1)}, u32[]{:S(2)}, u32[]{:S(2)}) collective-permute-start(bf16[192,2048]{1,0:T(8,128)(2,1)} %get-tuple-element.346), channel_id=1, source_target_pairs={{1,0},{0,1},{17,2},{16,3},{3,16},{2,17},{19,18},{18,19},{5,4},{4,5... | collective-permute-start | bytes 2359304 | tf_op jit(solution)/shard_map/ppermute | solution.py:725
  447.5 64.7 %collective-permute-start.45 = (bf16[192,2048]{1,0:T(8,128)(2,1)}, bf16[192,2048]{1,0:T(8,128)(2,1)}, u32[]{:S(2)}, u32[]{:S(2)}) collective-permute-start(bf16[192,2048]{1,0:T(8,128)(2,1)} %get-tuple-element.347), channel_id=1, source_target_pairs={{0,0},{1,1},{16,2},{17,3},{2,16},{3,17},{18,18},{19,19},{4,4},{5,5... | collective-permute-start | bytes 2359304 | tf_op jit(solution)/shard_map/ppermute | solution.py:725
  482.7 38.6 %collective-permute-start.49 = (bf16[768,768]{1,0:T(8,128)(2,1)}, bf16[768,768]{1,0:T(8,128)(2,1)}, u32[]{:S(2)}, u32[]{:S(2)}) collective-permute-start(bf16[768,768]{1,0:T(8,128)(2,1)} %get-tuple-element.310), channel_id=1, source_target_pairs={{16,12},{20,8},{24,4},{28,0},{17,13},{21,9},{25,5},{29,1},{18,14},... | collective-permute-start | bytes 3538952 | tf_op jit(solution)/shard_map/ppermute | solution.py:717
  484.1 37.2 %collective-permute-start.47 = (bf16[768,768]{1,0:T(8,128)(2,1)}, bf16[768,768]{1,0:T(8,128)(2,1)}, u32[]{:S(2)}, u32[]{:S(2)}) collective-permute-start(bf16[768,768]{1,0:T(8,128)(2,1)} %get-tuple-element.310), channel_id=1, source_target_pairs={{0,4},{4,0},{8,12},{12,8},{1,5},{5,1},{9,13},{13,9},{2,6},{6,2},{1... | collective-permute-start | bytes 3538952 | tf_op jit(solution)/shard_map/ppermute | solution.py:717
  491.9 26.4 %collective-permute-start.50 = (bf16[384,768]{1,0:T(8,128)(2,1)}, bf16[384,768]{1,0:T(8,128)(2,1)}, u32[]{:S(2)}, u32[]{:S(2)}) collective-permute-start(bf16[384,768]{1,0:T(8,128)(2,1)} %get-tuple-element.342), channel_id=1, source_target_pairs={{16,17},{17,16},{18,19},{19,18},{20,21},{21,20},{22,23},{23,22},{2... | collective-permute-start | bytes 1769480 | tf_op jit(solution)/shard_map/ppermute | solution.py:705
  493.5 27.8 %collective-permute-start.48 = (bf16[768,768]{1,0:T(8,128)(2,1)}, bf16[768,768]{1,0:T(8,128)(2,1)}, u32[]{:S(2)}, u32[]{:S(2)}) collective-permute-start(bf16[768,768]{1,0:T(8,128)(2,1)} %get-tuple-element.312.refs_0_), channel_id=1, source_target_pairs={{16,8},{20,12},{24,0},{28,4},{17,9},{21,13},{25,1},{29,5},{18,10},... | collective-permute-start | bytes 3538952 | tf_op jit(solution)/shard_map/ppermute | solution.py:717
  525.3 28.1 %collective-permute-start.53 = (bf16[192,1152]{1,0:T(8,128)(2,1)S(1)}, bf16[192,1152]{1,0:T(8,128)(2,1)S(1)}, u32[]{:S(2)}, u32[]{:S(2)}) collective-permute-start(bf16[192,1152]{1,0:T(8,128)(2,1)S(1)} %get-tuple-element.359), channel_id=1, source_target_pairs={{1,0},{0,1},{17,2},{16,3},{3,16},{2,17},{19,18},{18,19},{5,4},{4,5... | collective-permute-start | bytes 1327112 | tf_op jit(solution)/shard_map/ppermute | solution.py:725
  528.4 46.0 %collective-permute-start.61 = (bf16[192,768]{1,0:T(8,128)(2,1)}, bf16[192,768]{1,0:T(8,128)(2,1)S(1)}, u32[]{:S(2)}, u32[]{:S(2)}) collective-permute-start(bf16[192,768]{1,0:T(8,128)(2,1)} %slice.421), channel_id=1, source_target_pairs={{16,18},{17,19},{18,16},{19,17},{20,22},{21,23},{22,20},{23,21},{2... | collective-permute-start | bytes 884744 | tf_op jit(solution)/shard_map/ppermute | solution.py:705
  532.1 36.1 %collective-permute-start.57 = (bf16[192,768]{1,0:T(8,128)(2,1)S(1)}, bf16[192,768]{1,0:T(8,128)(2,1)S(1)}, u32[]{:S(2)}, u32[]{:S(2)}) collective-permute-start(bf16[192,768]{1,0:T(8,128)(2,1)S(1)} %get-tuple-element.320), channel_id=1, source_target_pairs={{0,2},{1,3},{2,0},{3,1},{4,6},{5,7},{6,4},{7,5},{8,10},{9,11},{10,... | collective-permute-start | bytes 884744 | tf_op jit(solution)/shard_map/ppermute | solution.py:705
  538.8 30.9 %collective-permute-start.58 = (bf16[192,768]{1,0:T(8,128)(2,1)S(1)}, bf16[192,768]{1,0:T(8,128)(2,1)S(1)}, u32[]{:S(2)}, u32[]{:S(2)}) collective-permute-start(bf16[192,768]{1,0:T(8,128)(2,1)S(1)} %get-tuple-element.321), channel_id=1, source_target_pairs={{0,1},{1,0},{2,3},{3,2},{4,5},{5,4},{6,7},{7,6},{8,9},{9,8},{10,11... | collective-permute-start | bytes 884744 | tf_op jit(solution)/shard_map/ppermute | solution.py:705
  542.7 30.3 %collective-permute-start.59 = (bf16[192,768]{1,0:T(8,128)(2,1)S(1)}, bf16[192,768]{1,0:T(8,128)(2,1)}, u32[]{:S(2)}, u32[]{:S(2)}) collective-permute-start(bf16[192,768]{1,0:T(8,128)(2,1)S(1)} %get-tuple-element.322), channel_id=1, source_target_pairs={{0,3},{1,2},{2,1},{3,0},{4,7},{5,6},{6,5},{7,4},{8,11},{9,10},{10,... | collective-permute-start | bytes 884744 | tf_op jit(solution)/shard_map/ppermute | solution.py:705
  (152 other events, 1617.4 us)
Sparse Core Ops, SparseCore 0:
  344.0 68.2 reduce-scatter.3
  415.3 79.4 reduce-scatter.5
  502.5 35.4 reduce-scatter.7

commit v5 on v4

--- a/solution.py
+++ b/solution.py
@@ -166,12 +166,13 @@
             value, _ = gelu_parts(both[:wide])
             hidden = (value * both[wide:]).astype(BF)
             part = nn(w_ref[:, 2 * wide :], hidden)
-            out_ref[...] = part if b == 0 else out_ref[...] + part
+            acc = part if b == 0 else acc + part
+        out_ref[...] = acc.astype(BF)
 
     return pl.pallas_call(
         body,
         out_shape=[jax.ShapeDtypeStruct((2 * wide, tokens), BF)] * n
-        + [jax.ShapeDtypeStruct((d, tokens), F32)],
+        + [jax.ShapeDtypeStruct((d, tokens), BF)],
         compiler_params=params(48, 0),
     )(*packs, normed)
 
@@ -201,13 +202,14 @@
                 dw_ref[s_ref[b], at, : 2 * wide] = first[p * size : (p + 1) * size]
                 dw_ref[s_ref[b], at, 2 * wide :] = second[p * size : (p + 1) * size]
             part = nn(w_ref[:, : 2 * wide], grads)
-            out_ref[...] = part if b == 0 else out_ref[...] + part
+            acc = part if b == 0 else acc + part
+        out_ref[...] = acc.astype(BF)
 
     return pl.pallas_call(
         body,
         out_shape=(
             jax.ShapeDtypeStruct((n, d, lanes), BF),
-            jax.ShapeDtypeStruct((d, tokens), F32),
+            jax.ShapeDtypeStruct((d, tokens), BF),
         ),
         grid_spec=pltpu.PrefetchScalarGridSpec(
             num_scalar_prefetch=1,
@@ -229,9 +231,9 @@
         x_refs, g_ref, sum_ref, norm_ref, scale_ref = refs[:n], refs[n], *refs[n + 1 :]
         states = x_refs[0][...].astype(F32)
         if n > 1:
-            rest = x_refs[1][...]
+            rest = x_refs[1][...].astype(F32)
             for ref in x_refs[2:]:
-                rest = rest + ref[...]
+                rest = rest + ref[...].astype(F32)
             states = states + rest
         scale = lax.rsqrt(jnp.mean(states * states, axis=0, keepdims=True) + EPS)
         sum_ref[...] = states
@@ -343,7 +345,7 @@
         part = nn(w_ref[0, :, at : at + high - low], x_ref[0])
         for b in range(1, blocks):
             part += nn(w_ref[b, :, at : at + high - low], x_ref[b])
-        o_ref[...] = part
+        o_ref[...] = part.astype(BF)
 
     return pl.pallas_call(
         body,
@@ -353,7 +355,7 @@
             whole((blocks, high - low, tokens)),
         ],
         out_specs=whole((d, tokens)),
-        out_shape=jax.ShapeDtypeStruct((d, tokens), F32),
+        out_shape=jax.ShapeDtypeStruct((d, tokens), BF),
         compiler_params=params(40),
     )(pack, rows)
 

time: 599 us -> 594 us (level)
    unnamed x238 -> x232, local copies, waits for them, and re-layouts: 49.1 us -> 46.5 us
  transfers between devices with their start and end apart: 67 -> 67, of which waited for: 31 -> 31; matrix products, arithmetic and copies ran while one was open for 9% -> 8% of each run, Pallas kernels for 29% -> 30%
where the time goes in v5:
time: 594 us; the launch traced here: 588 us
  Pallas kernels  214 us (36%)
  waiting for transfers between devices  149 us (25%)
  starting transfers between devices  100 us (17%)
  local copies, waits for them, and re-layouts  58.5 us (10%)
  other arithmetic  47.8 us (8%)
  between operations  18 us (3%)
    ppermute x12, waiting for transfers between devices, col(): return lax.ppermute(x, 'col', [(i, i ^ bit) for i in range(4)])  73.7 us
    unnamed x232, local copies, waits for them, and re-layouts  46.5 us
    pallas_call x2, Pallas kernels, vocab_forward(): pl.pallas_call(body, out_shape=(jax.ShapeDtypeStruct((chunks, width, step...  33.9 us
    pallas_call x2, Pallas kernels, attend_backward(): pl.pallas_call(body, out_shape=(jax.ShapeDtypeStruct((blocks, heads * HEA...  33.3 us
    ppermute x15, starting transfers between devices, rows(): return lax.ppermute(x, ('dp', 'row'), perm)  30.8 us
    pallas_call x2, Pallas kernels, vocab_hidden_grad(): pl.pallas_call(body, out_shape=(jax.ShapeDtypeStruct((chunks, width, step...  30.8 us
    ppermute x15, waiting for transfers between devices, rows(): return lax.ppermute(x, ('dp', 'row'), perm)  30.1 us
    ppermute x5, starting transfers between devices, cols(): return lax.ppermute(x, ('dp', 'col'), perm)  23.6 us
  transfers between devices with their start and end apart: 67, of which 31 were waited for; matrix products, arithmetic and copies ran while one was open for 8% of the time, Pallas kernels for 30%

profile of v5, /device:TPU:0, one launch (start us, length us, event | category | flops | bytes accessed | tf_op | source)
XLA Modules:
  0.0 587.7 jit_solution(3694673427382452081)
XLA Ops:
  10.7 5.1 collective-permute-start.2
  30.4 10.7 %collective-permute-done = bf16[192,768]{1,0:T(8,128)(2,1)} collective-permute-done((bf16[192,768]{1,0:T(8,128)(2,1)S(1)}, bf16[192,768]{1,0:T(8,128)(2,1)}, u32[]{:S(2)}, u32[]{:S(2)}) %collective-permute-start) | collective-permute-done | bytes 294944 | tf_op jit(solution)/shard_map/ppermute | solution.py:700
  46.1 12.3 %collective-permute-done.4 = bf16[192,1152]{1,0:T(8,128)(2,1)} collective-permute-done((bf16[192,1152]{1,0:T(8,128)(2,1)S(1)}, bf16[192,1152]{1,0:T(8,128)(2,1)}, u32[]{:S(2)}, u32[]{:S(2)}) %collective-permute-start.4) | collective-permute-done | bytes 442400 | tf_op jit(solution)/shard_map/ppermute | solution.py:727
  58.4 6.4 %collective-permute-start.6 = (bf16[192,768]{1,0:T(8,128)(2,1)}, bf16[192,768]{1,0:T(8,128)(2,1)S(1)}, u32[]{:S(2)}, u32[]{:S(2)}) collective-permute-start(bf16[192,768]{1,0:T(8,128)(2,1)} %maximum_select_fusion.2), channel_id=1, source_target_pairs={{0,2},{1,3},{2,0},{3,1},{4,6},{5,7},{6,4},{7,5},{8,10},{9,11},{10,... | collective-permute-start | bytes 884744 | tf_op jit(solution)/shard_map/ppermute | solution.py:700
  65.2 12.9 %collective-permute-done.6 = bf16[192,768]{1,0:T(8,128)(2,1)S(1)} collective-permute-done((bf16[192,768]{1,0:T(8,128)(2,1)}, bf16[192,768]{1,0:T(8,128)(2,1)S(1)}, u32[]{:S(2)}, u32[]{:S(2)}) %collective-permute-start.6) | collective-permute-done | bytes 294944 | tf_op jit(solution)/shard_map/ppermute | solution.py:700
  97.1 8.8 %collective-permute-done.11 = bf16[384,768]{1,0:T(8,128)(2,1)S(1)} collective-permute-done((bf16[384,768]{1,0:T(8,128)(2,1)S(1)}, bf16[384,768]{1,0:T(8,128)(2,1)S(1)}, u32[]{:S(2)}, u32[]{:S(2)}) %collective-permute-start.11) | collective-permute-done | bytes 589856 | tf_op jit(solution)/shard_map/ppermute | solution.py:700
  107.1 14.5 %collective-permute-done.14 = bf16[768,768]{1,0:T(8,128)(2,1)S(1)} collective-permute-done((bf16[768,768]{1,0:T(8,128)(2,1)}, bf16[768,768]{1,0:T(8,128)(2,1)S(1)}, u32[]{:S(2)}, u32[]{:S(2)}) %collective-permute-start.14) | collective-permute-done | bytes 1179680 | tf_op jit(solution)/shard_map/ppermute | solution.py:719
  124.2 8.1 %shard_map.349 = (bf16[2,192,512]{2,1,0:T(8,128)(2,1)S(1)}, f32[6,1,512]{2,1,0:T(1,128)S(1)}) custom-call(s32[3]{0:T(128)S(1)} %pad_add_fusion.2.s_ref.refs_0_, bf16[2,576,1024]{2,1,0:T(8,128)(2,1)S(1)} %shard_map.348.q_ref.k_ref.v_ref, bf16[2,576,1024]{2,1,0:T(8,128)(2,1)S(1)} %shard_map.348.q_ref.k_ref.v_ref, ...), custom_call_target="tpu_custom_call" | custom-call | tf_op jit(solution)/shard_map/pallas_call | solution.py:69
  145.6 5.2 collective-permute-done.19.refs_2_
  152.7 13.5 %shard_map.354 = (bf16[2,192,512]{2,1,0:T(8,128)(2,1)S(1)}, f32[6,1,512]{2,1,0:T(1,128)S(1)}) custom-call(s32[3]{0:T(128)S(1)} %pad_add_fusion.2.s_ref.refs_0_, bf16[2,192,512]{2,1,0:T(8,128)(2,1)S(1)} %shard_map.352.q_ref, bf16[2,384,2048]{2,1,0:T(8,128)(2,1)S(1)} %shard_map.353.k_ref.v_ref, bf16[2,384,2048]{2,1,0:T(8,128)(2,1)S(1)} %shard_map.353.k_ref.v_ref), custom_call_target="tpu_custom_call" | custom-call | tf_op jit(solution)/shard_map/pallas_call | solution.py:69
  172.9 6.0 %shard_map.357 = (bf16[512,512]{1,0:T(8,128)(2,1)S(1)}, bf16[512,512]{1,0:T(8,128)(2,1)S(1)}, bf16[512,512]{1,0:T(8,128)(2,1)S(1)}, bf16[512,512]{1,0:T(8,128)(2,1)S(1)}, bf16[768,512]{1,0:T(8,128)(2,1)}) custom-call(bf16[768,768]{1,0:T(8,128)(2,1)S(1)} %constant_dynamic-update-slice_fusion.2.refs_0_, bf16[768,768]{1,0:T(8,128)(2,1)S(1)} %collective-permute-done.16.refs_1_, ...), custom_call_target="tpu_custom_call" | custom-call | tf_op jit(solution)/shard_map/pallas_call | solution.py:172
  188.7 18.7 %collective-permute-done.23 = bf16[768,256]{1,0:T(8,128)(2,1)S(1)} collective-permute-done((bf16[768,256]{1,0:T(8,128)(2,1)S(1)}, bf16[768,256]{1,0:T(8,128)(2,1)S(1)}, u32[]{:S(2)}, u32[]{:S(2)}) %collective-permute-start.23) | collective-permute-done | bytes 393248 | tf_op jit(solution)/shard_map/ppermute | solution.py:700
  210.0 16.8 %shard_map.359 = (bf16[4,4096,256]{2,1,0:T(8,128)(2,1)}, f32[8,4,256]{2,1,0:T(4,128)S(1)}, f32[3,4,256]{2,1,0:T(4,128)S(1)}) custom-call(s32[2]{0:T(128)S(1)} %pad_add_fusion.s_ref, bf16[2,768,256]{2,1,0:T(8,128)(2,1)S(1)} %pad_maximum_fusion.12.h0_ref.refs_1_, bf16[2,768,256]{2,1,0:T(8,128)(2,1)} %collective-permute-done.26.h1_ref.refs_2_, ...), custom_call_target="tpu_custom_call" | custom-call | tf_op jit(solution)/shard_map/pallas_call | solution.py:521
  230.1 17.1 %shard_map.360 = (bf16[4,4096,256]{2,1,0:T(8,128)(2,1)}, f32[8,4,256]{2,1,0:T(4,128)S(1)}, f32[3,4,256]{2,1,0:T(4,128)S(1)}) custom-call(s32[2]{0:T(128)S(1)} %pad_add_fusion.s_ref, bf16[2,768,256]{2,1,0:T(8,128)(2,1)} %collective-permute-done.25.h0_ref.refs_3_, bf16[2,768,256]{2,1,0:T(8,128)(2,1)S(1)} %collective-permute-done.27.h1_ref.refs_4_, ...), custom_call_target="tpu_custom_call" | custom-call | tf_op jit(solution)/shard_map/pallas_call | solution.py:521
  259.8 15.4 %shard_map.363 = (bf16[4,4096,256]{2,1,0:T(8,128)(2,1)}, bf16[2,768,256]{2,1,0:T(8,128)(2,1)}, bf16[2,768,256]{2,1,0:T(8,128)(2,1)}) custom-call(s32[2]{0:T(128)} %copy-done.83, bf16[4,4096,256]{2,1,0:T(8,128)(2,1)} %get-tuple-element.248.e_ref, f32[8,4,256]{2,1,0:T(4,128)} %copy-done.77, f32[8,256]{1,0:T(8,128)} %copy-done.78, ...), custom_call_target="tpu_custom_call", output_to_operand_aliasing={{0}: (1, {})} | custom-call | tf_op jit(solution)/shard_map/pallas_call | solution.py:575
  279.1 15.4 %shard_map.364 = (bf16[4,4096,256]{2,1,0:T(8,128)(2,1)}, bf16[2,768,256]{2,1,0:T(8,128)(2,1)}, bf16[2,768,256]{2,1,0:T(8,128)(2,1)}) custom-call(s32[2]{0:T(128)} %copy-done.83, bf16[4,4096,256]{2,1,0:T(8,128)(2,1)} %get-tuple-element.254.e_ref, f32[8,4,256]{2,1,0:T(4,128)} %copy-done.76, f32[8,256]{1,0:T(8,128)} %copy-done.78, ...), custom_call_target="tpu_custom_call", output_to_operand_aliasing={{0}: (1, {})} | custom-call | tf_op jit(solution)/shard_map/pallas_call | solution.py:575
  297.1 17.5 %collective-permute-done.36 = bf16[2,768,256]{2,1,0:T(8,128)(2,1)S(1)} collective-permute-done((bf16[2,768,256]{2,1,0:T(8,128)(2,1)S(1)}, bf16[2,768,256]{2,1,0:T(8,128)(2,1)S(1)}, u32[]{:S(2)}, u32[]{:S(2)}) %collective-permute-start.36) | collective-permute-done | bytes 786464 | tf_op jit(solution)/shard_map/ppermute | solution.py:700
  318.9 18.3 %shard_map.365 = bf16[768,4096]{1,0:T(8,128)(2,1)} custom-call(s32[8]{0:T(128)S(1)} %copy-done.89, bf16[2,768,256]{2,1,0:T(8,128)(2,1)S(1)} %pad_maximum_fusion.12.h0_ref.refs_1_, bf16[2,768,256]{2,1,0:T(8,128)(2,1)} %collective-permute-done.26.h1_ref.refs_2_, bf16[2,768,256]{2,1,0:T(8,128)(2,1)} %collective-permute-done.25.h0_ref.refs_3_, ...), custom_call_target="tpu_custom_call" | custom-call | tf_op jit(solution)/shard_map/pallas_call | solution.py:621
  347.0 12.7 %shard_map.367 = (bf16[4,768,768]{2,1,0:T(8,128)(2,1)}, bf16[768,512]{1,0:T(8,128)(2,1)}) custom-call(s32[8]{0:T(128)} %stack.235.s_ref, bf16[768,768]{1,0:T(8,128)(2,1)} %copy-done.12, bf16[768,768]{1,0:T(8,128)(2,1)} %copy-done.22, bf16[768,768]{1,0:T(8,128)(2,1)} %copy-done.97, bf16[768,768]{1,0:T(8,128)(2,1)} %copy-done.98, bf16[512,512]{1,0:T(8,128)(2,1)} %copy-done.66, ...), custom_call_target="tpu_custom_call" | custom-call | tf_op jit(solution)/shard_map/pallas_call | solution.py:208
  371.5 21.0 %shard_map.370 = (bf16[2,192,512]{2,1,0:T(8,128)(2,1)S(1)}, bf16[2,192,2048]{2,1,0:T(8,128)(2,1)S(1)}, bf16[2,192,2048]{2,1,0:T(8,128)(2,1)S(1)}) custom-call(s32[3]{0:T(128)S(1)} %pad_add_fusion.2.s_ref.refs_0_, bf16[2,192,512]{2,1,0:T(8,128)(2,1)S(1)} %copy-done.30, bf16[2,384,2048]{2,1,0:T(8,128)(2,1)} %copy-done.2, bf16[2,384,2048]{2,1,0:T(8,128)(2,1)} %copy-done.2, ...), custom_call_target="tpu_custom_call" | custom-call | tf_op jit(solution)/shard_map/pallas_call | solution.py:113
  394.4 4.6 shard_map.372
  411.8 10.5 %shard_map.374 = (bf16[768,768]{1,0:T(8,128)(2,1)}, bf16[768,768]{1,0:T(8,128)(2,1)}) custom-call(s32[3]{0:T(128)S(1)} %pad_add_fusion.2.s_ref.refs_0_, bf16[768,512]{1,0:T(8,128)(2,1)S(1)} %copy-done.32, bf16[768,2048]{1,0:T(8,128)(2,1)} %copy-done.6, bf16[768,2048]{1,0:T(8,128)(2,1)} %copy-done.6, bf16[768,512]{1,0:T(8,128)(2,1)S(1)} %copy-done.34, ...), custom_call_target="tpu_custom_call" | custom-call | tf_op jit(solution)/shard_map/pallas_call | solution.py:384
  424.0 5.2 collective-permute-start.43
  438.4 7.4 %collective-permute-start.45 = (bf16[192,2048]{1,0:T(8,128)(2,1)}, bf16[192,2048]{1,0:T(8,128)(2,1)}, u32[]{:S(2)}, u32[]{:S(2)}) collective-permute-start(bf16[192,2048]{1,0:T(8,128)(2,1)} %get-tuple-element.347), channel_id=1, source_target_pairs={{0,0},{1,1},{16,2},{17,3},{2,16},{3,17},{18,18},{19,19},{4,4},{5,5... | collective-permute-start | bytes 2359304 | tf_op jit(solution)/shard_map/ppermute | solution.py:727
  445.9 12.3 %shard_map.376 = (bf16[2,192,512]{2,1,0:T(8,128)(2,1)S(1)}, bf16[2,192,1024]{2,1,0:T(8,128)(2,1)S(1)}, bf16[2,192,1024]{2,1,0:T(8,128)(2,1)S(1)}) custom-call(s32[3]{0:T(128)S(1)} %pad_add_fusion.2.s_ref.refs_0_, bf16[2,576,1024]{2,1,0:T(8,128)(2,1)S(1)} %shard_map.348.q_ref.k_ref.v_ref, bf16[2,576,1024]{2,1,0:T(8,128)(2,1)S(1)} %shard_map.348.q_ref.k_ref.v_ref, ...), custom_call_target="tpu_custom_call" | custom-call | tf_op jit(solution)/shard_map/pallas_call | solution.py:113
  460.7 5.9 %collective-permute-done.42 = bf16[768,768]{1,0:T(8,128)(2,1)} collective-permute-done((bf16[768,768]{1,0:T(8,128)(2,1)}, bf16[768,768]{1,0:T(8,128)(2,1)}, u32[]{:S(2)}, u32[]{:S(2)}) %collective-permute-start.42) | collective-permute-done | bytes 1179680 | tf_op jit(solution)/shard_map/ppermute | solution.py:719
  469.9 6.9 %shard_map.377 = (bf16[768,768]{1,0:T(8,128)(2,1)}, bf16[768,768]{1,0:T(8,128)(2,1)}) custom-call(s32[3]{0:T(128)S(1)} %pad_add_fusion.2.s_ref.refs_0_, bf16[768,1024]{1,0:T(8,128)(2,1)} %copy-done.9, bf16[768,1024]{1,0:T(8,128)(2,1)} %copy-done.9, bf16[768,1024]{1,0:T(8,128)(2,1)} %copy-done.9, bf16[768,512]{1,0:T(8,128)(2,1)S(1)} %copy-done.39, ...), custom_call_target="tpu_custom_call" | custom-call | tf_op jit(solution)/shard_map/pallas_call | solution.py:384
  481.9 4.1 add_convert_fusion.4
  504.4 4.0 shard_map.379
  527.1 6.8 %collective-permute-start.57 = (bf16[192,768]{1,0:T(8,128)(2,1)S(1)}, bf16[192,768]{1,0:T(8,128)(2,1)S(1)}, u32[]{:S(2)}, u32[]{:S(2)}) collective-permute-start(bf16[192,768]{1,0:T(8,128)(2,1)S(1)} %get-tuple-element.320), channel_id=1, source_target_pairs={{0,2},{1,3},{2,0},{3,1},{4,6},{5,7},{6,4},{7,5},{8,10},{9,11},{10,... | collective-permute-start | bytes 884744 | tf_op jit(solution)/shard_map/ppermute | solution.py:707
  537.6 10.8 %collective-permute-start.59 = (bf16[192,768]{1,0:T(8,128)(2,1)S(1)}, bf16[192,768]{1,0:T(8,128)(2,1)}, u32[]{:S(2)}, u32[]{:S(2)}) collective-permute-start(bf16[192,768]{1,0:T(8,128)(2,1)S(1)} %get-tuple-element.322), channel_id=1, source_target_pairs={{0,3},{1,2},{2,1},{3,0},{4,7},{5,6},{6,5},{7,4},{8,11},{9,10},{10,... | collective-permute-start | bytes 884744 | tf_op jit(solution)/shard_map/ppermute | solution.py:707
  549.1 13.7 %collective-permute-done.57 = bf16[192,768]{1,0:T(8,128)(2,1)S(1)} collective-permute-done((bf16[192,768]{1,0:T(8,128)(2,1)S(1)}, bf16[192,768]{1,0:T(8,128)(2,1)S(1)}, u32[]{:S(2)}, u32[]{:S(2)}) %collective-permute-start.57) | collective-permute-done | bytes 294944 | tf_op jit(solution)/shard_map/ppermute | solution.py:707
  (478 shorter events, 221.1 us)
Async XLA Ops:
  7.2 453.5 %reduce-scatter.4.cloned.1.call-start = ((), (), s32[]{:S(2)}) async-start(), calls=%async_computation.3 | async-start | bytes 7864320 | tf_op jit(solution)/shard_map/reduce_scatter | solution.py:986
  15.8 25.2 %collective-permute-start = (bf16[192,768]{1,0:T(8,128)(2,1)S(1)}, bf16[192,768]{1,0:T(8,128)(2,1)}, u32[]{:S(2)}, u32[]{:S(2)}) collective-permute-start(bf16[192,768]{1,0:T(8,128)(2,1)S(1)} %maximum_select_fusion.1), channel_id=1, source_target_pairs={{0,2},{1,3},{2,0},{3,1},{4,6},{5,7},{6,4},{7,5},{8,10},{9,11},{10,... | collective-permute-start | bytes 884744 | tf_op jit(solution)/shard_map/ppermute | solution.py:700
  18.9 59.3 %collective-permute-start.8 = (bf16[192,4096]{1,0:T(8,128)(2,1)S(1)}, bf16[192,4096]{1,0:T(8,128)(2,1)S(1)}, u32[]{:S(2)}, u32[]{:S(2)}) collective-permute-start(bf16[192,4096]{1,0:T(8,128)(2,1)S(1)} %fusion.own_ref), channel_id=1, source_target_pairs={{0,8},{4,12},{8,0},{12,4},{16,20},{20,16},{24,28},{28,24},{1,9},{5... | collective-permute-start | bytes 4718600 | tf_op jit(solution)/shard_map/ppermute | solution.py:719
  20.6 57.6 %collective-permute-start.7 = (bf16[192,4096]{1,0:T(8,128)(2,1)S(1)}, bf16[192,4096]{1,0:T(8,128)(2,1)}, u32[]{:S(2)}, u32[]{:S(2)}) collective-permute-start(bf16[192,4096]{1,0:T(8,128)(2,1)S(1)} %fusion.own_ref), channel_id=1, source_target_pairs={{0,4},{4,0},{8,12},{12,8},{16,24},{20,28},{24,16},{28,20},{1,5},{5... | collective-permute-start | bytes 4718600 | tf_op jit(solution)/shard_map/ppermute | solution.py:719
  43.2 34.9 %collective-permute-start.5 = (bf16[768,768]{1,0:T(8,128)(2,1)}, bf16[768,768]{1,0:T(8,128)(2,1)}, u32[]{:S(2)}, u32[]{:S(2)}) collective-permute-start(bf16[768,768]{1,0:T(8,128)(2,1)} %pad_maximum_fusion.8), channel_id=1, source_target_pairs={{0,4},{4,0},{8,12},{12,8},{16,24},{20,28},{24,16},{28,20},{1,5},{5... | collective-permute-start | bytes 3538952 | tf_op jit(solution)/shard_map/ppermute | solution.py:719
  58.4 19.7 %collective-permute-start.6 = (bf16[192,768]{1,0:T(8,128)(2,1)}, bf16[192,768]{1,0:T(8,128)(2,1)S(1)}, u32[]{:S(2)}, u32[]{:S(2)}) collective-permute-start(bf16[192,768]{1,0:T(8,128)(2,1)} %maximum_select_fusion.2), channel_id=1, source_target_pairs={{0,2},{1,3},{2,0},{3,1},{4,6},{5,7},{6,4},{7,5},{8,10},{9,11},{10,... | collective-permute-start | bytes 884744 | tf_op jit(solution)/shard_map/ppermute | solution.py:700
  82.2 23.8 %collective-permute-start.11 = (bf16[384,768]{1,0:T(8,128)(2,1)S(1)}, bf16[384,768]{1,0:T(8,128)(2,1)S(1)}, u32[]{:S(2)}, u32[]{:S(2)}) collective-permute-start(bf16[384,768]{1,0:T(8,128)(2,1)S(1)} %constant_dynamic-update-slice_fusion), channel_id=1, source_target_pairs={{0,1},{1,0},{2,3},{3,2},{4,5},{5,4},{6,7},{7,6},{8,9},{9,8},{10,11... | collective-permute-start | bytes 1769480 | tf_op jit(solution)/shard_map/ppermute | solution.py:700
  82.3 23.7 %collective-permute-start.12 = (bf16[192,2048]{1,0:T(8,128)(2,1)}, bf16[192,2048]{1,0:T(8,128)(2,1)S(1)}, u32[]{:S(2)}, u32[]{:S(2)}) collective-permute-start(bf16[192,2048]{1,0:T(8,128)(2,1)} %param.21), channel_id=1, source_target_pairs={{0,0},{1,1},{2,16},{3,17},{16,2},{17,3},{18,18},{19,19},{4,4},{5,5... | collective-permute-start | bytes 2359304 | tf_op jit(solution)/shard_map/ppermute | solution.py:727
  84.1 23.0 %collective-permute-start.13 = (bf16[768,768]{1,0:T(8,128)(2,1)}, bf16[768,768]{1,0:T(8,128)(2,1)S(1)}, u32[]{:S(2)}, u32[]{:S(2)}) collective-permute-start(bf16[768,768]{1,0:T(8,128)(2,1)} %pad_maximum_fusion.8), channel_id=1, source_target_pairs={{0,24},{4,28},{8,16},{12,20},{16,4},{20,0},{24,12},{28,8},{1,25},{... | collective-permute-start | bytes 3538952 | tf_op jit(solution)/shard_map/ppermute | solution.py:719
  87.4 34.2 %collective-permute-start.14 = (bf16[768,768]{1,0:T(8,128)(2,1)}, bf16[768,768]{1,0:T(8,128)(2,1)S(1)}, u32[]{:S(2)}, u32[]{:S(2)}) collective-permute-start(bf16[768,768]{1,0:T(8,128)(2,1)} %collective-permute-done.5), channel_id=1, source_target_pairs={{0,24},{4,28},{8,16},{12,20},{16,4},{20,0},{24,12},{28,8},{1,25},{... | collective-permute-start | bytes 3538952 | tf_op jit(solution)/shard_map/ppermute | solution.py:719
  106.1 26.2 %collective-permute-start.16 = (bf16[768,768]{1,0:T(8,128)(2,1)S(1)}, bf16[768,768]{1,0:T(8,128)(2,1)S(1)}, u32[]{:S(2)}, u32[]{:S(2)}) collective-permute-start(bf16[768,768]{1,0:T(8,128)(2,1)S(1)} %constant_dynamic-update-slice_fusion.2.refs_0_), channel_id=1, source_target_pairs={{0,4},{4,0},{8,12},{12,8},{16,24},{20,28},{24,16},{28,20},{1,5},{5... | collective-permute-start | bytes 3538952 | tf_op jit(solution)/shard_map/ppermute | solution.py:719
  107.1 25.2 %collective-permute-start.15 = (bf16[192,2048]{1,0:T(8,128)(2,1)}, bf16[192,2048]{1,0:T(8,128)(2,1)S(1)}, u32[]{:S(2)}, u32[]{:S(2)}) collective-permute-start(bf16[192,2048]{1,0:T(8,128)(2,1)} %param.21), channel_id=1, source_target_pairs={{0,1},{1,0},{2,17},{3,16},{16,3},{17,2},{18,19},{19,18},{4,5},{5,4... | collective-permute-start | bytes 2359304 | tf_op jit(solution)/shard_map/ppermute | solution.py:727
  182.4 25.1 %collective-permute-start.24 = (bf16[192,4096]{1,0:T(8,128)(2,1)}, bf16[192,4096]{1,0:T(8,128)(2,1)}, u32[]{:S(2)}, u32[]{:S(2)}) collective-permute-start(bf16[192,4096]{1,0:T(8,128)(2,1)} %collective-permute-done.7.one_ref), channel_id=1, source_target_pairs={{0,8},{4,12},{8,0},{12,4},{16,20},{20,16},{24,28},{28,24},{1,9},{5... | collective-permute-start | bytes 4718600 | tf_op jit(solution)/shard_map/ppermute | solution.py:719
  207.6 20.0 %collective-permute-start.25 = (bf16[2,768,256]{2,1,0:T(8,128)(2,1)S(1)}, bf16[2,768,256]{2,1,0:T(8,128)(2,1)}, u32[]{:S(2)}, u32[]{:S(2)}) collective-permute-start(bf16[2,768,256]{2,1,0:T(8,128)(2,1)S(1)} %pad_maximum_fusion.12.h0_ref.refs_1_), channel_id=1, source_target_pairs={{0,1},{1,0},{2,3},{3,2},{4,5},{5,4},{6,7},{7,6},{8,9},{9,8},{10,11... | collective-permute-start | bytes 2359304 | tf_op jit(solution)/shard_map/ppermute | solution.py:700
  294.7 19.8 %collective-permute-start.36 = (bf16[2,768,256]{2,1,0:T(8,128)(2,1)S(1)}, bf16[2,768,256]{2,1,0:T(8,128)(2,1)S(1)}, u32[]{:S(2)}, u32[]{:S(2)}) collective-permute-start(bf16[2,768,256]{2,1,0:T(8,128)(2,1)S(1)} %add_convert_fusion.2), channel_id=1, source_target_pairs={{0,1},{1,0},{2,3},{3,2},{4,5},{5,4},{6,7},{7,6},{8,9},{9,8},{10,11... | collective-permute-start | bytes 2359304 | tf_op jit(solution)/shard_map/ppermute | solution.py:700
  317.9 20.2 %collective-permute-start.37 = (bf16[768,256]{1,0:T(8,128)(2,1)}, bf16[768,256]{1,0:T(8,128)(2,1)}, u32[]{:S(2)}, u32[]{:S(2)}) collective-permute-start(bf16[768,256]{1,0:T(8,128)(2,1)} %fusion.9), channel_id=1, source_target_pairs={{0,2},{1,3},{2,0},{3,1},{4,6},{5,7},{6,4},{7,5},{8,10},{9,11},{10,... | collective-permute-start | bytes 1179656 | tf_op jit(solution)/shard_map/ppermute | solution.py:700
  338.1 154.5 %reduce-scatter.6.cloned.1.call-start = ((), (), s32[]{:S(2)}) async-start(), calls=%async_computation.4 | async-start | bytes 5898240 | tf_op jit(solution)/shard_map/reduce_scatter | solution.py:998
  359.7 207.7 %reduce-scatter.8.cloned.1.call-start = ((), (), s32[]{:S(2)}) async-start(), calls=%async_computation.5 | async-start | bytes 1474560 | tf_op jit(solution)/shard_map/reduce_scatter | solution.py:1039
  422.3 44.3 %collective-permute-start.44 = (bf16[768,768]{1,0:T(8,128)(2,1)}, bf16[768,768]{1,0:T(8,128)(2,1)}, u32[]{:S(2)}, u32[]{:S(2)}) collective-permute-start(bf16[768,768]{1,0:T(8,128)(2,1)} %get-tuple-element.291), channel_id=1, source_target_pairs={{16,24},{20,28},{24,16},{28,20},{17,25},{21,29},{25,17},{29,21},{1... | collective-permute-start | bytes 3538952 | tf_op jit(solution)/shard_map/ppermute | solution.py:719
  424.0 42.7 %collective-permute-start.43 = (bf16[768,768]{1,0:T(8,128)(2,1)}, bf16[768,768]{1,0:T(8,128)(2,1)}, u32[]{:S(2)}, u32[]{:S(2)}) collective-permute-start(bf16[768,768]{1,0:T(8,128)(2,1)} %get-tuple-element.291), channel_id=1, source_target_pairs={{0,28},{4,24},{8,20},{12,16},{1,29},{5,25},{9,21},{13,17},{2,30},{... | collective-permute-start | bytes 3538952 | tf_op jit(solution)/shard_map/ppermute | solution.py:719
  429.2 37.4 %collective-permute-start.42 = (bf16[768,768]{1,0:T(8,128)(2,1)}, bf16[768,768]{1,0:T(8,128)(2,1)}, u32[]{:S(2)}, u32[]{:S(2)}) collective-permute-start(bf16[768,768]{1,0:T(8,128)(2,1)} %get-tuple-element.290), channel_id=1, source_target_pairs={{0,20},{4,16},{8,28},{12,24},{1,21},{5,17},{9,29},{13,25},{2,22},{... | collective-permute-start | bytes 3538952 | tf_op jit(solution)/shard_map/ppermute | solution.py:719
  435.6 51.9 %collective-permute-start.46 = (bf16[192,2048]{1,0:T(8,128)(2,1)}, bf16[192,2048]{1,0:T(8,128)(2,1)}, u32[]{:S(2)}, u32[]{:S(2)}) collective-permute-start(bf16[192,2048]{1,0:T(8,128)(2,1)} %get-tuple-element.346), channel_id=1, source_target_pairs={{1,0},{0,1},{17,2},{16,3},{3,16},{2,17},{19,18},{18,19},{5,4},{4,5... | collective-permute-start | bytes 2359304 | tf_op jit(solution)/shard_map/ppermute | solution.py:727
  438.4 70.5 %collective-permute-start.45 = (bf16[192,2048]{1,0:T(8,128)(2,1)}, bf16[192,2048]{1,0:T(8,128)(2,1)}, u32[]{:S(2)}, u32[]{:S(2)}) collective-permute-start(bf16[192,2048]{1,0:T(8,128)(2,1)} %get-tuple-element.347), channel_id=1, source_target_pairs={{0,0},{1,1},{16,2},{17,3},{2,16},{3,17},{18,18},{19,19},{4,4},{5,5... | collective-permute-start | bytes 2359304 | tf_op jit(solution)/shard_map/ppermute | solution.py:727
  476.9 39.5 %collective-permute-start.49 = (bf16[768,768]{1,0:T(8,128)(2,1)}, bf16[768,768]{1,0:T(8,128)(2,1)}, u32[]{:S(2)}, u32[]{:S(2)}) collective-permute-start(bf16[768,768]{1,0:T(8,128)(2,1)} %get-tuple-element.310), channel_id=1, source_target_pairs={{16,12},{20,8},{24,4},{28,0},{17,13},{21,9},{25,5},{29,1},{18,14},... | collective-permute-start | bytes 3538952 | tf_op jit(solution)/shard_map/ppermute | solution.py:719
  478.3 38.0 %collective-permute-start.47 = (bf16[768,768]{1,0:T(8,128)(2,1)}, bf16[768,768]{1,0:T(8,128)(2,1)}, u32[]{:S(2)}, u32[]{:S(2)}) collective-permute-start(bf16[768,768]{1,0:T(8,128)(2,1)} %get-tuple-element.310), channel_id=1, source_target_pairs={{0,4},{4,0},{8,12},{12,8},{1,5},{5,1},{9,13},{13,9},{2,6},{6,2},{1... | collective-permute-start | bytes 3538952 | tf_op jit(solution)/shard_map/ppermute | solution.py:719
  485.9 26.5 %collective-permute-start.50 = (bf16[384,768]{1,0:T(8,128)(2,1)}, bf16[384,768]{1,0:T(8,128)(2,1)}, u32[]{:S(2)}, u32[]{:S(2)}) collective-permute-start(bf16[384,768]{1,0:T(8,128)(2,1)} %get-tuple-element.342), channel_id=1, source_target_pairs={{16,17},{17,16},{18,19},{19,18},{20,21},{21,20},{22,23},{23,22},{2... | collective-permute-start | bytes 1769480 | tf_op jit(solution)/shard_map/ppermute | solution.py:707
  487.6 28.8 %collective-permute-start.48 = (bf16[768,768]{1,0:T(8,128)(2,1)}, bf16[768,768]{1,0:T(8,128)(2,1)}, u32[]{:S(2)}, u32[]{:S(2)}) collective-permute-start(bf16[768,768]{1,0:T(8,128)(2,1)} %get-tuple-element.312.refs_0_), channel_id=1, source_target_pairs={{16,8},{20,12},{24,0},{28,4},{17,9},{21,13},{25,1},{29,5},{18,10},... | collective-permute-start | bytes 3538952 | tf_op jit(solution)/shard_map/ppermute | solution.py:719
  520.3 28.1 %collective-permute-start.53 = (bf16[192,1152]{1,0:T(8,128)(2,1)S(1)}, bf16[192,1152]{1,0:T(8,128)(2,1)S(1)}, u32[]{:S(2)}, u32[]{:S(2)}) collective-permute-start(bf16[192,1152]{1,0:T(8,128)(2,1)S(1)} %get-tuple-element.359), channel_id=1, source_target_pairs={{1,0},{0,1},{17,2},{16,3},{3,16},{2,17},{19,18},{18,19},{5,4},{4,5... | collective-permute-start | bytes 1327112 | tf_op jit(solution)/shard_map/ppermute | solution.py:727
  523.4 45.5 %collective-permute-start.61 = (bf16[192,768]{1,0:T(8,128)(2,1)}, bf16[192,768]{1,0:T(8,128)(2,1)S(1)}, u32[]{:S(2)}, u32[]{:S(2)}) collective-permute-start(bf16[192,768]{1,0:T(8,128)(2,1)} %slice.421), channel_id=1, source_target_pairs={{16,18},{17,19},{18,16},{19,17},{20,22},{21,23},{22,20},{23,21},{2... | collective-permute-start | bytes 884744 | tf_op jit(solution)/shard_map/ppermute | solution.py:707
  527.1 35.7 %collective-permute-start.57 = (bf16[192,768]{1,0:T(8,128)(2,1)S(1)}, bf16[192,768]{1,0:T(8,128)(2,1)S(1)}, u32[]{:S(2)}, u32[]{:S(2)}) collective-permute-start(bf16[192,768]{1,0:T(8,128)(2,1)S(1)} %get-tuple-element.320), channel_id=1, source_target_pairs={{0,2},{1,3},{2,0},{3,1},{4,6},{5,7},{6,4},{7,5},{8,10},{9,11},{10,... | collective-permute-start | bytes 884744 | tf_op jit(solution)/shard_map/ppermute | solution.py:707
  533.8 30.4 %collective-permute-start.58 = (bf16[192,768]{1,0:T(8,128)(2,1)S(1)}, bf16[192,768]{1,0:T(8,128)(2,1)S(1)}, u32[]{:S(2)}, u32[]{:S(2)}) collective-permute-start(bf16[192,768]{1,0:T(8,128)(2,1)S(1)} %get-tuple-element.321), channel_id=1, source_target_pairs={{0,1},{1,0},{2,3},{3,2},{4,5},{5,4},{6,7},{7,6},{8,9},{9,8},{10,11... | collective-permute-start | bytes 884744 | tf_op jit(solution)/shard_map/ppermute | solution.py:707
  537.6 29.8 %collective-permute-start.59 = (bf16[192,768]{1,0:T(8,128)(2,1)S(1)}, bf16[192,768]{1,0:T(8,128)(2,1)}, u32[]{:S(2)}, u32[]{:S(2)}) collective-permute-start(bf16[192,768]{1,0:T(8,128)(2,1)S(1)} %get-tuple-element.322), channel_id=1, source_target_pairs={{0,3},{1,2},{2,1},{3,0},{4,7},{5,6},{6,5},{7,4},{8,11},{9,10},{10,... | collective-permute-start | bytes 884744 | tf_op jit(solution)/shard_map/ppermute | solution.py:707
  (149 other events, 1565.1 us)
Sparse Core Ops, SparseCore 0:
  338.2 68.2 reduce-scatter.3
  409.6 82.9 reduce-scatter.5
  499.3 32.6 reduce-scatter.7
